TPU v7x, 768 devices: a whole 4x8x12 slice. The times are simulated.
768 devices in a mesh: cells: 192 (over y_hi, x, z, core), bands: 4 (over y_lo).
Axes of the slice: x: 4, y: 8 (y_hi: 2, y_lo: 4; y = y_hi * 4 + y_lo), z: 12, core: 2. Of those that a mesh axis runs over, the one named last changes fastest.
Arguments:
- start_bands: bfloat16 [224, 98304], P('bands', 'cells'), may hold values from -24 to 24, as said below
- cell_ham: bfloat16 [192, 729, 729], P('cells'), may hold values from -3 to 4, as said below
- node_index: int32 [192, 729], P('cells'), may hold values from 0 to 98431, as said below
Outputs:
- ortho_bands: bfloat16 [224, 98304], P('bands', 'cells')
Inputs may be any that keep to these rules, and one draw needn't show every extreme that they name: `start_bands`: random bands whose scale varies from one partition's nodes to the next and from band to band. `cell_ham`: every cell matrix is symmetric. `node_index`: for a cell of partition p (cells p * 1 to (p + 1) - 1) every entry lies in p * 512 to p * 512 + 639, and each of these 640 indices appears in some cell of partition p.
All inputs are finite; a program needn't handle non-finite values.
Results may differ from a plain program's by a relative error of at most 0.0078.
Values may be sent and summed in bfloat16 or wider, within the bound.
No kernel may reach another device: no remote copies, remote signals or barrier semaphores. Data moves between devices by JAX's collectives and lax.ppermute only.
A program may use at most 64 MiB of HBM per device.

v0:
```python
import jax
import jax.numpy as jnp
from jax import lax
from jax.sharding import PartitionSpec as P

CELL_NODES = 729
CELL_DEV = 1
NODE_DEV = 512
SHARED = 64
NODE_EXT = 640


filter_center = 2.75
filter_half = 2.25


def with_halo(shard, sides, width):
    for axis, dim in sides:
        size, length = (lax.axis_size(axis), shard.shape[dim])
        up = [(i, (i + 1) % size) for i in range(size - 1)]
        down = [(j, i) for i, j in up]
        last = lax.slice_in_dim(shard, length - width, length, axis=dim)
        leading = lax.slice_in_dim(shard, 0, width, axis=dim)
        before = lax.ppermute(last, axis, up)
        after = lax.ppermute(leading, axis, down)
        shard = jnp.concatenate([before, shard, after], axis=dim)
    return shard


def in_order(pieces, dim):
    dims = list(pieces.shape[1:])
    dims[dim] *= pieces.shape[0]
    return jnp.moveaxis(pieces, 0, dim).reshape(dims)


def from_everyone(shard, axis):
    copies = jnp.broadcast_to(shard, (lax.axis_size(axis), *shard.shape))
    return lax.all_to_all(copies, axis, split_axis=0, concat_axis=0, tiled=True)


def gathered_copies(shard, axis, dim):
    return in_order(from_everyone(shard, axis), dim)


def gathered_total(shard, axis):
    pieces = lax.all_gather(shard, axis)
    return pieces.sum(axis=0)


def next_term(applied, current, previous):
    shifted = (applied - filter_center * current.astype(jnp.float32)) / filter_half
    if previous is None:
        return shifted.astype(jnp.bfloat16)
    return (2.0 * shifted - previous.astype(jnp.float32)).astype(jnp.bfloat16)


def apply_operator(bands_now, cell_ham, local_index):
    band_count = bands_now.shape[0]
    widened = with_halo(bands_now, (("cells", 1),), SHARED)
    columns = jnp.take(widened, local_index, axis=1).reshape(band_count, CELL_DEV, CELL_NODES)
    product = jnp.einsum("bcj,cij->bci", columns, cell_ham, preferred_element_type=jnp.float32)
    partial_value = (
        jnp.zeros((band_count, NODE_EXT), jnp.float32)
        .at[:, local_index]
        .add(product.reshape(band_count, -1))
    )
    shared_sum = with_halo(partial_value, (("cells", 1),), SHARED)
    owned = partial_value[:, SHARED : SHARED + NODE_DEV]
    from_left = jnp.pad(shared_sum[:, :SHARED], ((0, 0), (0, NODE_DEV - SHARED)))
    from_right = jnp.pad(shared_sum[:, NODE_EXT + SHARED :], ((0, 0), (NODE_DEV - SHARED, 0)))
    return owned + from_left + from_right


def shards(start_bands, cell_ham, node_index):
    partition = lax.axis_index("cells")
    local_index = node_index.reshape(-1) - partition * NODE_DEV
    first = next_term(apply_operator(start_bands, cell_ham, local_index), start_bands, None)
    second = next_term(apply_operator(first, cell_ham, local_index), first, start_bands)
    third = next_term(apply_operator(second, cell_ham, local_index), second, first)
    gathered = gathered_copies(third, "bands", 0)
    node_total = float(NODE_DEV * lax.axis_size("cells"))
    contract = (((1,), (1,)), ((), ()))
    column_part = lax.dot_general(gathered, third, contract, preferred_element_type=jnp.float32)
    column_sum = gathered_total(column_part, "cells")
    margin = gathered_copies(column_sum, "bands", 1)
    margin = margin / node_total
    lower = jnp.linalg.cholesky(margin)
    identity = jnp.eye(margin.shape[0], dtype=jnp.float32)
    inverse = lax.linalg.triangular_solve(lower, identity, left_side=True, lower=True)
    band_count = third.shape[0]
    band_rows = lax.dynamic_slice_in_dim(
        inverse, lax.axis_index("bands") * band_count, band_count, 0
    ).astype(jnp.bfloat16)
    return jnp.dot(band_rows, gathered, preferred_element_type=jnp.float32).astype(jnp.bfloat16)


def solution(mesh):
    return jax.shard_map(
        shards,
        mesh=mesh,
        in_specs=(P("bands", "cells"), P("cells", None, None), P("cells", None)),
        out_specs=P("bands", "cells"),
        check_vma=False,
    )
```

profile of v0, /device:TPU:1, one launch (start us, length us, event | category | flops | bytes accessed | tf_op | source)
XLA Modules:
  0.0 432.4 jit_solution(17698502183376533153)
XLA Ops:
  6.5 0.9 fusion.56
  7.4 5.4 %collective-permute-start = (bf16[56,64]{1,0:T(8,128)(2,1)S(1)}, bf16[56,64]{1,0:T(8,128)(2,1)S(1)}, u32[]{:S(2)}, u32[]{:S(2)}) collective-permute-start(bf16[56,64]{1,0:T(8,128)(2,1)S(1)} %get-tuple-element.38), channel_id=1, source_target_pairs={{0,4},{4,8},{8,12},{12,16},{16,20},{20,24},{24,28},{28,32},{32,36}... | collective-permute-start | bytes 21512 | tf_op jit(solution)/shard_map/ppermute | solution.py:24
  12.8 8.3 %collective-permute-start.1 = (bf16[56,64]{1,0:T(8,128)(2,1)S(1)}, bf16[56,64]{1,0:T(8,128)(2,1)S(1)}, u32[]{:S(2)}, u32[]{:S(2)}) collective-permute-start(bf16[56,64]{1,0:T(8,128)(2,1)S(1)} %get-tuple-element.39), channel_id=1, source_target_pairs={{4,0},{8,4},{12,8},{16,12},{20,16},{24,20},{28,24},{32,28},{36,32}... | collective-permute-start | bytes 21512 | tf_op jit(solution)/shard_map/ppermute | solution.py:25
  21.1 0.7 subtract_reduce_fusion
  21.9 0.7 fusion.45
  22.6 0.9 pad_maximum_fusion.3
  23.7 2.0 gather_fusion
  25.8 0.6 convolution_bitcast_fusion.2
  26.5 6.1 %scatter_custom_fusion = f32[56,640]{0,1:T(8,128)S(1)} fusion(s32[729]{0:T(1024)S(1)} %fusion.45, f32[729,56]{1,0:T(8,128)S(1)} %copy.39, f32[]{:T(128)} %constant.111.clone.1), kind=kCustom, calls=%fused_computation.57 | custom fusion | flops 40824 | bytes 143364 | tf_op jit(solution)/shard_map/scatter-add | solution.py:65
  32.6 1.9 collective-permute-start.2
  34.6 2.4 collective-permute-start.3
  37.1 2.7 collective-permute-done.3
  39.9 1.9 collective-permute-start.4
  41.8 2.4 collective-permute-start.5
  44.2 2.6 collective-permute-done.5
  46.9 2.0 gather_fusion.1
  49.0 0.6 convolution_bitcast_fusion.1
  49.7 6.1 %scatter_custom_fusion.1 = f32[56,640]{0,1:T(8,128)S(1)} fusion(s32[729]{0:T(1024)S(1)} %fusion.45, f32[729,56]{1,0:T(8,128)S(1)} %copy.41, f32[]{:T(128)} %constant.111.clone.1), kind=kCustom, calls=%fused_computation.55 | custom fusion | flops 40824 | bytes 143364 | tf_op jit(solution)/shard_map/scatter-add | solution.py:65
  55.8 1.9 collective-permute-start.6
  57.8 2.4 collective-permute-start.7
  60.2 2.8 collective-permute-done.7
  63.1 1.9 collective-permute-start.8
  65.0 2.4 collective-permute-start.9
  67.4 3.8 collective-permute-done.9
  71.3 2.0 gather_fusion.2
  73.4 0.6 convolution_bitcast_fusion
  74.1 6.1 %scatter_custom_fusion.2 = f32[56,640]{0,1:T(8,128)S(1)} fusion(s32[729]{0:T(1024)S(1)} %fusion.45, f32[729,56]{1,0:T(8,128)S(1)} %copy.42, f32[]{:T(128)} %constant.111.clone.1), kind=kCustom, calls=%fused_computation.53 | custom fusion | flops 40824 | bytes 143364 | tf_op jit(solution)/shard_map/scatter-add | solution.py:65
  80.2 1.9 collective-permute-start.10
  82.2 2.4 collective-permute-start.11
  84.6 4.0 collective-permute-done.11
  88.8 10.7 %all_to_all.10 = bf16[4,56,512]{2,1,0:T(8,128)(2,1)S(1)} all-to-all(bf16[4,56,512]{2,1,0:T(8,128)(2,1)S(1)} %broadcast_in_dim.20), channel_id=1, replica_groups=mesh['cells'=192,'bands'=4] {'bands'}, dimensions={0} | all-to-all | bytes 458752 | tf_op jit(solution)/shard_map/all_to_all | solution.py:38
  99.5 0.8 convolution_bitcast_fusion.3
  100.4 254.0 %all-gather.4.cloned.1.call-done = f32[192,224,56]{1,2,0:T(8,128)} async-done(((f32[1,224,56]{1,2,0:T(8,128)}), f32[192,224,56]{1,2,0:T(8,128)}) %all-gather.4.cloned.1.call-update) | async-done | bytes 9633808 | tf_op jit(solution)/shard_map/all_gather | solution.py:46
  354.4 4.8 %reduce_sum.9 = f32[224,56]{0,1:T(8,128)S(1)} reduce(f32[192,224,56]{1,2,0:T(8,128)} %all-gather.4.cloned.1.call-done, f32[]{:T(128)} %constant.111.clone.1), dimensions={0}, to_apply=%region_3.5 | reduce | flops 2395904 | bytes 9683972 | tf_op jit(solution)/shard_map/reduce_sum | solution.py:47
  359.2 0.7 broadcast_in_dim.21
  359.9 3.6 all-to-all-start.1
  363.5 6.5 %all-to-all-done.1 = f32[4,224,56]{1,2,0:T(8,128)S(1)} async-done(((f32[4,224,56]{1,2,0:T(8,128)}), f32[4,224,56]{1,2,0:T(8,128)S(1)}, u32[]{:S(2)}, u32[]{:S(2)}) %all-to-all-start.1) | async-done | bytes 200736 | tf_op jit(solution)/shard_map/all_to_all | solution.py:38
  370.3 11.7 %cholesky.51 = f32[128,128]{1,0:T(8,128)S(1)} custom-call(f32[128,128]{1,0:T(8,128)S(1)} %cholesky.124), custom_call_target="Cholesky" | custom-call | tf_op jit(solution)/shard_map/jit(cholesky)/cholesky | solution.py:87
  382.1 9.8 %custom-call.14 = f32[1,128,128]{1,2,0:T(8,128)S(1)} custom-call(f32[1,128,128]{2,1,0:T(8,128)S(1)} %get-tuple-element.37), custom_call_target="InvertDiagBlocksLowerTriangular" | custom-call | tf_op jit(solution)/shard_map/jit(cholesky)/cholesky | solution.py:87
  392.1 0.2 convolution_subtract_fusion.1
  392.3 8.8 %cholesky.110 = f32[96,96]{1,0:T(8,128)S(1)} custom-call(f32[96,96]{1,0:T(8,128)S(1)} %convolution_subtract_fusion.1), custom_call_target="Cholesky" | custom-call | tf_op jit(solution)/shard_map/jit(cholesky)/cholesky | solution.py:87
  401.1 0.7 compare_reduce_fusion
  401.8 0.6 compare_reduce_fusion.1
  404.0 19.7 %custom-call.15 = f32[2,128,128]{1,2,0:T(8,128)S(1)} custom-call(f32[2,128,128]{2,1,0:T(8,128)S(1)} %pad_maximum_fusion.2), custom_call_target="InvertDiagBlocksLowerTriangular" | custom-call | tf_op jit(solution)/shard_map/triangular_solve | solution.py:89
  423.7 0.3 fusion.31
  423.9 0.4 convolution_subtract_fusion
  424.3 0.4 fusion.43
  424.7 0.9 convolution_convert_fusion
  (48 shorter events, 1.9 us)
Async XLA Ops:
  6.5 19.2 %copy-start = (bf16[1,729,729]{2,1,0:T(8,128)(2,1)S(1)}, bf16[1,729,729]{2,1,0:T(8,128)(2,1)}, u32[]{:S(2)}) copy-start(bf16[1,729,729]{2,1,0:T(8,128)(2,1)} %param.6) | copy-start | bytes 3188650
  6.5 347.8 %all-gather.4.cloned.1.call-start = ((), (), s32[]{:S(2)}) async-start(), calls=%async_computation.2 | async-start | bytes 11067392 | tf_op jit(solution)/shard_map/all_gather | solution.py:46
  7.4 15.1 %collective-permute-start = (bf16[56,64]{1,0:T(8,128)(2,1)S(1)}, bf16[56,64]{1,0:T(8,128)(2,1)S(1)}, u32[]{:S(2)}, u32[]{:S(2)}) collective-permute-start(bf16[56,64]{1,0:T(8,128)(2,1)S(1)} %get-tuple-element.38), channel_id=1, source_target_pairs={{0,4},{4,8},{8,12},{12,16},{16,20},{20,24},{24,28},{28,32},{32,36}... | collective-permute-start | bytes 21512 | tf_op jit(solution)/shard_map/ppermute | solution.py:24
  12.8 9.8 %collective-permute-start.1 = (bf16[56,64]{1,0:T(8,128)(2,1)S(1)}, bf16[56,64]{1,0:T(8,128)(2,1)S(1)}, u32[]{:S(2)}, u32[]{:S(2)}) collective-permute-start(bf16[56,64]{1,0:T(8,128)(2,1)S(1)} %get-tuple-element.39), channel_id=1, source_target_pairs={{4,0},{8,4},{12,8},{16,12},{20,16},{24,20},{28,24},{32,28},{36,32}... | collective-permute-start | bytes 21512 | tf_op jit(solution)/shard_map/ppermute | solution.py:25
  25.7 11.2 %copy-start.1 = (bf16[56,512]{1,0:T(8,128)(2,1)S(1)}, bf16[56,512]{1,0:T(8,128)(2,1)}, u32[]{:S(2)}) copy-start(bf16[56,512]{1,0:T(8,128)(2,1)} %param.5) | copy-start | bytes 172036
  32.6 4.5 %collective-permute-start.2 = (f32[56,64]{0,1:T(8,128)S(1)}, f32[56,64]{0,1:T(8,128)S(1)}, u32[]{:S(2)}, u32[]{:S(2)}) collective-permute-start(f32[56,64]{0,1:T(8,128)S(1)} %get-tuple-element.30), channel_id=1, source_target_pairs={{0,4},{4,8},{8,12},{12,16},{16,20},{20,24},{24,28},{28,32},{32,36}... | collective-permute-start | bytes 43016 | tf_op jit(solution)/shard_map/ppermute | solution.py:24
  34.6 5.2 %collective-permute-start.3 = (f32[56,64]{0,1:T(8,128)S(1)}, f32[56,64]{0,1:T(8,128)S(1)}, u32[]{:S(2)}, u32[]{:S(2)}) collective-permute-start(f32[56,64]{0,1:T(8,128)S(1)} %get-tuple-element.31), channel_id=1, source_target_pairs={{4,0},{8,4},{12,8},{16,12},{20,16},{24,20},{28,24},{32,28},{36,32}... | collective-permute-start | bytes 43016 | tf_op jit(solution)/shard_map/ppermute | solution.py:25
  39.9 4.3 %collective-permute-start.4 = (bf16[56,64]{0,1:T(8,128)(2,1)S(1)}, bf16[56,64]{0,1:T(8,128)(2,1)S(1)}, u32[]{:S(2)}, u32[]{:S(2)}) collective-permute-start(bf16[56,64]{0,1:T(8,128)(2,1)S(1)} %get-tuple-element.34), channel_id=1, source_target_pairs={{0,4},{4,8},{8,12},{12,16},{16,20},{20,24},{24,28},{28,32},{32,36}... | collective-permute-start | bytes 21512 | tf_op jit(solution)/shard_map/ppermute | solution.py:24
  41.8 5.1 %collective-permute-start.5 = (bf16[56,64]{0,1:T(8,128)(2,1)S(1)}, bf16[56,64]{0,1:T(8,128)(2,1)S(1)}, u32[]{:S(2)}, u32[]{:S(2)}) collective-permute-start(bf16[56,64]{0,1:T(8,128)(2,1)S(1)} %get-tuple-element.35), channel_id=1, source_target_pairs={{4,0},{8,4},{12,8},{16,12},{20,16},{24,20},{28,24},{32,28},{36,32}... | collective-permute-start | bytes 21512 | tf_op jit(solution)/shard_map/ppermute | solution.py:25
  55.8 4.3 %collective-permute-start.6 = (f32[56,64]{0,1:T(8,128)S(1)}, f32[56,64]{0,1:T(8,128)S(1)}, u32[]{:S(2)}, u32[]{:S(2)}) collective-permute-start(f32[56,64]{0,1:T(8,128)S(1)} %get-tuple-element.28), channel_id=1, source_target_pairs={{0,4},{4,8},{8,12},{12,16},{16,20},{20,24},{24,28},{28,32},{32,36}... | collective-permute-start | bytes 43016 | tf_op jit(solution)/shard_map/ppermute | solution.py:24
  57.8 5.2 %collective-permute-start.7 = (f32[56,64]{0,1:T(8,128)S(1)}, f32[56,64]{0,1:T(8,128)S(1)}, u32[]{:S(2)}, u32[]{:S(2)}) collective-permute-start(f32[56,64]{0,1:T(8,128)S(1)} %get-tuple-element.29), channel_id=1, source_target_pairs={{4,0},{8,4},{12,8},{16,12},{20,16},{24,20},{28,24},{32,28},{36,32}... | collective-permute-start | bytes 43016 | tf_op jit(solution)/shard_map/ppermute | solution.py:25
  63.1 4.3 %collective-permute-start.8 = (bf16[56,64]{0,1:T(8,128)(2,1)S(1)}, bf16[56,64]{0,1:T(8,128)(2,1)S(1)}, u32[]{:S(2)}, u32[]{:S(2)}) collective-permute-start(bf16[56,64]{0,1:T(8,128)(2,1)S(1)} %get-tuple-element.32), channel_id=1, source_target_pairs={{0,4},{4,8},{8,12},{12,16},{16,20},{20,24},{24,28},{28,32},{32,36}... | collective-permute-start | bytes 21512 | tf_op jit(solution)/shard_map/ppermute | solution.py:24
  65.0 6.2 %collective-permute-start.9 = (bf16[56,64]{0,1:T(8,128)(2,1)S(1)}, bf16[56,64]{0,1:T(8,128)(2,1)S(1)}, u32[]{:S(2)}, u32[]{:S(2)}) collective-permute-start(bf16[56,64]{0,1:T(8,128)(2,1)S(1)} %get-tuple-element.33), channel_id=1, source_target_pairs={{4,0},{8,4},{12,8},{16,12},{20,16},{24,20},{28,24},{32,28},{36,32}... | collective-permute-start | bytes 21512 | tf_op jit(solution)/shard_map/ppermute | solution.py:25
  80.2 4.3 %collective-permute-start.10 = (f32[56,64]{0,1:T(8,128)S(1)}, f32[56,64]{0,1:T(8,128)S(1)}, u32[]{:S(2)}, u32[]{:S(2)}) collective-permute-start(f32[56,64]{0,1:T(8,128)S(1)} %get-tuple-element.26), channel_id=1, source_target_pairs={{0,4},{4,8},{8,12},{12,16},{16,20},{20,24},{24,28},{28,32},{32,36}... | collective-permute-start | bytes 43016 | tf_op jit(solution)/shard_map/ppermute | solution.py:24
  82.2 6.4 %collective-permute-start.11 = (f32[56,64]{0,1:T(8,128)S(1)}, f32[56,64]{0,1:T(8,128)S(1)}, u32[]{:S(2)}, u32[]{:S(2)}) collective-permute-start(f32[56,64]{0,1:T(8,128)S(1)} %get-tuple-element.27), channel_id=1, source_target_pairs={{4,0},{8,4},{12,8},{16,12},{20,16},{24,20},{28,24},{32,28},{36,32}... | collective-permute-start | bytes 43016 | tf_op jit(solution)/shard_map/ppermute | solution.py:25
  359.9 10.2 %all-to-all-start.1 = ((f32[4,224,56]{1,2,0:T(8,128)}), f32[4,224,56]{1,2,0:T(8,128)S(1)}, u32[]{:S(2)}, u32[]{:S(2)}) async-start(f32[4,224,56]{1,2,0:T(8,128)} %broadcast_in_dim.21), calls=%async_computation.1 | async-start | bytes 458752 | tf_op jit(solution)/shard_map/all_to_all | solution.py:38
Sparse Core Ops, SparseCore 0:
  100.5 253.8 all-gather.3
where the time goes:
time: 434 us; the launch traced here: 432 us
  waiting for transfers between devices  277 us (64%)
  other arithmetic  77.4 us (18%)
  starting transfers between devices  38.9 us (9%)
  between operations  15.3 us (4%)
  blocking collectives  10.7 us (2%)
  local copies, waits for them, and re-layouts  8.82 us (2%)
  matrix products  4.86 us (1%)
    all_gather x1, waiting for transfers between devices, gathered_total(): pieces = lax.all_gather(shard, axis)  254 us
    another operation x7, other arithmetic, shards(): lower = jnp.linalg.cholesky(margin)  31.7 us
    ppermute x6, starting transfers between devices, with_halo(): after = lax.ppermute(leading, axis, down)  20.3 us
    another operation x6, other arithmetic, shards(): lax.linalg.triangular_solve(lower, identity, left_side=True, lower=True)  19.8 us
    scatter-add x3, other arithmetic, apply_operator(): partial_value = jnp.zeros((band_count, NODE_EXT), jnp.float32).at[:, loca...  18.3 us
    ppermute x6, waiting for transfers between devices, with_halo(): after = lax.ppermute(leading, axis, down)  16 us
    ppermute x6, starting transfers between devices, with_halo(): before = lax.ppermute(last, axis, up)  15 us
    all_to_all x1, blocking collectives, from_everyone(): return lax.all_to_all(copies, axis, split_axis=0, concat_axis=0, tiled=True)  10.7 us
  transfers between devices with their start and end apart: 14, of which 7 were waited for; matrix products, arithmetic and copies ran while one was open for 0% of the time, Pallas kernels for 0%

commit v1 on v0

v1 whole, which is shorter than its diff:
```python
import jax
import jax.numpy as jnp
from jax import lax
from jax.sharding import Mesh, PartitionSpec as P

CELL_NODES = 729
BANDS = 224
BLOCK = 56
NODE_DEV = 512
SHARED = 64
NODE_EXT = 640
EDGE = 2 * SHARED
CELLS = ("yh", "x", "z", "core")
INNER = ("z", "core")
OUTER = ("yh", "x", "bands")
N_CELLS = 192
N_INNER = 24
N_OUTER = 32
ROWS = 4
UP = [(i, i + 1) for i in range(N_CELLS - 1)]
DOWN = [(j, i) for i, j in UP]

filter_center = 2.75
filter_half = 2.25


def exchange(to_right, to_left):
    from_left = lax.ppermute(to_right, CELLS, UP)
    from_right = lax.ppermute(to_left, CELLS, DOWN)
    return from_left, from_right


def from_everyone(shard, axis, size):
    copies = jnp.broadcast_to(shard, (size, *shard.shape))
    return lax.all_to_all(copies, axis, split_axis=0, concat_axis=0, tiled=True)


def split(value):
    high = lax.reduce_precision(value, 8, 7)
    return high.astype(jnp.bfloat16), (value - high).astype(jnp.bfloat16)


def dot(a, b, dims):
    return lax.dot_general(a, b, (dims, ((), ())), preferred_element_type=jnp.float32)


def assembled(cell_ham, local_index):
    nodes = lax.broadcasted_iota(jnp.int32, (CELL_NODES, NODE_EXT), 1)
    pick = (local_index[:, None] == nodes).astype(jnp.bfloat16)
    high, low = split(dot(cell_ham, pick, ((1,), (0,))))
    total = dot(pick, high, ((0,), (0,))) + dot(pick, low, ((0,), (0,)))
    return split(total)


def next_term(applied, current, previous):
    shifted = (applied - filter_center * current.astype(jnp.float32)) / filter_half
    if previous is None:
        return shifted.astype(jnp.bfloat16)
    return (2.0 * shifted - previous.astype(jnp.float32)).astype(jnp.bfloat16)


def packed_gram(gathered, third, band):
    full = dot(gathered, third, ((1,), (1,))).reshape(4, BLOCK, BLOCK)
    here = lax.dynamic_index_in_dim(full, band, 0, False)
    one = lax.dynamic_index_in_dim(full, (band + 1) % 4, 0, False)
    two = lax.dynamic_index_in_dim(full, (band + 2) % 4, 0, False)
    half = BLOCK // 2
    top = jnp.concatenate([here, one], axis=1)
    bottom = jnp.concatenate([two[:half], two[half:]], axis=1)
    rows = jnp.concatenate([top, bottom], axis=0)
    rows = jnp.pad(rows, ((0, N_INNER * ROWS - rows.shape[0]), (0, 128 - rows.shape[1])))
    return rows.reshape(N_INNER, ROWS, 128)


def unpacked_gram(rows):
    half = BLOCK // 2
    blocks = {}
    for b in range(4):
        here = rows[b, :BLOCK, :BLOCK]
        one = rows[b, :BLOCK, BLOCK : 2 * BLOCK]
        low = rows[b, BLOCK : BLOCK + half]
        two = jnp.concatenate([low[:, :BLOCK], low[:, BLOCK : 2 * BLOCK]], axis=0)
        c, d = (b + 1) % 4, (b + 2) % 4
        blocks[b, b] = here
        blocks[c, b] = one
        blocks[b, c] = one.T
        blocks[d, b] = two
    return jnp.concatenate([jnp.concatenate([blocks[i, j] for j in range(4)], axis=1) for i in range(4)], axis=0)


def shards(start_bands, cell_ham, node_index):
    partition = lax.axis_index(CELLS)
    band = lax.axis_index("bands")
    left, right = exchange(start_bands[:, NODE_DEV - SHARED :], start_bands[:, :SHARED])
    local_index = node_index.reshape(-1) - partition * NODE_DEV
    high, low = assembled(cell_ham[0], local_index)
    node = lax.broadcasted_iota(jnp.int32, (1, NODE_EXT), 1) + partition * NODE_DEV
    inside = (node >= SHARED) & (node < SHARED + N_CELLS * NODE_DEV)

    def applied(bands_now):
        partial = dot(bands_now, high, ((1,), (0,))) + dot(bands_now, low, ((1,), (0,)))
        from_left, from_right = exchange(partial[:, NODE_EXT - EDGE :], partial[:, :EDGE])
        zeros = jnp.zeros((BLOCK, NODE_EXT - 2 * EDGE), jnp.float32)
        return jnp.where(inside, partial + jnp.concatenate([from_left, zeros, from_right], axis=1), 0.0)

    start = jnp.concatenate([left, start_bands, right], axis=1)
    first = next_term(applied(start), start, None)
    second = next_term(applied(first), first, start)
    third = next_term(applied(second), second, first)[:, SHARED : SHARED + NODE_DEV]

    gathered = from_everyone(third, "bands", 4).reshape(BANDS, NODE_DEV)
    rows = packed_gram(gathered, third, band)
    rows = lax.all_to_all(rows, INNER, split_axis=0, concat_axis=0, tiled=True).sum(axis=0)
    rows = from_everyone(rows, OUTER, N_OUTER).reshape(8, 4, ROWS, 128).sum(axis=0)
    rows = from_everyone(rows, INNER, N_INNER)
    rows = jnp.swapaxes(rows, 0, 1).reshape(4, N_INNER * ROWS, 128)
    margin = unpacked_gram(rows) / float(NODE_DEV * N_CELLS)

    lower = jnp.linalg.cholesky(margin)
    identity = jnp.eye(BANDS, dtype=jnp.float32)
    inverse = lax.linalg.triangular_solve(lower, identity, left_side=True, lower=True)
    band_rows = lax.dynamic_slice_in_dim(inverse, band * BLOCK, BLOCK, 0).astype(jnp.bfloat16)
    return dot(band_rows, gathered, ((1,), (0,))).astype(jnp.bfloat16)


def solution(mesh):
    inner = Mesh(mesh.devices.reshape(2, 4, 12, 2, 4), ("yh", "x", "z", "core", "bands"))
    return jax.shard_map(
        shards,
        mesh=inner,
        in_specs=(P("bands", CELLS), P(CELLS, None, None), P(CELLS, None)),
        out_specs=P("bands", CELLS),
        check_vma=False,
    )
```

time: 434 us -> 195 us (0.45)
  waiting for transfers between devices: 277 us -> 29.1 us
  blocking collectives: 10.7 us -> 63.2 us
  other arithmetic: 77.4 us -> 53.4 us
  between operations: 15.3 us -> 1.76 us
  local copies, waits for them, and re-layouts: 8.82 us -> 3.55 us
    all_gather x1 -> x0, waiting for transfers between devices: 254 us -> none  [gathered_total(): pieces = lax.all_gather(shard, axis)]
    all_to_all x1, blocking collectives: 10.7 us -> 37.8 us  [from_everyone(): return lax.all_to_all(copies, axis, split_axis=0, concat_axis=0, tiled=True)]
    all_to_all x0 -> x1, blocking collectives: none -> 25.5 us  [shards(): lax.all_to_all(rows, INNER, split_axis=0, concat_axis=0, tiled=True)]
    scatter-add x3 -> x0, other arithmetic: 18.3 us -> none  [apply_operator(): partial_value = jnp.zeros((band_count, NODE_EXT), jnp.float32).at[:, loca...]
    all_to_all x1 -> x2, waiting for transfers between devices: 6.53 us -> 20.9 us  [from_everyone(): return lax.all_to_all(copies, axis, split_axis=0, concat_axis=0, tiled=True)]
    ppermute x12 -> x8, starting transfers between devices: 35.3 us -> 26.6 us  [the longest x4 15.5 us: exchange(): from_right = lax.ppermute(to_left, CELLS, DOWN)]
    ppermute x12 -> x8, waiting for transfers between devices: 16 us -> 8.21 us  [the longest x4 8.2 us: exchange(): from_right = lax.ppermute(to_left, CELLS, DOWN)]
    gather x3 -> x0, local copies, waits for them, and re-layouts: 6.14 us -> none  [apply_operator(): jnp.take(widened, local_index, axis=1)]
  transfers between devices with their start and end apart: 14 -> 10, of which waited for: 7 -> 5; matrix products, arithmetic and copies ran while one was open for 0% -> 2% of each run, Pallas kernels for 0% -> 0%
where the time goes in v1:
time: 195 us
  blocking collectives  63.2 us (32%)
  other arithmetic  53.4 us (27%)
  starting transfers between devices  35.6 us (18%)
  waiting for transfers between devices  29.1 us (15%)
  matrix products  7.91 us (4%)
  local copies, waits for them, and re-layouts  3.55 us (2%)
    all_to_all x1, blocking collectives, from_everyone(): return lax.all_to_all(copies, axis, split_axis=0, concat_axis=0, tiled=True)  37.8 us
    another operation x7, other arithmetic, shards(): lower = jnp.linalg.cholesky(margin)  31.6 us
    all_to_all x1, blocking collectives, shards(): lax.all_to_all(rows, INNER, split_axis=0, concat_axis=0, tiled=True)  25.5 us
    all_to_all x2, waiting for transfers between devices, from_everyone(): return lax.all_to_all(copies, axis, split_axis=0, concat_axis=0, tiled=True)  20.9 us
    another operation x6, other arithmetic, shards(): lax.linalg.triangular_solve(lower, identity, left_side=True, lower=True)  19.8 us
    ppermute x4, starting transfers between devices, exchange(): from_right = lax.ppermute(to_left, CELLS, DOWN)  15.5 us
    ppermute x4, starting transfers between devices, exchange(): from_left = lax.ppermute(to_right, CELLS, UP)  11.1 us
    all_to_all x2, starting transfers between devices, from_everyone(): return lax.all_to_all(copies, axis, split_axis=0, concat_axis=0, tiled=True)  8.95 us
  transfers between devices with their start and end apart: 10, of which 5 were waited for; matrix products, arithmetic and copies ran while one was open for 2% of the time, Pallas kernels for 0%

profile of v1, /device:TPU:1, one launch (start us, length us, event | category | flops | bytes accessed | tf_op | source)
XLA Modules:
  0.0 194.6 jit_solution(2710320464916635005)
XLA Ops:
  0.0 0.9 fusion.56
  0.9 5.4 %collective-permute-start = (bf16[56,64]{1,0:T(8,128)(2,1)S(1)}, bf16[56,64]{1,0:T(8,128)(2,1)S(1)}, u32[]{:S(2)}, u32[]{:S(2)}) collective-permute-start(bf16[56,64]{1,0:T(8,128)(2,1)S(1)} %get-tuple-element.57), channel_id=1, source_target_pairs={{0,4},{4,8},{8,12},{12,16},{16,20},{20,24},{24,28},{28,32},{32,36}... | collective-permute-start | bytes 21512 | tf_op jit(solution)/shard_map/ppermute | solution.py:28
  6.3 8.3 %collective-permute-start.1 = (bf16[56,64]{1,0:T(8,128)(2,1)S(1)}, bf16[56,64]{1,0:T(8,128)(2,1)S(1)}, u32[]{:S(2)}, u32[]{:S(2)}) collective-permute-start(bf16[56,64]{1,0:T(8,128)(2,1)S(1)} %get-tuple-element.58), channel_id=1, source_target_pairs={{4,0},{8,4},{12,8},{16,12},{20,16},{24,20},{28,24},{32,28},{36,32}... | collective-permute-start | bytes 21512 | tf_op jit(solution)/shard_map/ppermute | solution.py:29
  14.6 0.7 subtract_reduce_fusion
  15.3 1.2 fusion.3
  16.5 1.2 fusion.1
  17.7 1.2 fusion.5
  19.0 0.3 fusion.43
  19.3 0.3 convolution_add_fusion.2
  19.6 1.9 collective-permute-start.2
  21.6 2.4 %collective-permute-start.3 = (f32[56,128]{1,0:T(8,128)S(1)}, f32[56,128]{1,0:T(8,128)S(1)}, u32[]{:S(2)}, u32[]{:S(2)}) collective-permute-start(f32[56,128]{1,0:T(8,128)S(1)} %get-tuple-element.46), channel_id=1, source_target_pairs={{4,0},{8,4},{12,8},{16,12},{20,16},{24,20},{28,24},{32,28},{36,32}... | collective-permute-start | bytes 86024 | tf_op jit(solution)/shard_map/ppermute | solution.py:29
  24.0 2.7 %collective-permute-done.3 = f32[56,128]{1,0:T(8,128)S(1)} collective-permute-done((f32[56,128]{1,0:T(8,128)S(1)}, f32[56,128]{1,0:T(8,128)S(1)}, u32[]{:S(2)}, u32[]{:S(2)}) %collective-permute-start.3) | collective-permute-done | bytes 28704 | tf_op jit(solution)/shard_map/ppermute | solution.py:29
  26.9 0.3 fusion.45
  27.1 0.3 convolution_add_fusion.1
  27.4 1.9 collective-permute-start.4
  29.4 2.4 %collective-permute-start.5 = (f32[56,128]{1,0:T(8,128)S(1)}, f32[56,128]{1,0:T(8,128)S(1)}, u32[]{:S(2)}, u32[]{:S(2)}) collective-permute-start(f32[56,128]{1,0:T(8,128)S(1)} %get-tuple-element.44), channel_id=1, source_target_pairs={{4,0},{8,4},{12,8},{16,12},{20,16},{24,20},{28,24},{32,28},{36,32}... | collective-permute-start | bytes 86024 | tf_op jit(solution)/shard_map/ppermute | solution.py:29
  31.8 2.8 %collective-permute-done.5 = f32[56,128]{1,0:T(8,128)S(1)} collective-permute-done((f32[56,128]{1,0:T(8,128)S(1)}, f32[56,128]{1,0:T(8,128)S(1)}, u32[]{:S(2)}, u32[]{:S(2)}) %collective-permute-start.5) | collective-permute-done | bytes 28704 | tf_op jit(solution)/shard_map/ppermute | solution.py:29
  34.7 0.3 fusion.44
  34.9 0.3 convolution_add_fusion
  35.3 1.9 collective-permute-start.6
  37.2 2.4 %collective-permute-start.7 = (f32[56,128]{1,0:T(8,128)S(1)}, f32[56,128]{1,0:T(8,128)S(1)}, u32[]{:S(2)}, u32[]{:S(2)}) collective-permute-start(f32[56,128]{1,0:T(8,128)S(1)} %get-tuple-element.42), channel_id=1, source_target_pairs={{4,0},{8,4},{12,8},{16,12},{20,16},{24,20},{28,24},{32,28},{36,32}... | collective-permute-start | bytes 86024 | tf_op jit(solution)/shard_map/ppermute | solution.py:29
  39.7 2.7 %collective-permute-done.7 = f32[56,128]{1,0:T(8,128)S(1)} collective-permute-done((f32[56,128]{1,0:T(8,128)S(1)}, f32[56,128]{1,0:T(8,128)S(1)}, u32[]{:S(2)}, u32[]{:S(2)}) %collective-permute-start.7) | collective-permute-done | bytes 28704 | tf_op jit(solution)/shard_map/ppermute | solution.py:29
  42.4 0.2 fusion.24
  42.6 0.7 broadcast_in_dim.34
  43.3 3.4 %all-to-all-start = ((bf16[4,56,512]{2,1,0:T(8,128)(2,1)}), bf16[4,56,512]{2,1,0:T(8,128)(2,1)S(1)}, u32[]{:S(2)}, u32[]{:S(2)}) async-start(bf16[4,56,512]{2,1,0:T(8,128)(2,1)} %broadcast_in_dim.34), calls=%async_computation | async-start | bytes 458752 | tf_op jit(solution)/shard_map/all_to_all | solution.py:35
  46.7 7.3 %all-to-all-done = bf16[4,56,512]{2,1,0:T(8,128)(2,1)S(1)} async-done(((bf16[4,56,512]{2,1,0:T(8,128)(2,1)}), bf16[4,56,512]{2,1,0:T(8,128)(2,1)S(1)}, u32[]{:S(2)}, u32[]{:S(2)}) %all-to-all-start) | async-done | bytes 229408 | tf_op jit(solution)/shard_map/all_to_all | solution.py:35
  54.0 0.2 fusion.32
  54.3 25.5 %all_to_all.20 = f32[24,4,128]{2,1,0:T(4,128)S(1)} all-to-all(f32[24,4,128]{2,1,0:T(4,128)S(1)} %bitcast.100), channel_id=1, replica_groups=mesh['yh'=2,'x'=4,'z'=12,'core'=2,'bands'=4] {'z','core'}, dimensions={0} | all-to-all | bytes 98304 | tf_op jit(solution)/shard_map/all_to_all | solution.py:113
  79.8 37.8 %all_to_all.21 = f32[32,4,128]{2,1,0:T(4,128)S(1)} all-to-all(f32[32,4,128]{2,1,0:T(4,128)S(1)} %broadcast_in_dim.35), channel_id=1, replica_groups=mesh['yh'=2,'x'=4,'z'=12,'core'=2,'bands'=4] {'yh','x','bands'}, dimensions={0} | all-to-all | bytes 131072 | tf_op jit(solution)/shard_map/all_to_all | solution.py:35
  117.6 0.7 broadcast_in_dim.36
  118.3 5.6 %all-to-all-start.3 = ((f32[24,4,4,128]{3,2,1,0:T(4,128)}), f32[24,4,4,128]{3,2,1,0:T(4,128)S(1)}, u32[]{:S(2)}, u32[]{:S(2)}) async-start(f32[24,4,4,128]{3,2,1,0:T(4,128)} %broadcast_in_dim.36), calls=%async_computation.3 | async-start | bytes 393216 | tf_op jit(solution)/shard_map/all_to_all | solution.py:35
  124.0 13.6 %all-to-all-done.3 = f32[24,4,4,128]{3,2,1,0:T(4,128)S(1)} async-done(((f32[24,4,4,128]{3,2,1,0:T(4,128)}), f32[24,4,4,128]{3,2,1,0:T(4,128)S(1)}, u32[]{:S(2)}, u32[]{:S(2)}) %all-to-all-start.3) | async-done | bytes 196640 | tf_op jit(solution)/shard_map/all_to_all | solution.py:35
  138.2 0.1 pad_maximum_fusion.4
  138.8 0.2 maximum_multiply_fusion
  139.1 0.1 copy.67
  139.2 0.2 fusion.11
  139.4 11.7 %cholesky.51 = f32[128,128]{1,0:T(8,128)S(1)} custom-call(f32[128,128]{1,0:T(8,128)S(1)} %cholesky.124), custom_call_target="Cholesky" | custom-call | tf_op jit(solution)/shard_map/jit(cholesky)/cholesky | solution.py:119
  151.2 9.8 %custom-call.14 = f32[1,128,128]{1,2,0:T(8,128)S(1)} custom-call(f32[1,128,128]{2,1,0:T(8,128)S(1)} %get-tuple-element.52), custom_call_target="InvertDiagBlocksLowerTriangular" | custom-call | tf_op jit(solution)/shard_map/jit(cholesky)/cholesky | solution.py:119
  161.0 0.2 constant_dynamic-update-slice_fusion
  161.2 0.2 convolution_subtract_fusion.1
  161.5 8.8 %cholesky.110 = f32[96,96]{1,0:T(8,128)S(1)} custom-call(f32[96,96]{1,0:T(8,128)S(1)} %convolution_subtract_fusion.1), custom_call_target="Cholesky" | custom-call | tf_op jit(solution)/shard_map/jit(cholesky)/cholesky | solution.py:119
  170.3 0.6 compare_reduce_fusion
  170.9 0.6 compare_reduce_fusion.1
  172.9 19.7 %custom-call.15 = f32[2,128,128]{1,2,0:T(8,128)S(1)} custom-call(f32[2,128,128]{2,1,0:T(8,128)S(1)} %pad_maximum_fusion.1), custom_call_target="InvertDiagBlocksLowerTriangular" | custom-call | tf_op jit(solution)/shard_map/triangular_solve | solution.py:121
  192.6 0.3 fusion.20
  192.9 0.4 convolution_subtract_fusion
  193.3 0.4 fusion.35
  193.7 0.9 convolution_convert_fusion
  (51 shorter events, 1.9 us)
Async XLA Ops:
  0.0 15.3 %copy-start = (bf16[1,729,729]{2,1,0:T(8,128)(2,1)S(1)}, bf16[1,729,729]{2,1,0:T(8,128)(2,1)}, u32[]{:S(2)}) copy-start(bf16[1,729,729]{2,1,0:T(8,128)(2,1)} %param.4) | copy-start | bytes 3188650
  0.9 18.0 %collective-permute-start = (bf16[56,64]{1,0:T(8,128)(2,1)S(1)}, bf16[56,64]{1,0:T(8,128)(2,1)S(1)}, u32[]{:S(2)}, u32[]{:S(2)}) collective-permute-start(bf16[56,64]{1,0:T(8,128)(2,1)S(1)} %get-tuple-element.57), channel_id=1, source_target_pairs={{0,4},{4,8},{8,12},{12,16},{16,20},{20,24},{24,28},{28,32},{32,36}... | collective-permute-start | bytes 21512 | tf_op jit(solution)/shard_map/ppermute | solution.py:28
  6.3 12.7 %collective-permute-start.1 = (bf16[56,64]{1,0:T(8,128)(2,1)S(1)}, bf16[56,64]{1,0:T(8,128)(2,1)S(1)}, u32[]{:S(2)}, u32[]{:S(2)}) collective-permute-start(bf16[56,64]{1,0:T(8,128)(2,1)S(1)} %get-tuple-element.58), channel_id=1, source_target_pairs={{4,0},{8,4},{12,8},{16,12},{20,16},{24,20},{28,24},{32,28},{36,32}... | collective-permute-start | bytes 21512 | tf_op jit(solution)/shard_map/ppermute | solution.py:29
  17.7 1.2 copy-start.1
  19.6 4.4 %collective-permute-start.2 = (f32[56,128]{1,0:T(8,128)S(1)}, f32[56,128]{1,0:T(8,128)S(1)}, u32[]{:S(2)}, u32[]{:S(2)}) collective-permute-start(f32[56,128]{1,0:T(8,128)S(1)} %get-tuple-element.45), channel_id=1, source_target_pairs={{0,4},{4,8},{8,12},{12,16},{16,20},{20,24},{24,28},{28,32},{32,36}... | collective-permute-start | bytes 86024 | tf_op jit(solution)/shard_map/ppermute | solution.py:28
  21.6 5.2 %collective-permute-start.3 = (f32[56,128]{1,0:T(8,128)S(1)}, f32[56,128]{1,0:T(8,128)S(1)}, u32[]{:S(2)}, u32[]{:S(2)}) collective-permute-start(f32[56,128]{1,0:T(8,128)S(1)} %get-tuple-element.46), channel_id=1, source_target_pairs={{4,0},{8,4},{12,8},{16,12},{20,16},{24,20},{28,24},{32,28},{36,32}... | collective-permute-start | bytes 86024 | tf_op jit(solution)/shard_map/ppermute | solution.py:29
  27.4 4.3 %collective-permute-start.4 = (f32[56,128]{1,0:T(8,128)S(1)}, f32[56,128]{1,0:T(8,128)S(1)}, u32[]{:S(2)}, u32[]{:S(2)}) collective-permute-start(f32[56,128]{1,0:T(8,128)S(1)} %get-tuple-element.43), channel_id=1, source_target_pairs={{0,4},{4,8},{8,12},{12,16},{16,20},{20,24},{24,28},{28,32},{32,36}... | collective-permute-start | bytes 86024 | tf_op jit(solution)/shard_map/ppermute | solution.py:28
  29.4 5.2 %collective-permute-start.5 = (f32[56,128]{1,0:T(8,128)S(1)}, f32[56,128]{1,0:T(8,128)S(1)}, u32[]{:S(2)}, u32[]{:S(2)}) collective-permute-start(f32[56,128]{1,0:T(8,128)S(1)} %get-tuple-element.44), channel_id=1, source_target_pairs={{4,0},{8,4},{12,8},{16,12},{20,16},{24,20},{28,24},{32,28},{36,32}... | collective-permute-start | bytes 86024 | tf_op jit(solution)/shard_map/ppermute | solution.py:29
  35.3 4.4 %collective-permute-start.6 = (f32[56,128]{1,0:T(8,128)S(1)}, f32[56,128]{1,0:T(8,128)S(1)}, u32[]{:S(2)}, u32[]{:S(2)}) collective-permute-start(f32[56,128]{1,0:T(8,128)S(1)} %get-tuple-element.41), channel_id=1, source_target_pairs={{0,4},{4,8},{8,12},{12,16},{16,20},{20,24},{24,28},{28,32},{32,36}... | collective-permute-start | bytes 86024 | tf_op jit(solution)/shard_map/ppermute | solution.py:28
  37.2 5.2 %collective-permute-start.7 = (f32[56,128]{1,0:T(8,128)S(1)}, f32[56,128]{1,0:T(8,128)S(1)}, u32[]{:S(2)}, u32[]{:S(2)}) collective-permute-start(f32[56,128]{1,0:T(8,128)S(1)} %get-tuple-element.42), channel_id=1, source_target_pairs={{4,0},{8,4},{12,8},{16,12},{20,16},{24,20},{28,24},{32,28},{36,32}... | collective-permute-start | bytes 86024 | tf_op jit(solution)/shard_map/ppermute | solution.py:29
  43.3 10.7 %all-to-all-start = ((bf16[4,56,512]{2,1,0:T(8,128)(2,1)}), bf16[4,56,512]{2,1,0:T(8,128)(2,1)S(1)}, u32[]{:S(2)}, u32[]{:S(2)}) async-start(bf16[4,56,512]{2,1,0:T(8,128)(2,1)} %broadcast_in_dim.34), calls=%async_computation | async-start | bytes 458752 | tf_op jit(solution)/shard_map/all_to_all | solution.py:35
  118.3 19.2 %all-to-all-start.3 = ((f32[24,4,4,128]{3,2,1,0:T(4,128)}), f32[24,4,4,128]{3,2,1,0:T(4,128)S(1)}, u32[]{:S(2)}, u32[]{:S(2)}) async-start(f32[24,4,4,128]{3,2,1,0:T(4,128)} %broadcast_in_dim.36), calls=%async_computation.3 | async-start | bytes 393216 | tf_op jit(solution)/shard_map/all_to_all | solution.py:35

commit v2 on v1

--- a/solution.py
+++ b/solution.py
@@ -1,6 +1,8 @@
 import jax
 import jax.numpy as jnp
 from jax import lax
+from jax.experimental import pallas as pl
+from jax.experimental.pallas import tpu as pltpu
 from jax.sharding import Mesh, PartitionSpec as P
 
 CELL_NODES = 729
@@ -11,23 +13,22 @@
 NODE_EXT = 640
 EDGE = 2 * SHARED
 CELLS = ("yh", "x", "z", "core")
-INNER = ("z", "core")
+SPREAD = ("yh", "x")
 OUTER = ("yh", "x", "bands")
 N_CELLS = 192
-N_INNER = 24
-N_OUTER = 32
-ROWS = 4
-UP = [(i, i + 1) for i in range(N_CELLS - 1)]
-DOWN = [(j, i) for i, j in UP]
+ROWS = 12
+PANEL = 32
+SWAPS = [(i, i + 1) for i in range(1, N_CELLS - 1, 2)] + [(i + 1, i) for i in range(1, N_CELLS - 1, 2)]
 
 filter_center = 2.75
 filter_half = 2.25
 
 
 def exchange(to_right, to_left):
-    from_left = lax.ppermute(to_right, CELLS, UP)
-    from_right = lax.ppermute(to_left, CELLS, DOWN)
-    return from_left, from_right
+    first_cell = lax.axis_index("core") == 0
+    outer = lax.ppermute(jnp.where(first_cell, to_left, to_right), CELLS, SWAPS)
+    inner = lax.ppermute(jnp.where(first_cell, to_right, to_left), "core", [(0, 1), (1, 0)])
+    return jnp.where(first_cell, outer, inner), jnp.where(first_cell, inner, outer)
 
 
 def from_everyone(shard, axis, size):
@@ -68,8 +69,8 @@
     top = jnp.concatenate([here, one], axis=1)
     bottom = jnp.concatenate([two[:half], two[half:]], axis=1)
     rows = jnp.concatenate([top, bottom], axis=0)
-    rows = jnp.pad(rows, ((0, N_INNER * ROWS - rows.shape[0]), (0, 128 - rows.shape[1])))
-    return rows.reshape(N_INNER, ROWS, 128)
+    rows = jnp.pad(rows, ((0, 8 * ROWS - rows.shape[0]), (0, 128 - rows.shape[1])))
+    return rows.reshape(8, 3, 4, 128)
 
 
 def unpacked_gram(rows):
@@ -86,6 +87,44 @@
         blocks[b, c] = one.T
         blocks[d, b] = two
     return jnp.concatenate([jnp.concatenate([blocks[i, j] for j in range(4)], axis=1) for i in range(4)], axis=0)
+
+
+def exact_dot(a, b, dims):
+    return lax.dot_general(a, b, (dims, ((), ())), precision=lax.Precision.HIGHEST, preferred_element_type=jnp.float32)
+
+
+def inverse_factor_kernel(margin_ref, inverse_ref, left_ref):
+    left_ref[...] = margin_ref[...]
+    at_row = lax.broadcasted_iota(jnp.int32, (BANDS, BANDS), 0)
+    at_column = lax.broadcasted_iota(jnp.int32, (BANDS, BANDS), 1)
+    inverse_ref[...] = (at_row == at_column).astype(jnp.float32)
+    row = lax.broadcasted_iota(jnp.int32, (PANEL, PANEL), 0)
+    diagonal = row == lax.broadcasted_iota(jnp.int32, (PANEL, PANEL), 1)
+    for start in range(0, BANDS, PANEL):
+        stop = start + PANEL
+        both = jnp.concatenate([left_ref[start:stop, start:stop], diagonal.astype(jnp.float32)], axis=1)
+        for j in range(PANEL):
+            factor = both[:, j : j + 1] * (1.0 / both[j : j + 1, j : j + 1])
+            both = both - jnp.where(row[:, :1] > j, factor, 0.0) * both[j : j + 1, :]
+        pivots = jnp.sum(jnp.where(diagonal, both[:, :PANEL], 0.0), axis=1, keepdims=True)
+        scaled = both[:, PANEL:] * lax.rsqrt(pivots)
+        upper = exact_dot(scaled, left_ref[start:stop, :], ((1,), (0,)))
+        rows = exact_dot(scaled, inverse_ref[start:stop, :], ((1,), (0,)))
+        inverse_ref[start:stop, :] = rows
+        if stop < BANDS:
+            below = upper[:, stop:]
+            left_ref[stop:, :] = left_ref[stop:, :] - exact_dot(below, upper, ((0,), (0,)))
+            inverse_ref[stop:, :] = inverse_ref[stop:, :] - exact_dot(below, rows, ((0,), (0,)))
+
+
+def inverse_factor(margin):
+    return pl.pallas_call(
+        inverse_factor_kernel,
+        out_shape=jax.ShapeDtypeStruct((BANDS, BANDS), jnp.float32),
+        in_specs=[pl.BlockSpec(memory_space=pltpu.VMEM)],
+        out_specs=pl.BlockSpec(memory_space=pltpu.VMEM),
+        scratch_shapes=[pltpu.VMEM((BANDS, BANDS), jnp.float32)],
+    )(margin)
 
 
 def shards(start_bands, cell_ham, node_index):
@@ -110,15 +149,14 @@
 
     gathered = from_everyone(third, "bands", 4).reshape(BANDS, NODE_DEV)
     rows = packed_gram(gathered, third, band)
-    rows = lax.all_to_all(rows, INNER, split_axis=0, concat_axis=0, tiled=True).sum(axis=0)
-    rows = from_everyone(rows, OUTER, N_OUTER).reshape(8, 4, ROWS, 128).sum(axis=0)
-    rows = from_everyone(rows, INNER, N_INNER)
-    rows = jnp.swapaxes(rows, 0, 1).reshape(4, N_INNER * ROWS, 128)
+    rows = lax.all_to_all(rows, SPREAD, split_axis=0, concat_axis=0, tiled=True).sum(axis=0)
+    rows = from_everyone(rows, "z", 12).sum(axis=0)
+    rows = rows + lax.ppermute(rows, "core", [(0, 1), (1, 0)])
+    rows = from_everyone(rows, OUTER, 32).reshape(8, 4, ROWS, 128)
+    rows = jnp.swapaxes(rows, 0, 1).reshape(4, 8 * ROWS, 128)
     margin = unpacked_gram(rows) / float(NODE_DEV * N_CELLS)
 
-    lower = jnp.linalg.cholesky(margin)
-    identity = jnp.eye(BANDS, dtype=jnp.float32)
-    inverse = lax.linalg.triangular_solve(lower, identity, left_side=True, lower=True)
+    inverse = inverse_factor(margin)
     band_rows = lax.dynamic_slice_in_dim(inverse, band * BLOCK, BLOCK, 0).astype(jnp.bfloat16)
     return dot(band_rows, gathered, ((1,), (0,))).astype(jnp.bfloat16)
 

time: 195 us -> 158 us (0.81)
  other arithmetic: 53.4 us -> 3.22 us
  Pallas kernels: 0 us -> 24.6 us
  blocking collectives: 63.2 us -> 53.9 us
  starting transfers between devices: 35.6 us -> 43 us
  waiting for transfers between devices: 29.1 us -> 22 us
    another operation x13 -> x0, other arithmetic: 51.4 us -> none  [the longest x7 31.6 us: shards(): lower = jnp.linalg.cholesky(margin)]
    pallas_call x0 -> x1, Pallas kernels: none -> 24.6 us  [inverse_factor(): pl.pallas_call(inverse_factor_kernel, out_shape=jax.ShapeDtypeStruct((BAN...]
    all_to_all x1, blocking collectives: 37.8 us -> 14.6 us  [from_everyone(): return lax.all_to_all(copies, axis, split_axis=0, concat_axis=0, tiled=True)]
    all_to_all x1, blocking collectives: 25.5 us -> 39.3 us  [shards(): lax.all_to_all(rows, SPREAD, split_axis=0, concat_axis=0, tiled=True)]
    ppermute x8 -> x9, starting transfers between devices: 26.6 us -> 34.2 us  [the longest x4 13.4 us: exchange(): lax.ppermute(jnp.where(first_cell, to_right, to_left), 'core', [(0, 1), (...]
    ppermute x8 -> x9, waiting for transfers between devices: 8.21 us -> 4.35 us  [the longest x4 2.09 us: exchange(): outer = lax.ppermute(jnp.where(first_cell, to_left, to_right), CELLS, SWAPS)]
    all_to_all x2, waiting for transfers between devices: 20.9 us -> 17.7 us  [from_everyone(): return lax.all_to_all(copies, axis, split_axis=0, concat_axis=0, tiled=True)]
  transfers between devices with their start and end apart: 10 -> 11, of which waited for: 5 -> 7; matrix products, arithmetic and copies ran while one was open for 2% -> 3% of each run, Pallas kernels for 0% -> 0%
where the time goes in v2:
time: 158 us; the launch traced here: 157 us
  blocking collectives  53.9 us (34%)
  starting transfers between devices  43 us (27%)
  Pallas kernels  24.6 us (16%)
  waiting for transfers between devices  22 us (14%)
  matrix products  7.17 us (5%)
  other arithmetic  3.22 us (2%)
  local copies, waits for them, and re-layouts  2.79 us (2%)
    all_to_all x1, blocking collectives, shards(): lax.all_to_all(rows, SPREAD, split_axis=0, concat_axis=0, tiled=True)  39.3 us
    pallas_call x1, Pallas kernels, inverse_factor(): pl.pallas_call(inverse_factor_kernel, out_shape=jax.ShapeDtypeStruct((BAN...  24.6 us
    all_to_all x2, waiting for transfers between devices, from_everyone(): return lax.all_to_all(copies, axis, split_axis=0, concat_axis=0, tiled=True)  17.7 us
    all_to_all x1, blocking collectives, from_everyone(): return lax.all_to_all(copies, axis, split_axis=0, concat_axis=0, tiled=True)  14.6 us
    ppermute x4, starting transfers between devices, exchange(): lax.ppermute(jnp.where(first_cell, to_right, to_left), 'core', [(0, 1), (...  13.4 us
    ppermute x4, starting transfers between devices, exchange(): outer = lax.ppermute(jnp.where(first_cell, to_left, to_right), CELLS, SWAPS)  13.1 us
    all_to_all x2, starting transfers between devices, from_everyone(): return lax.all_to_all(copies, axis, split_axis=0, concat_axis=0, tiled=True)  8.84 us
    ppermute x1, starting transfers between devices, shards(): rows = rows + lax.ppermute(rows, 'core', [(0, 1), (1, 0)])  7.64 us
  transfers between devices with their start and end apart: 11, of which 7 were waited for; matrix products, arithmetic and copies ran while one was open for 3% of the time, Pallas kernels for 0%

profile of v2, /device:TPU:1, one launch (start us, length us, event | category | flops | bytes accessed | tf_op | source)
XLA Modules:
  0.0 157.2 jit_solution(7013839412606136765)
XLA Ops:
  0.0 0.9 broadcast_select_fusion.9
  0.9 5.4 %collective-permute-start = (bf16[56,64]{1,0:T(8,128)(2,1)S(1)}, bf16[56,64]{1,0:T(8,128)(2,1)S(1)}, u32[]{:S(2)}, u32[]{:S(2)}) collective-permute-start(bf16[56,64]{1,0:T(8,128)(2,1)S(1)} %get-tuple-element.39), channel_id=1, source_target_pairs={{4,8},{12,16},{20,24},{28,32},{36,40},{44,48},{52,56},{60,64},{68,... | collective-permute-start | bytes 21512 | tf_op jit(solution)/shard_map/ppermute | solution.py:29
  6.3 7.7 %collective-permute-start.1 = (bf16[56,64]{1,0:T(8,128)(2,1)S(1)}, bf16[56,64]{1,0:T(8,128)(2,1)S(1)}, u32[]{:S(2)}, u32[]{:S(2)}) collective-permute-start(bf16[56,64]{1,0:T(8,128)(2,1)S(1)} %get-tuple-element.40), channel_id=1, source_target_pairs={{0,4},{4,0},{1,5},{5,1},{2,6},{6,2},{3,7},{7,3},{8,12},{12,8},{9,1... | collective-permute-start | bytes 21512 | tf_op jit(solution)/shard_map/ppermute | solution.py:30
  14.0 0.7 subtract_reduce_fusion
  14.7 1.2 fusion.3
  15.9 1.2 fusion.1
  17.1 1.2 fusion.5
  18.4 0.3 fusion.30
  18.7 0.3 convolution_add_fusion.2
  19.0 1.9 %collective-permute-start.2 = (f32[56,128]{1,0:T(8,128)S(1)}, f32[56,128]{1,0:T(8,128)S(1)}, u32[]{:S(2)}, u32[]{:S(2)}) collective-permute-start(f32[56,128]{1,0:T(8,128)S(1)} %get-tuple-element.23), channel_id=1, source_target_pairs={{4,8},{12,16},{20,24},{28,32},{36,40},{44,48},{52,56},{60,64},{68,... | collective-permute-start | bytes 86024 | tf_op jit(solution)/shard_map/ppermute | solution.py:29
  21.0 1.9 %collective-permute-start.3 = (f32[56,128]{1,0:T(8,128)S(1)}, f32[56,128]{1,0:T(8,128)S(1)}, u32[]{:S(2)}, u32[]{:S(2)}) collective-permute-start(f32[56,128]{1,0:T(8,128)S(1)} %get-tuple-element.24), channel_id=1, source_target_pairs={{0,4},{4,0},{1,5},{5,1},{2,6},{6,2},{3,7},{7,3},{8,12},{12,8},{9,1... | collective-permute-start | bytes 86024 | tf_op jit(solution)/shard_map/ppermute | solution.py:30
  22.9 1.3 collective-permute-done.2
  24.2 0.1 fusion.36
  24.3 0.3 fusion.32
  24.6 0.3 convolution_add_fusion.1
  24.9 3.5 %collective-permute-start.4 = (f32[56,128]{1,0:T(8,128)S(1)}, f32[56,128]{1,0:T(8,128)S(1)}, u32[]{:S(2)}, u32[]{:S(2)}) collective-permute-start(f32[56,128]{1,0:T(8,128)S(1)} %get-tuple-element.21), channel_id=1, source_target_pairs={{4,8},{12,16},{20,24},{28,32},{36,40},{44,48},{52,56},{60,64},{68,... | collective-permute-start | bytes 86024 | tf_op jit(solution)/shard_map/ppermute | solution.py:29
  28.4 1.9 %collective-permute-start.5 = (f32[56,128]{1,0:T(8,128)S(1)}, f32[56,128]{1,0:T(8,128)S(1)}, u32[]{:S(2)}, u32[]{:S(2)}) collective-permute-start(f32[56,128]{1,0:T(8,128)S(1)} %get-tuple-element.22), channel_id=1, source_target_pairs={{0,4},{4,0},{1,5},{5,1},{2,6},{6,2},{3,7},{7,3},{8,12},{12,8},{9,1... | collective-permute-start | bytes 86024 | tf_op jit(solution)/shard_map/ppermute | solution.py:30
  30.4 1.2 collective-permute-done.5
  31.5 0.1 fusion.14
  31.6 0.3 fusion.31
  31.9 0.3 convolution_add_fusion
  32.2 2.4 %collective-permute-start.6 = (f32[56,128]{1,0:T(8,128)S(1)}, f32[56,128]{1,0:T(8,128)S(1)}, u32[]{:S(2)}, u32[]{:S(2)}) collective-permute-start(f32[56,128]{1,0:T(8,128)S(1)} %get-tuple-element.19), channel_id=1, source_target_pairs={{4,8},{12,16},{20,24},{28,32},{36,40},{44,48},{52,56},{60,64},{68,... | collective-permute-start | bytes 86024 | tf_op jit(solution)/shard_map/ppermute | solution.py:29
  34.6 1.9 %collective-permute-start.7 = (f32[56,128]{1,0:T(8,128)S(1)}, f32[56,128]{1,0:T(8,128)S(1)}, u32[]{:S(2)}, u32[]{:S(2)}) collective-permute-start(f32[56,128]{1,0:T(8,128)S(1)} %get-tuple-element.20), channel_id=1, source_target_pairs={{0,4},{4,0},{1,5},{5,1},{2,6},{6,2},{3,7},{7,3},{8,12},{12,8},{9,1... | collective-permute-start | bytes 86024 | tf_op jit(solution)/shard_map/ppermute | solution.py:30
  36.6 0.8 collective-permute-done.6
  37.4 0.3 collective-permute-done.7
  37.7 0.2 fusion.19
  37.9 0.7 broadcast_in_dim.32
  38.6 4.6 %all-to-all-start = ((bf16[4,56,512]{2,1,0:T(8,128)(2,1)}), bf16[4,56,512]{2,1,0:T(8,128)(2,1)S(1)}, u32[]{:S(2)}, u32[]{:S(2)}) async-start(bf16[4,56,512]{2,1,0:T(8,128)(2,1)} %broadcast_in_dim.32), calls=%async_computation | async-start | bytes 458752 | tf_op jit(solution)/shard_map/all_to_all | solution.py:36
  43.2 6.8 %all-to-all-done = bf16[4,56,512]{2,1,0:T(8,128)(2,1)S(1)} async-done(((bf16[4,56,512]{2,1,0:T(8,128)(2,1)}), bf16[4,56,512]{2,1,0:T(8,128)(2,1)S(1)}, u32[]{:S(2)}, u32[]{:S(2)}) %all-to-all-start) | async-done | bytes 229408 | tf_op jit(solution)/shard_map/all_to_all | solution.py:36
  50.1 0.2 fusion.23
  50.3 0.1 fusion.25
  50.4 39.3 %all_to_all.20 = f32[8,3,4,128]{3,2,1,0:T(4,128)S(1)} all-to-all(f32[8,3,4,128]{3,2,1,0:T(4,128)S(1)} %bitcast.77), channel_id=1, replica_groups=mesh['yh'=2,'x'=4,'z'=12,'core'=2,'bands'=4] {'yh','x'}, dimensions={0} | all-to-all | bytes 98304 | tf_op jit(solution)/shard_map/all_to_all | solution.py:152
  89.8 14.6 %all_to_all.21 = f32[12,3,4,128]{3,2,1,0:T(4,128)S(1)} all-to-all(f32[12,3,4,128]{3,2,1,0:T(4,128)S(1)} %broadcast_in_dim.33), channel_id=1, replica_groups=mesh['yh'=2,'x'=4,'z'=12,'core'=2,'bands'=4] {'z'}, dimensions={0} | all-to-all | bytes 147456 | tf_op jit(solution)/shard_map/all_to_all | solution.py:36
  104.4 7.6 %collective-permute-start.8 = (f32[3,4,128]{2,1,0:T(4,128)S(1)}, f32[3,4,128]{2,1,0:T(4,128)S(1)}, u32[]{:S(2)}, u32[]{:S(2)}) collective-permute-start(f32[3,4,128]{2,1,0:T(4,128)S(1)} %reduce_sum.19), channel_id=1, source_target_pairs={{0,4},{4,0},{1,5},{5,1},{2,6},{6,2},{3,7},{7,3},{8,12},{12,8},{9,1... | collective-permute-start | bytes 18440 | tf_op jit(solution)/shard_map/ppermute | solution.py:154
  112.0 0.8 collective-permute-done.8
  112.8 0.7 broadcast_in_dim.34
  113.5 4.2 %all-to-all-start.3 = ((f32[32,3,4,128]{3,2,1,0:T(4,128)}), f32[32,3,4,128]{3,2,1,0:T(4,128)S(1)}, u32[]{:S(2)}, u32[]{:S(2)}) async-start(f32[32,3,4,128]{3,2,1,0:T(4,128)} %broadcast_in_dim.34), calls=%async_computation.3 | async-start | bytes 393216 | tf_op jit(solution)/shard_map/all_to_all | solution.py:36
  117.8 10.8 %all-to-all-done.3 = f32[32,3,4,128]{3,2,1,0:T(4,128)S(1)} async-done(((f32[32,3,4,128]{3,2,1,0:T(4,128)}), f32[32,3,4,128]{3,2,1,0:T(4,128)S(1)}, u32[]{:S(2)}, u32[]{:S(2)}) %all-to-all-start.3) | async-done | bytes 196640 | tf_op jit(solution)/shard_map/all_to_all | solution.py:36
  128.7 0.3 fusion.38
  129.2 0.1 copy.61
  129.4 0.1 pad_maximum_fusion.1
  129.4 0.1 copy.57
  129.7 0.1 copy.66
  129.8 0.1 pad_maximum_fusion.2
  129.9 0.1 copy.58
  130.1 0.8 maximum_multiply_fusion.margin_ref
  131.0 24.6 %shard_map.37 = f32[224,224]{1,0:T(8,128)} custom-call(f32[224,224]{1,0:T(8,128)} %maximum_multiply_fusion.margin_ref), custom_call_target="tpu_custom_call" | custom-call | tf_op jit(solution)/shard_map/pallas_call | solution.py:121
  155.6 1.6 %convolution_convert_fusion = bf16[56,512]{1,0:T(8,128)(2,1)} fusion(bf16[224,512]{1,0:T(8,128)(2,1)S(1)} %bitcast.63, f32[224,224]{1,0:T(8,128)} %shard_map.37, s32[]{:T(128)S(6)} %select_n.132), kind=kOutput, calls=%fused_computation.15 | convolution fusion | flops 12873728 | bytes 315396 | tf_op jit(solution)/shard_map/dot_general | solution.py:45
  (38 shorter events, 0.8 us)
Async XLA Ops:
  0.0 14.7 %copy-start = (bf16[1,729,729]{2,1,0:T(8,128)(2,1)S(1)}, bf16[1,729,729]{2,1,0:T(8,128)(2,1)}, u32[]{:S(2)}) copy-start(bf16[1,729,729]{2,1,0:T(8,128)(2,1)} %param.4) | copy-start | bytes 3188650
  0.9 17.4 %collective-permute-start = (bf16[56,64]{1,0:T(8,128)(2,1)S(1)}, bf16[56,64]{1,0:T(8,128)(2,1)S(1)}, u32[]{:S(2)}, u32[]{:S(2)}) collective-permute-start(bf16[56,64]{1,0:T(8,128)(2,1)S(1)} %get-tuple-element.39), channel_id=1, source_target_pairs={{4,8},{12,16},{20,24},{28,32},{36,40},{44,48},{52,56},{60,64},{68,... | collective-permute-start | bytes 21512 | tf_op jit(solution)/shard_map/ppermute | solution.py:29
  6.3 12.1 %collective-permute-start.1 = (bf16[56,64]{1,0:T(8,128)(2,1)S(1)}, bf16[56,64]{1,0:T(8,128)(2,1)S(1)}, u32[]{:S(2)}, u32[]{:S(2)}) collective-permute-start(bf16[56,64]{1,0:T(8,128)(2,1)S(1)} %get-tuple-element.40), channel_id=1, source_target_pairs={{0,4},{4,0},{1,5},{5,1},{2,6},{6,2},{3,7},{7,3},{8,12},{12,8},{9,1... | collective-permute-start | bytes 21512 | tf_op jit(solution)/shard_map/ppermute | solution.py:30
  17.1 1.2 copy-start.1
  19.0 5.2 %collective-permute-start.2 = (f32[56,128]{1,0:T(8,128)S(1)}, f32[56,128]{1,0:T(8,128)S(1)}, u32[]{:S(2)}, u32[]{:S(2)}) collective-permute-start(f32[56,128]{1,0:T(8,128)S(1)} %get-tuple-element.23), channel_id=1, source_target_pairs={{4,8},{12,16},{20,24},{28,32},{36,40},{44,48},{52,56},{60,64},{68,... | collective-permute-start | bytes 86024 | tf_op jit(solution)/shard_map/ppermute | solution.py:29
  21.0 3.3 %collective-permute-start.3 = (f32[56,128]{1,0:T(8,128)S(1)}, f32[56,128]{1,0:T(8,128)S(1)}, u32[]{:S(2)}, u32[]{:S(2)}) collective-permute-start(f32[56,128]{1,0:T(8,128)S(1)} %get-tuple-element.24), channel_id=1, source_target_pairs={{0,4},{4,0},{1,5},{5,1},{2,6},{6,2},{3,7},{7,3},{8,12},{12,8},{9,1... | collective-permute-start | bytes 86024 | tf_op jit(solution)/shard_map/ppermute | solution.py:30
  24.9 5.4 %collective-permute-start.4 = (f32[56,128]{1,0:T(8,128)S(1)}, f32[56,128]{1,0:T(8,128)S(1)}, u32[]{:S(2)}, u32[]{:S(2)}) collective-permute-start(f32[56,128]{1,0:T(8,128)S(1)} %get-tuple-element.21), channel_id=1, source_target_pairs={{4,8},{12,16},{20,24},{28,32},{36,40},{44,48},{52,56},{60,64},{68,... | collective-permute-start | bytes 86024 | tf_op jit(solution)/shard_map/ppermute | solution.py:29
  28.4 3.1 %collective-permute-start.5 = (f32[56,128]{1,0:T(8,128)S(1)}, f32[56,128]{1,0:T(8,128)S(1)}, u32[]{:S(2)}, u32[]{:S(2)}) collective-permute-start(f32[56,128]{1,0:T(8,128)S(1)} %get-tuple-element.22), channel_id=1, source_target_pairs={{0,4},{4,0},{1,5},{5,1},{2,6},{6,2},{3,7},{7,3},{8,12},{12,8},{9,1... | collective-permute-start | bytes 86024 | tf_op jit(solution)/shard_map/ppermute | solution.py:30
  32.2 5.2 %collective-permute-start.6 = (f32[56,128]{1,0:T(8,128)S(1)}, f32[56,128]{1,0:T(8,128)S(1)}, u32[]{:S(2)}, u32[]{:S(2)}) collective-permute-start(f32[56,128]{1,0:T(8,128)S(1)} %get-tuple-element.19), channel_id=1, source_target_pairs={{4,8},{12,16},{20,24},{28,32},{36,40},{44,48},{52,56},{60,64},{68,... | collective-permute-start | bytes 86024 | tf_op jit(solution)/shard_map/ppermute | solution.py:29
  34.6 3.1 %collective-permute-start.7 = (f32[56,128]{1,0:T(8,128)S(1)}, f32[56,128]{1,0:T(8,128)S(1)}, u32[]{:S(2)}, u32[]{:S(2)}) collective-permute-start(f32[56,128]{1,0:T(8,128)S(1)} %get-tuple-element.20), channel_id=1, source_target_pairs={{0,4},{4,0},{1,5},{5,1},{2,6},{6,2},{3,7},{7,3},{8,12},{12,8},{9,1... | collective-permute-start | bytes 86024 | tf_op jit(solution)/shard_map/ppermute | solution.py:30
  38.6 11.4 %all-to-all-start = ((bf16[4,56,512]{2,1,0:T(8,128)(2,1)}), bf16[4,56,512]{2,1,0:T(8,128)(2,1)S(1)}, u32[]{:S(2)}, u32[]{:S(2)}) async-start(bf16[4,56,512]{2,1,0:T(8,128)(2,1)} %broadcast_in_dim.32), calls=%async_computation | async-start | bytes 458752 | tf_op jit(solution)/shard_map/all_to_all | solution.py:36
  104.4 8.5 %collective-permute-start.8 = (f32[3,4,128]{2,1,0:T(4,128)S(1)}, f32[3,4,128]{2,1,0:T(4,128)S(1)}, u32[]{:S(2)}, u32[]{:S(2)}) collective-permute-start(f32[3,4,128]{2,1,0:T(4,128)S(1)} %reduce_sum.19), channel_id=1, source_target_pairs={{0,4},{4,0},{1,5},{5,1},{2,6},{6,2},{3,7},{7,3},{8,12},{12,8},{9,1... | collective-permute-start | bytes 18440 | tf_op jit(solution)/shard_map/ppermute | solution.py:154
  113.5 15.1 %all-to-all-start.3 = ((f32[32,3,4,128]{3,2,1,0:T(4,128)}), f32[32,3,4,128]{3,2,1,0:T(4,128)S(1)}, u32[]{:S(2)}, u32[]{:S(2)}) async-start(f32[32,3,4,128]{3,2,1,0:T(4,128)} %broadcast_in_dim.34), calls=%async_computation.3 | async-start | bytes 393216 | tf_op jit(solution)/shard_map/all_to_all | solution.py:36

commit v3 on v2

v3 whole, which is shorter than its diff:
```python
import jax
import jax.numpy as jnp
from jax import lax
from jax.experimental import pallas as pl
from jax.experimental.pallas import tpu as pltpu
from jax.sharding import Mesh, PartitionSpec as P

CELL_NODES = 729
BANDS = 224
BLOCK = 56
NODE_DEV = 512
SHARED = 64
NODE_EXT = 640
EDGE = 2 * SHARED
CELLS = ("yh", "x", "z", "core")
SPREAD = ("yh", "x")
OUTER = ("yh", "x", "bands")
N_CELLS = 192
ROWS = 12
GROUP = 14
SWAPS = [(i, i + 1) for i in range(1, N_CELLS - 1, 2)] + [(i + 1, i) for i in range(1, N_CELLS - 1, 2)]

filter_center = 2.75
filter_half = 2.25


def exchange(to_right, to_left):
    first_cell = lax.axis_index("core") == 0
    outer = lax.ppermute(jnp.where(first_cell, to_left, to_right), CELLS, SWAPS)
    inner = lax.ppermute(jnp.where(first_cell, to_right, to_left), "core", [(0, 1), (1, 0)])
    return jnp.where(first_cell, outer, inner), jnp.where(first_cell, inner, outer)


def from_everyone(shard, axis, size):
    copies = jnp.broadcast_to(shard, (size, *shard.shape))
    return lax.all_to_all(copies, axis, split_axis=0, concat_axis=0, tiled=True)


def split(value):
    high = lax.reduce_precision(value, 8, 7)
    return high.astype(jnp.bfloat16), (value - high).astype(jnp.bfloat16)


def dot(a, b, dims):
    return lax.dot_general(a, b, (dims, ((), ())), preferred_element_type=jnp.float32)


def assembled(cell_ham, local_index):
    nodes = lax.broadcasted_iota(jnp.int32, (CELL_NODES, NODE_EXT), 1)
    pick = (local_index[:, None] == nodes).astype(jnp.bfloat16)
    high, low = split(dot(cell_ham, pick, ((1,), (0,))))
    total = dot(pick, high, ((0,), (0,))) + dot(pick, low, ((0,), (0,)))
    return split(total)


def next_term(applied, current, previous):
    shifted = (applied - filter_center * current.astype(jnp.float32)) / filter_half
    if previous is None:
        return shifted.astype(jnp.bfloat16)
    return (2.0 * shifted - previous.astype(jnp.float32)).astype(jnp.bfloat16)


def gram_kernel(band_ref, gathered_ref, packed_ref, rows_ref):
    band = band_ref[0]
    other = lax.rem(band + 1, 4)
    low = lax.rem(band, 2)

    def product(i, j):
        return dot(gathered_ref[i], gathered_ref[j], ((1,), (1,)))

    rows_ref[...] = jnp.zeros_like(rows_ref)
    two = product(low, low + 2)
    half = BLOCK // 2
    rows_ref[:BLOCK, :BLOCK] = product(band, band)
    rows_ref[:BLOCK, BLOCK : 2 * BLOCK] = product(jnp.minimum(band, other), jnp.maximum(band, other))
    rows_ref[BLOCK : BLOCK + half, :BLOCK] = two[:half]
    rows_ref[BLOCK : BLOCK + half, BLOCK : 2 * BLOCK] = two[half:]
    for i in range(8):
        for j in range(3):
            packed_ref[i, j] = rows_ref[pl.ds(12 * i + 4 * j, 4), :]


def packed_gram(band, gathered):
    return pl.pallas_call(
        gram_kernel,
        out_shape=jax.ShapeDtypeStruct((8, 3, 4, 128), jnp.float32),
        in_specs=[pl.BlockSpec(memory_space=pltpu.SMEM), pl.BlockSpec(memory_space=pltpu.VMEM)],
        out_specs=pl.BlockSpec(memory_space=pltpu.VMEM),
        scratch_shapes=[pltpu.VMEM((8 * ROWS, 128), jnp.float32)],
    )(band, gathered)


def exact_dot(a, b, dims):
    return lax.dot_general(a, b, (dims, ((), ())), precision=lax.Precision.HIGHEST, preferred_element_type=jnp.float32)


def finish_kernel(band_ref, rows_ref, gathered_ref, out_ref, packed_ref, left_ref, inverse_ref):
    for i in range(8):
        for b in range(4):
            for j in range(3):
                packed_ref[b, pl.ds(12 * i + 4 * j, 4), :] = rows_ref[4 * i + b, j]
    half = BLOCK // 2
    scale = 1.0 / float(NODE_DEV * N_CELLS)
    left_ref[...] = jnp.zeros_like(left_ref)
    for b in range(4):
        c, s = (b + 1) % 4, b * BLOCK
        left_ref[s : s + BLOCK, s : s + BLOCK] = packed_ref[b, :BLOCK, :BLOCK] * scale
        r, t = min(b, c) * BLOCK, max(b, c) * BLOCK
        left_ref[r : r + BLOCK, t : t + BLOCK] = packed_ref[b, :BLOCK, BLOCK : 2 * BLOCK] * scale
        if b < 2:
            t = s + 2 * BLOCK
            left_ref[s : s + half, t : t + BLOCK] = packed_ref[b, BLOCK : BLOCK + half, :BLOCK] * scale
            left_ref[s + half : s + BLOCK, t : t + BLOCK] = packed_ref[b, BLOCK : BLOCK + half, BLOCK : 2 * BLOCK] * scale

    at_row = lax.broadcasted_iota(jnp.int32, (BANDS, BANDS), 0)
    at_column = lax.broadcasted_iota(jnp.int32, (BANDS, BANDS), 1)
    inverse_ref[...] = (at_row == at_column).astype(jnp.float32)
    row = lax.broadcasted_iota(jnp.int32, (BLOCK, 128), 0)
    column = lax.broadcasted_iota(jnp.int32, (BLOCK, 128), 1)
    unit = (row + BLOCK == column).astype(jnp.float32)

    def spread(value, i):
        return jnp.broadcast_to(value[i : i + 1, :], (BLOCK, 128))

    for start in range(0, BANDS, BLOCK):
        stop = start + BLOCK
        corner = left_ref[start:stop, start:stop]
        both = jnp.concatenate([corner, jnp.zeros((BLOCK, 128 - BLOCK), jnp.float32)], axis=1) + unit
        for j in range(0, BLOCK, GROUP):
            columns = [jnp.broadcast_to(both[:, j + k : j + k + 1], (BLOCK, 128)) for k in range(GROUP)]
            lines = [spread(both, j + k) for k in range(GROUP)]
            for k in range(GROUP):
                reciprocal = 1.0 / spread(columns[k], j + k)
                factor = jnp.where(row > j + k, columns[k], 0.0) * reciprocal
                for m in range(k + 1, GROUP):
                    entry = spread(columns[k], j + m)
                    columns[m] = columns[m] - factor * entry
                    lines[m] = lines[m] - (entry * reciprocal) * lines[k]
                both = both - factor * lines[k]
        pivots = jnp.sum(jnp.where(row == column, both, 0.0), axis=1, keepdims=True)
        scaled = both[:, BLOCK : 2 * BLOCK] * lax.rsqrt(pivots)
        lines = exact_dot(scaled, inverse_ref[start:stop, :], ((1,), (0,)))
        inverse_ref[start:stop, :] = lines
        if stop < BANDS:
            upper = exact_dot(scaled, left_ref[start:stop, :], ((1,), (0,)))
            right = upper[:, stop:]
            left_ref[stop:, :] = left_ref[stop:, :] - exact_dot(right, upper, ((0,), (0,)))
            inverse_ref[stop:, :] = inverse_ref[stop:, :] - exact_dot(right, lines, ((0,), (0,)))

    band_rows = inverse_ref[pl.ds(pl.multiple_of(band_ref[0] * BLOCK, 8), BLOCK), :].astype(jnp.bfloat16)
    out_ref[...] = dot(band_rows, gathered_ref[...], ((1,), (0,))).astype(jnp.bfloat16)


def finished(band, rows, gathered):
    vmem = pl.BlockSpec(memory_space=pltpu.VMEM)
    return pl.pallas_call(
        finish_kernel,
        out_shape=jax.ShapeDtypeStruct((BLOCK, NODE_DEV), jnp.bfloat16),
        in_specs=[pl.BlockSpec(memory_space=pltpu.SMEM), vmem, vmem],
        out_specs=vmem,
        scratch_shapes=[
            pltpu.VMEM((4, 8 * ROWS, 128), jnp.float32),
            pltpu.VMEM((BANDS, BANDS), jnp.float32),
            pltpu.VMEM((BANDS, BANDS), jnp.float32),
        ],
    )(band, rows, gathered)


def shards(start_bands, cell_ham, node_index):
    partition = lax.axis_index(CELLS)
    band = lax.axis_index("bands")
    left, right = exchange(start_bands[:, NODE_DEV - SHARED :], start_bands[:, :SHARED])
    local_index = node_index.reshape(-1) - partition * NODE_DEV
    high, low = assembled(cell_ham[0], local_index)
    node = lax.broadcasted_iota(jnp.int32, (1, NODE_EXT), 1) + partition * NODE_DEV
    inside = (node >= SHARED) & (node < SHARED + N_CELLS * NODE_DEV)

    def applied(bands_now):
        partial = dot(bands_now, high, ((1,), (0,))) + dot(bands_now, low, ((1,), (0,)))
        from_left, from_right = exchange(partial[:, NODE_EXT - EDGE :], partial[:, :EDGE])
        zeros = jnp.zeros((BLOCK, NODE_EXT - 2 * EDGE), jnp.float32)
        return jnp.where(inside, partial + jnp.concatenate([from_left, zeros, from_right], axis=1), 0.0)

    start = jnp.concatenate([left, start_bands, right], axis=1)
    first = next_term(applied(start), start, None)
    second = next_term(applied(first), first, start)
    third = next_term(applied(second), second, first)[:, SHARED : SHARED + NODE_DEV]

    gathered = from_everyone(third, "bands", 4)
    place = jnp.full((1,), band, jnp.int32)
    rows = packed_gram(place, gathered)
    rows = lax.all_to_all(rows, SPREAD, split_axis=0, concat_axis=0, tiled=True).sum(axis=0)
    rows = from_everyone(rows, "z", 12).sum(axis=0)
    rows = rows + lax.ppermute(rows, "core", [(0, 1), (1, 0)])
    rows = from_everyone(rows, OUTER, 32)
    return finished(place, rows, gathered.reshape(BANDS, NODE_DEV))


def solution(mesh):
    inner = Mesh(mesh.devices.reshape(2, 4, 12, 2, 4), ("yh", "x", "z", "core", "bands"))
    return jax.shard_map(
        shards,
        mesh=inner,
        in_specs=(P("bands", CELLS), P(CELLS, None, None), P(CELLS, None)),
        out_specs=P("bands", CELLS),
        check_vma=False,
    )
```

time: 158 us -> 141 us (0.89)
  blocking collectives: 53.9 us -> 69.1 us
  Pallas kernels: 24.6 us -> 12 us
  waiting for transfers between devices: 22 us -> 11.2 us
  starting transfers between devices: 43 us -> 38.8 us
  matrix products: 7.17 us -> 5.38 us
    all_to_all x1 -> x2, blocking collectives: 14.6 us -> 29.6 us  [from_everyone(): return lax.all_to_all(copies, axis, split_axis=0, concat_axis=0, tiled=True)]
    pallas_call x1 -> x2, Pallas kernels: 24.6 us -> 12 us  [the longest x1 10.2 us: finished(): pl.pallas_call(finish_kernel, out_shape=jax.ShapeDtypeStruct((BLOCK, NODE...]
    all_to_all x2 -> x1, waiting for transfers between devices: 17.7 us -> 6.84 us  [from_everyone(): return lax.all_to_all(copies, axis, split_axis=0, concat_axis=0, tiled=True)]
    all_to_all x2 -> x1, starting transfers between devices: 8.84 us -> 4.59 us  [from_everyone(): return lax.all_to_all(copies, axis, split_axis=0, concat_axis=0, tiled=True)]
    dot_general x11 -> x9, matrix products: 7.17 us -> 5.38 us  [dot(): lax.dot_general(a, b, (dims, ((), ())), preferred_element_type=jnp.float32)]
  transfers between devices with their start and end apart: 11 -> 10, of which waited for: 7 -> 6; matrix products, arithmetic and copies ran while one was open for 3% -> 3% of each run, Pallas kernels for 0% -> 0%
where the time goes in v3:
time: 141 us; the launch traced here: 140 us
  blocking collectives  69.1 us (49%)
  starting transfers between devices  38.8 us (28%)
  Pallas kernels  12 us (9%)
  waiting for transfers between devices  11.2 us (8%)
  matrix products  5.38 us (4%)
  other arithmetic  2.12 us (2%)
  local copies, waits for them, and re-layouts  1.53 us (1%)
    all_to_all x1, blocking collectives, shards(): lax.all_to_all(rows, SPREAD, split_axis=0, concat_axis=0, tiled=True)  39.5 us
    all_to_all x2, blocking collectives, from_everyone(): return lax.all_to_all(copies, axis, split_axis=0, concat_axis=0, tiled=True)  29.6 us
    ppermute x4, starting transfers between devices, exchange(): lax.ppermute(jnp.where(first_cell, to_right, to_left), 'core', [(0, 1), (...  13.4 us
    ppermute x4, starting transfers between devices, exchange(): outer = lax.ppermute(jnp.where(first_cell, to_left, to_right), CELLS, SWAPS)  13.1 us
    pallas_call x1, Pallas kernels, finished(): pl.pallas_call(finish_kernel, out_shape=jax.ShapeDtypeStruct((BLOCK, NODE...  10.2 us
    ppermute x1, starting transfers between devices, shards(): rows = rows + lax.ppermute(rows, 'core', [(0, 1), (1, 0)])  7.65 us
    all_to_all x1, waiting for transfers between devices, from_everyone(): return lax.all_to_all(copies, axis, split_axis=0, concat_axis=0, tiled=True)  6.84 us
    dot_general x9, matrix products, dot(): lax.dot_general(a, b, (dims, ((), ())), preferred_element_type=jnp.float32)  5.38 us
  transfers between devices with their start and end apart: 10, of which 6 were waited for; matrix products, arithmetic and copies ran while one was open for 3% of the time, Pallas kernels for 0%

profile of v3, /device:TPU:1, one launch (start us, length us, event | category | flops | bytes accessed | tf_op | source)
XLA Modules:
  0.0 140.4 jit_solution(5167768790913399886)
XLA Ops:
  0.0 0.0 copy-start
  0.0 0.9 broadcast_select_fusion.9
  0.9 5.4 %collective-permute-start = (bf16[56,64]{1,0:T(8,128)(2,1)S(1)}, bf16[56,64]{1,0:T(8,128)(2,1)S(1)}, u32[]{:S(2)}, u32[]{:S(2)}) collective-permute-start(bf16[56,64]{1,0:T(8,128)(2,1)S(1)} %get-tuple-element.19), channel_id=1, source_target_pairs={{4,8},{12,16},{20,24},{28,32},{36,40},{44,48},{52,56},{60,64},{68,... | collective-permute-start | bytes 21512 | tf_op jit(solution)/shard_map/ppermute | solution.py:29
  6.3 7.7 %collective-permute-start.1 = (bf16[56,64]{1,0:T(8,128)(2,1)S(1)}, bf16[56,64]{1,0:T(8,128)(2,1)S(1)}, u32[]{:S(2)}, u32[]{:S(2)}) collective-permute-start(bf16[56,64]{1,0:T(8,128)(2,1)S(1)} %get-tuple-element.20), channel_id=1, source_target_pairs={{0,4},{4,0},{1,5},{5,1},{2,6},{6,2},{3,7},{7,3},{8,12},{12,8},{9,1... | collective-permute-start | bytes 21512 | tf_op jit(solution)/shard_map/ppermute | solution.py:30
  14.0 0.7 subtract_reduce_fusion
  14.7 0.0 copy-done
  14.7 1.2 fusion.3
  15.9 1.2 fusion.1
  17.1 0.0 copy-start.2
  17.1 1.2 fusion.5
  18.3 0.0 collective-permute-done
  18.3 0.0 collective-permute-done.1
  18.4 0.0 copy-done.2
  18.4 0.3 fusion.26
  18.7 0.3 convolution_add_fusion.2
  19.0 1.9 %collective-permute-start.2 = (f32[56,128]{1,0:T(8,128)S(1)}, f32[56,128]{1,0:T(8,128)S(1)}, u32[]{:S(2)}, u32[]{:S(2)}) collective-permute-start(f32[56,128]{1,0:T(8,128)S(1)} %get-tuple-element.11), channel_id=1, source_target_pairs={{4,8},{12,16},{20,24},{28,32},{36,40},{44,48},{52,56},{60,64},{68,... | collective-permute-start | bytes 86024 | tf_op jit(solution)/shard_map/ppermute | solution.py:29
  21.0 1.9 %collective-permute-start.3 = (f32[56,128]{1,0:T(8,128)S(1)}, f32[56,128]{1,0:T(8,128)S(1)}, u32[]{:S(2)}, u32[]{:S(2)}) collective-permute-start(f32[56,128]{1,0:T(8,128)S(1)} %get-tuple-element.12), channel_id=1, source_target_pairs={{0,4},{4,0},{1,5},{5,1},{2,6},{6,2},{3,7},{7,3},{8,12},{12,8},{9,1... | collective-permute-start | bytes 86024 | tf_op jit(solution)/shard_map/ppermute | solution.py:30
  22.9 1.3 collective-permute-done.2
  24.2 0.0 collective-permute-done.3
  24.2 0.1 fusion.32
  24.3 0.3 fusion.28
  24.6 0.3 convolution_add_fusion.1
  24.9 3.5 %collective-permute-start.4 = (f32[56,128]{1,0:T(8,128)S(1)}, f32[56,128]{1,0:T(8,128)S(1)}, u32[]{:S(2)}, u32[]{:S(2)}) collective-permute-start(f32[56,128]{1,0:T(8,128)S(1)} %get-tuple-element.9), channel_id=1, source_target_pairs={{4,8},{12,16},{20,24},{28,32},{36,40},{44,48},{52,56},{60,64},{68,... | collective-permute-start | bytes 86024 | tf_op jit(solution)/shard_map/ppermute | solution.py:29
  28.4 1.9 %collective-permute-start.5 = (f32[56,128]{1,0:T(8,128)S(1)}, f32[56,128]{1,0:T(8,128)S(1)}, u32[]{:S(2)}, u32[]{:S(2)}) collective-permute-start(f32[56,128]{1,0:T(8,128)S(1)} %get-tuple-element.10), channel_id=1, source_target_pairs={{0,4},{4,0},{1,5},{5,1},{2,6},{6,2},{3,7},{7,3},{8,12},{12,8},{9,1... | collective-permute-start | bytes 86024 | tf_op jit(solution)/shard_map/ppermute | solution.py:30
  30.3 0.0 collective-permute-done.4
  30.4 1.2 collective-permute-done.5
  31.5 0.1 fusion.14
  31.6 0.3 fusion.27
  31.9 0.3 convolution_add_fusion
  32.2 2.4 %collective-permute-start.6 = (f32[56,128]{1,0:T(8,128)S(1)}, f32[56,128]{1,0:T(8,128)S(1)}, u32[]{:S(2)}, u32[]{:S(2)}) collective-permute-start(f32[56,128]{1,0:T(8,128)S(1)} %get-tuple-element.7), channel_id=1, source_target_pairs={{4,8},{12,16},{20,24},{28,32},{36,40},{44,48},{52,56},{60,64},{68,... | collective-permute-start | bytes 86024 | tf_op jit(solution)/shard_map/ppermute | solution.py:29
  34.6 1.9 %collective-permute-start.7 = (f32[56,128]{1,0:T(8,128)S(1)}, f32[56,128]{1,0:T(8,128)S(1)}, u32[]{:S(2)}, u32[]{:S(2)}) collective-permute-start(f32[56,128]{1,0:T(8,128)S(1)} %get-tuple-element.8), channel_id=1, source_target_pairs={{0,4},{4,0},{1,5},{5,1},{2,6},{6,2},{3,7},{7,3},{8,12},{12,8},{9,1... | collective-permute-start | bytes 86024 | tf_op jit(solution)/shard_map/ppermute | solution.py:30
  36.5 0.1 slice.45
  36.6 0.8 collective-permute-done.6
  37.4 0.3 collective-permute-done.7
  37.7 0.2 fusion.19
  37.9 0.7 broadcast_in_dim.36
  38.6 4.6 %all-to-all-start = ((bf16[4,56,512]{2,1,0:T(8,128)(2,1)}), bf16[4,56,512]{2,1,0:T(8,128)(2,1)S(1)}, u32[]{:S(2)}, u32[]{:S(2)}) async-start(bf16[4,56,512]{2,1,0:T(8,128)(2,1)} %broadcast_in_dim.36), calls=%async_computation | async-start | bytes 458752 | tf_op jit(solution)/shard_map/all_to_all | solution.py:36
  43.2 6.8 %all-to-all-done.gathered_ref = bf16[4,56,512]{2,1,0:T(8,128)(2,1)S(1)} async-done(((bf16[4,56,512]{2,1,0:T(8,128)(2,1)}), bf16[4,56,512]{2,1,0:T(8,128)(2,1)S(1)}, u32[]{:S(2)}, u32[]{:S(2)}) %all-to-all-start) | async-done | bytes 229408 | tf_op jit(solution)/shard_map/all_to_all | solution.py:36
  50.1 0.0 copy-start.1
  50.1 0.7 copy-done.1
  50.7 1.8 %shard_map.37 = f32[8,3,4,128]{3,2,1,0:T(4,128)} custom-call(s32[1]{0:T(128)} %bitcast.band_ref, bf16[4,56,512]{2,1,0:T(8,128)(2,1)} %copy-done.1), custom_call_target="tpu_custom_call" | custom-call | tf_op jit(solution)/shard_map/pallas_call | solution.py:84
  52.6 39.5 %all_to_all.20 = f32[8,3,4,128]{3,2,1,0:T(4,128)S(1)} all-to-all(f32[8,3,4,128]{3,2,1,0:T(4,128)} %shard_map.37), channel_id=1, replica_groups=mesh['yh'=2,'x'=4,'z'=12,'core'=2,'bands'=4] {'yh','x'}, dimensions={0} | all-to-all | bytes 98304 | tf_op jit(solution)/shard_map/all_to_all | solution.py:192
  92.1 14.6 %all_to_all.21 = f32[12,3,4,128]{3,2,1,0:T(4,128)S(1)} all-to-all(f32[12,3,4,128]{3,2,1,0:T(4,128)S(1)} %broadcast_in_dim.37), channel_id=1, replica_groups=mesh['yh'=2,'x'=4,'z'=12,'core'=2,'bands'=4] {'z'}, dimensions={0} | all-to-all | bytes 147456 | tf_op jit(solution)/shard_map/all_to_all | solution.py:36
  106.8 7.6 %collective-permute-start.8 = (f32[3,4,128]{2,1,0:T(4,128)S(1)}, f32[3,4,128]{2,1,0:T(4,128)S(1)}, u32[]{:S(2)}, u32[]{:S(2)}) collective-permute-start(f32[3,4,128]{2,1,0:T(4,128)S(1)} %reduce_sum.19), channel_id=1, source_target_pairs={{0,4},{4,0},{1,5},{5,1},{2,6},{6,2},{3,7},{7,3},{8,12},{12,8},{9,1... | collective-permute-start | bytes 18440 | tf_op jit(solution)/shard_map/ppermute | solution.py:194
  114.4 0.8 collective-permute-done.8
  115.3 15.0 %all_to_all.22.rows_ref = f32[32,3,4,128]{3,2,1,0:T(4,128)} all-to-all(f32[32,3,4,128]{3,2,1,0:T(4,128)S(1)} %broadcast_in_dim.38), channel_id=1, replica_groups=mesh['yh'=2,'x'=4,'z'=12,'core'=2,'bands'=4] {'yh','x','bands'}, dimensions={0} | all-to-all | bytes 393216 | tf_op jit(solution)/shard_map/all_to_all | solution.py:36
  130.2 10.2 %shard_map.38 = bf16[56,512]{1,0:T(8,128)(2,1)} custom-call(s32[1]{0:T(128)} %bitcast.band_ref, f32[32,3,4,128]{3,2,1,0:T(4,128)} %all_to_all.22.rows_ref, bf16[224,512]{1,0:T(8,128)(2,1)} %bitcast.14), custom_call_target="tpu_custom_call" | custom-call | tf_op jit(solution)/shard_map/pallas_call | solution.py:156
  (16 shorter events, 0.2 us)
Async XLA Ops:
  0.0 14.7 %copy-start = (bf16[1,729,729]{2,1,0:T(8,128)(2,1)S(1)}, bf16[1,729,729]{2,1,0:T(8,128)(2,1)}, u32[]{:S(2)}) copy-start(bf16[1,729,729]{2,1,0:T(8,128)(2,1)} %param.4) | copy-start | bytes 3188650
  0.9 17.4 %collective-permute-start = (bf16[56,64]{1,0:T(8,128)(2,1)S(1)}, bf16[56,64]{1,0:T(8,128)(2,1)S(1)}, u32[]{:S(2)}, u32[]{:S(2)}) collective-permute-start(bf16[56,64]{1,0:T(8,128)(2,1)S(1)} %get-tuple-element.19), channel_id=1, source_target_pairs={{4,8},{12,16},{20,24},{28,32},{36,40},{44,48},{52,56},{60,64},{68,... | collective-permute-start | bytes 21512 | tf_op jit(solution)/shard_map/ppermute | solution.py:29
  6.3 12.1 %collective-permute-start.1 = (bf16[56,64]{1,0:T(8,128)(2,1)S(1)}, bf16[56,64]{1,0:T(8,128)(2,1)S(1)}, u32[]{:S(2)}, u32[]{:S(2)}) collective-permute-start(bf16[56,64]{1,0:T(8,128)(2,1)S(1)} %get-tuple-element.20), channel_id=1, source_target_pairs={{0,4},{4,0},{1,5},{5,1},{2,6},{6,2},{3,7},{7,3},{8,12},{12,8},{9,1... | collective-permute-start | bytes 21512 | tf_op jit(solution)/shard_map/ppermute | solution.py:30
  17.1 1.2 copy-start.2
  19.0 5.2 %collective-permute-start.2 = (f32[56,128]{1,0:T(8,128)S(1)}, f32[56,128]{1,0:T(8,128)S(1)}, u32[]{:S(2)}, u32[]{:S(2)}) collective-permute-start(f32[56,128]{1,0:T(8,128)S(1)} %get-tuple-element.11), channel_id=1, source_target_pairs={{4,8},{12,16},{20,24},{28,32},{36,40},{44,48},{52,56},{60,64},{68,... | collective-permute-start | bytes 86024 | tf_op jit(solution)/shard_map/ppermute | solution.py:29
  21.0 3.3 %collective-permute-start.3 = (f32[56,128]{1,0:T(8,128)S(1)}, f32[56,128]{1,0:T(8,128)S(1)}, u32[]{:S(2)}, u32[]{:S(2)}) collective-permute-start(f32[56,128]{1,0:T(8,128)S(1)} %get-tuple-element.12), channel_id=1, source_target_pairs={{0,4},{4,0},{1,5},{5,1},{2,6},{6,2},{3,7},{7,3},{8,12},{12,8},{9,1... | collective-permute-start | bytes 86024 | tf_op jit(solution)/shard_map/ppermute | solution.py:30
  24.9 5.4 %collective-permute-start.4 = (f32[56,128]{1,0:T(8,128)S(1)}, f32[56,128]{1,0:T(8,128)S(1)}, u32[]{:S(2)}, u32[]{:S(2)}) collective-permute-start(f32[56,128]{1,0:T(8,128)S(1)} %get-tuple-element.9), channel_id=1, source_target_pairs={{4,8},{12,16},{20,24},{28,32},{36,40},{44,48},{52,56},{60,64},{68,... | collective-permute-start | bytes 86024 | tf_op jit(solution)/shard_map/ppermute | solution.py:29
  28.4 3.1 %collective-permute-start.5 = (f32[56,128]{1,0:T(8,128)S(1)}, f32[56,128]{1,0:T(8,128)S(1)}, u32[]{:S(2)}, u32[]{:S(2)}) collective-permute-start(f32[56,128]{1,0:T(8,128)S(1)} %get-tuple-element.10), channel_id=1, source_target_pairs={{0,4},{4,0},{1,5},{5,1},{2,6},{6,2},{3,7},{7,3},{8,12},{12,8},{9,1... | collective-permute-start | bytes 86024 | tf_op jit(solution)/shard_map/ppermute | solution.py:30
  32.2 5.2 %collective-permute-start.6 = (f32[56,128]{1,0:T(8,128)S(1)}, f32[56,128]{1,0:T(8,128)S(1)}, u32[]{:S(2)}, u32[]{:S(2)}) collective-permute-start(f32[56,128]{1,0:T(8,128)S(1)} %get-tuple-element.7), channel_id=1, source_target_pairs={{4,8},{12,16},{20,24},{28,32},{36,40},{44,48},{52,56},{60,64},{68,... | collective-permute-start | bytes 86024 | tf_op jit(solution)/shard_map/ppermute | solution.py:29
  34.6 3.1 %collective-permute-start.7 = (f32[56,128]{1,0:T(8,128)S(1)}, f32[56,128]{1,0:T(8,128)S(1)}, u32[]{:S(2)}, u32[]{:S(2)}) collective-permute-start(f32[56,128]{1,0:T(8,128)S(1)} %get-tuple-element.8), channel_id=1, source_target_pairs={{0,4},{4,0},{1,5},{5,1},{2,6},{6,2},{3,7},{7,3},{8,12},{12,8},{9,1... | collective-permute-start | bytes 86024 | tf_op jit(solution)/shard_map/ppermute | solution.py:30
  38.6 11.4 %all-to-all-start = ((bf16[4,56,512]{2,1,0:T(8,128)(2,1)}), bf16[4,56,512]{2,1,0:T(8,128)(2,1)S(1)}, u32[]{:S(2)}, u32[]{:S(2)}) async-start(bf16[4,56,512]{2,1,0:T(8,128)(2,1)} %broadcast_in_dim.36), calls=%async_computation | async-start | bytes 458752 | tf_op jit(solution)/shard_map/all_to_all | solution.py:36
  50.1 0.7 copy-start.1
  106.8 8.5 %collective-permute-start.8 = (f32[3,4,128]{2,1,0:T(4,128)S(1)}, f32[3,4,128]{2,1,0:T(4,128)S(1)}, u32[]{:S(2)}, u32[]{:S(2)}) collective-permute-start(f32[3,4,128]{2,1,0:T(4,128)S(1)} %reduce_sum.19), channel_id=1, source_target_pairs={{0,4},{4,0},{1,5},{5,1},{2,6},{6,2},{3,7},{7,3},{8,12},{12,8},{9,1... | collective-permute-start | bytes 18440 | tf_op jit(solution)/shard_map/ppermute | solution.py:194

commit v4 on v3

--- a/solution.py
+++ b/solution.py
@@ -60,34 +60,17 @@
     return (2.0 * shifted - previous.astype(jnp.float32)).astype(jnp.bfloat16)
 
 
-def gram_kernel(band_ref, gathered_ref, packed_ref, rows_ref):
-    band = band_ref[0]
-    other = lax.rem(band + 1, 4)
-    low = lax.rem(band, 2)
-
-    def product(i, j):
-        return dot(gathered_ref[i], gathered_ref[j], ((1,), (1,)))
-
-    rows_ref[...] = jnp.zeros_like(rows_ref)
-    two = product(low, low + 2)
+def packed_gram(band, gathered, third):
+    full = dot(gathered, third, ((2,), (1,)))
+    here = lax.dynamic_index_in_dim(full, band, 0, False)
+    one = lax.dynamic_index_in_dim(full, (band + 1) % 4, 0, False)
+    two = lax.dynamic_index_in_dim(full, (band + 2) % 4, 0, False)
     half = BLOCK // 2
-    rows_ref[:BLOCK, :BLOCK] = product(band, band)
-    rows_ref[:BLOCK, BLOCK : 2 * BLOCK] = product(jnp.minimum(band, other), jnp.maximum(band, other))
-    rows_ref[BLOCK : BLOCK + half, :BLOCK] = two[:half]
-    rows_ref[BLOCK : BLOCK + half, BLOCK : 2 * BLOCK] = two[half:]
-    for i in range(8):
-        for j in range(3):
-            packed_ref[i, j] = rows_ref[pl.ds(12 * i + 4 * j, 4), :]
-
-
-def packed_gram(band, gathered):
-    return pl.pallas_call(
-        gram_kernel,
-        out_shape=jax.ShapeDtypeStruct((8, 3, 4, 128), jnp.float32),
-        in_specs=[pl.BlockSpec(memory_space=pltpu.SMEM), pl.BlockSpec(memory_space=pltpu.VMEM)],
-        out_specs=pl.BlockSpec(memory_space=pltpu.VMEM),
-        scratch_shapes=[pltpu.VMEM((8 * ROWS, 128), jnp.float32)],
-    )(band, gathered)
+    top = jnp.concatenate([here, one], axis=1)
+    bottom = jnp.concatenate([two[:half], two[half:]], axis=1)
+    rows = jnp.concatenate([top, bottom], axis=0)
+    rows = jnp.pad(rows, ((0, 8 * ROWS - rows.shape[0]), (0, 128 - rows.shape[1])))
+    return rows.reshape(8, 3, 4, 128)
 
 
 def exact_dot(a, b, dims):
@@ -106,11 +89,12 @@
         c, s = (b + 1) % 4, b * BLOCK
         left_ref[s : s + BLOCK, s : s + BLOCK] = packed_ref[b, :BLOCK, :BLOCK] * scale
         r, t = min(b, c) * BLOCK, max(b, c) * BLOCK
-        left_ref[r : r + BLOCK, t : t + BLOCK] = packed_ref[b, :BLOCK, BLOCK : 2 * BLOCK] * scale
-        if b < 2:
-            t = s + 2 * BLOCK
-            left_ref[s : s + half, t : t + BLOCK] = packed_ref[b, BLOCK : BLOCK + half, :BLOCK] * scale
-            left_ref[s + half : s + BLOCK, t : t + BLOCK] = packed_ref[b, BLOCK : BLOCK + half, BLOCK : 2 * BLOCK] * scale
+        one = packed_ref[b, :BLOCK, BLOCK : 2 * BLOCK] * scale
+        left_ref[r : r + BLOCK, t : t + BLOCK] = one.T if b < 3 else one
+        if b >= 2:
+            r = s - 2 * BLOCK
+            left_ref[r : r + half, s : s + BLOCK] = packed_ref[b, BLOCK : BLOCK + half, :BLOCK] * scale
+            left_ref[r + half : r + BLOCK, s : s + BLOCK] = packed_ref[b, BLOCK : BLOCK + half, BLOCK : 2 * BLOCK] * scale
 
     at_row = lax.broadcasted_iota(jnp.int32, (BANDS, BANDS), 0)
     at_column = lax.broadcasted_iota(jnp.int32, (BANDS, BANDS), 1)
@@ -188,7 +172,7 @@
 
     gathered = from_everyone(third, "bands", 4)
     place = jnp.full((1,), band, jnp.int32)
-    rows = packed_gram(place, gathered)
+    rows = packed_gram(band, gathered, third)
     rows = lax.all_to_all(rows, SPREAD, split_axis=0, concat_axis=0, tiled=True).sum(axis=0)
     rows = from_everyone(rows, "z", 12).sum(axis=0)
     rows = rows + lax.ppermute(rows, "core", [(0, 1), (1, 0)])

time: 141 us -> 139 us (0.986)
  Pallas kernels: 12 us -> 10.3 us
    pallas_call x1 -> x0, Pallas kernels: 1.84 us -> none  [packed_gram(): pl.pallas_call(gram_kernel, out_shape=jax.ShapeDtypeStruct((8, 3, 4, 128)...]
    dot_general x9 -> x10, matrix products: 5.38 us -> 5.57 us  [dot(): lax.dot_general(a, b, (dims, ((), ())), preferred_element_type=jnp.float32)]
where the time goes in v4:
time: 139 us; the launch traced here: 138 us
  blocking collectives  68.9 us (50%)
  starting transfers between devices  38.8 us (28%)
  waiting for transfers between devices  11.2 us (8%)
  Pallas kernels  10.3 us (7%)
  matrix products  5.57 us (4%)
  other arithmetic  2.21 us (2%)
    all_to_all x1, blocking collectives, shards(): lax.all_to_all(rows, SPREAD, split_axis=0, concat_axis=0, tiled=True)  39.3 us
    all_to_all x2, blocking collectives, from_everyone(): return lax.all_to_all(copies, axis, split_axis=0, concat_axis=0, tiled=True)  29.6 us
    ppermute x4, starting transfers between devices, exchange(): lax.ppermute(jnp.where(first_cell, to_right, to_left), 'core', [(0, 1), (...  13.4 us
    ppermute x4, starting transfers between devices, exchange(): outer = lax.ppermute(jnp.where(first_cell, to_left, to_right), CELLS, SWAPS)  13.1 us
    pallas_call x1, Pallas kernels, finished(): pl.pallas_call(finish_kernel, out_shape=jax.ShapeDtypeStruct((BLOCK, NODE...  10.3 us
    ppermute x1, starting transfers between devices, shards(): rows = rows + lax.ppermute(rows, 'core', [(0, 1), (1, 0)])  7.64 us
    all_to_all x1, waiting for transfers between devices, from_everyone(): return lax.all_to_all(copies, axis, split_axis=0, concat_axis=0, tiled=True)  6.84 us
    dot_general x10, matrix products, dot(): lax.dot_general(a, b, (dims, ((), ())), preferred_element_type=jnp.float32)  5.57 us
  transfers between devices with their start and end apart: 10, of which 6 were waited for; matrix products, arithmetic and copies ran while one was open for 3% of the time, Pallas kernels for 0%

profile of v4, /device:TPU:1, one launch (start us, length us, event | category | flops | bytes accessed | tf_op | source)
XLA Modules:
  0.0 138.2 jit_solution(14161204350868705058)
XLA Ops:
  0.0 0.0 copy-start
  0.0 0.9 broadcast_select_fusion.9
  0.9 5.4 %collective-permute-start = (bf16[56,64]{1,0:T(8,128)(2,1)S(1)}, bf16[56,64]{1,0:T(8,128)(2,1)S(1)}, u32[]{:S(2)}, u32[]{:S(2)}) collective-permute-start(bf16[56,64]{1,0:T(8,128)(2,1)S(1)} %get-tuple-element.23), channel_id=1, source_target_pairs={{4,8},{12,16},{20,24},{28,32},{36,40},{44,48},{52,56},{60,64},{68,... | collective-permute-start | bytes 21512 | tf_op jit(solution)/shard_map/ppermute | solution.py:29
  6.3 7.7 %collective-permute-start.1 = (bf16[56,64]{1,0:T(8,128)(2,1)S(1)}, bf16[56,64]{1,0:T(8,128)(2,1)S(1)}, u32[]{:S(2)}, u32[]{:S(2)}) collective-permute-start(bf16[56,64]{1,0:T(8,128)(2,1)S(1)} %get-tuple-element.24), channel_id=1, source_target_pairs={{0,4},{4,0},{1,5},{5,1},{2,6},{6,2},{3,7},{7,3},{8,12},{12,8},{9,1... | collective-permute-start | bytes 21512 | tf_op jit(solution)/shard_map/ppermute | solution.py:30
  14.0 0.7 subtract_reduce_fusion
  14.7 0.0 copy-done
  14.7 1.2 fusion.3
  15.9 1.2 fusion.1
  17.1 0.0 copy-start.2
  17.1 1.2 fusion.5
  18.3 0.0 collective-permute-done
  18.3 0.0 collective-permute-done.1
  18.4 0.0 copy-done.2
  18.4 0.3 fusion.29
  18.7 0.3 convolution_add_fusion.2
  19.0 1.9 %collective-permute-start.2 = (f32[56,128]{1,0:T(8,128)S(1)}, f32[56,128]{1,0:T(8,128)S(1)}, u32[]{:S(2)}, u32[]{:S(2)}) collective-permute-start(f32[56,128]{1,0:T(8,128)S(1)} %get-tuple-element.11), channel_id=1, source_target_pairs={{4,8},{12,16},{20,24},{28,32},{36,40},{44,48},{52,56},{60,64},{68,... | collective-permute-start | bytes 86024 | tf_op jit(solution)/shard_map/ppermute | solution.py:29
  21.0 1.9 %collective-permute-start.3 = (f32[56,128]{1,0:T(8,128)S(1)}, f32[56,128]{1,0:T(8,128)S(1)}, u32[]{:S(2)}, u32[]{:S(2)}) collective-permute-start(f32[56,128]{1,0:T(8,128)S(1)} %get-tuple-element.12), channel_id=1, source_target_pairs={{0,4},{4,0},{1,5},{5,1},{2,6},{6,2},{3,7},{7,3},{8,12},{12,8},{9,1... | collective-permute-start | bytes 86024 | tf_op jit(solution)/shard_map/ppermute | solution.py:30
  22.9 1.3 collective-permute-done.2
  24.2 0.0 collective-permute-done.3
  24.2 0.1 fusion.35
  24.3 0.3 fusion.31
  24.6 0.3 convolution_add_fusion.1
  24.9 3.5 %collective-permute-start.4 = (f32[56,128]{1,0:T(8,128)S(1)}, f32[56,128]{1,0:T(8,128)S(1)}, u32[]{:S(2)}, u32[]{:S(2)}) collective-permute-start(f32[56,128]{1,0:T(8,128)S(1)} %get-tuple-element.9), channel_id=1, source_target_pairs={{4,8},{12,16},{20,24},{28,32},{36,40},{44,48},{52,56},{60,64},{68,... | collective-permute-start | bytes 86024 | tf_op jit(solution)/shard_map/ppermute | solution.py:29
  28.4 1.9 %collective-permute-start.5 = (f32[56,128]{1,0:T(8,128)S(1)}, f32[56,128]{1,0:T(8,128)S(1)}, u32[]{:S(2)}, u32[]{:S(2)}) collective-permute-start(f32[56,128]{1,0:T(8,128)S(1)} %get-tuple-element.10), channel_id=1, source_target_pairs={{0,4},{4,0},{1,5},{5,1},{2,6},{6,2},{3,7},{7,3},{8,12},{12,8},{9,1... | collective-permute-start | bytes 86024 | tf_op jit(solution)/shard_map/ppermute | solution.py:30
  30.3 0.0 collective-permute-done.4
  30.4 1.2 collective-permute-done.5
  31.5 0.1 fusion.14
  31.6 0.3 fusion.30
  31.9 0.3 convolution_add_fusion
  32.2 2.4 %collective-permute-start.6 = (f32[56,128]{1,0:T(8,128)S(1)}, f32[56,128]{1,0:T(8,128)S(1)}, u32[]{:S(2)}, u32[]{:S(2)}) collective-permute-start(f32[56,128]{1,0:T(8,128)S(1)} %get-tuple-element.7), channel_id=1, source_target_pairs={{4,8},{12,16},{20,24},{28,32},{36,40},{44,48},{52,56},{60,64},{68,... | collective-permute-start | bytes 86024 | tf_op jit(solution)/shard_map/ppermute | solution.py:29
  34.6 1.9 %collective-permute-start.7 = (f32[56,128]{1,0:T(8,128)S(1)}, f32[56,128]{1,0:T(8,128)S(1)}, u32[]{:S(2)}, u32[]{:S(2)}) collective-permute-start(f32[56,128]{1,0:T(8,128)S(1)} %get-tuple-element.8), channel_id=1, source_target_pairs={{0,4},{4,0},{1,5},{5,1},{2,6},{6,2},{3,7},{7,3},{8,12},{12,8},{9,1... | collective-permute-start | bytes 86024 | tf_op jit(solution)/shard_map/ppermute | solution.py:30
  36.5 0.1 slice.61
  36.6 0.8 collective-permute-done.6
  37.4 0.3 collective-permute-done.7
  37.7 0.2 fusion.19
  37.9 0.7 broadcast_in_dim.36
  38.6 4.6 %all-to-all-start = ((bf16[4,56,512]{2,1,0:T(8,128)(2,1)}), bf16[4,56,512]{2,1,0:T(8,128)(2,1)S(1)}, u32[]{:S(2)}, u32[]{:S(2)}) async-start(bf16[4,56,512]{2,1,0:T(8,128)(2,1)} %broadcast_in_dim.36), calls=%async_computation | async-start | bytes 458752 | tf_op jit(solution)/shard_map/all_to_all | solution.py:36
  43.2 6.8 %all-to-all-done = bf16[4,56,512]{2,1,0:T(8,128)(2,1)S(1)} async-done(((bf16[4,56,512]{2,1,0:T(8,128)(2,1)}), bf16[4,56,512]{2,1,0:T(8,128)(2,1)S(1)}, u32[]{:S(2)}, u32[]{:S(2)}) %all-to-all-start) | async-done | bytes 229408 | tf_op jit(solution)/shard_map/all_to_all | solution.py:36
  50.1 0.0 copy-start.1
  50.1 0.2 fusion.23
  50.3 0.1 fusion.25
  50.4 39.3 %all_to_all.20 = f32[8,3,4,128]{3,2,1,0:T(4,128)S(1)} all-to-all(f32[8,3,4,128]{3,2,1,0:T(4,128)S(1)} %bitcast.28), channel_id=1, replica_groups=mesh['yh'=2,'x'=4,'z'=12,'core'=2,'bands'=4] {'yh','x'}, dimensions={0} | all-to-all | bytes 98304 | tf_op jit(solution)/shard_map/all_to_all | solution.py:176
  89.8 14.6 %all_to_all.21 = f32[12,3,4,128]{3,2,1,0:T(4,128)S(1)} all-to-all(f32[12,3,4,128]{3,2,1,0:T(4,128)S(1)} %broadcast_in_dim.37), channel_id=1, replica_groups=mesh['yh'=2,'x'=4,'z'=12,'core'=2,'bands'=4] {'z'}, dimensions={0} | all-to-all | bytes 147456 | tf_op jit(solution)/shard_map/all_to_all | solution.py:36
  104.4 7.6 %collective-permute-start.8 = (f32[3,4,128]{2,1,0:T(4,128)S(1)}, f32[3,4,128]{2,1,0:T(4,128)S(1)}, u32[]{:S(2)}, u32[]{:S(2)}) collective-permute-start(f32[3,4,128]{2,1,0:T(4,128)S(1)} %reduce_sum.19), channel_id=1, source_target_pairs={{0,4},{4,0},{1,5},{5,1},{2,6},{6,2},{3,7},{7,3},{8,12},{12,8},{9,1... | collective-permute-start | bytes 18440 | tf_op jit(solution)/shard_map/ppermute | solution.py:178
  112.0 0.8 collective-permute-done.8
  112.9 15.0 %all_to_all.22.rows_ref = f32[32,3,4,128]{3,2,1,0:T(4,128)} all-to-all(f32[32,3,4,128]{3,2,1,0:T(4,128)S(1)} %broadcast_in_dim.38), channel_id=1, replica_groups=mesh['yh'=2,'x'=4,'z'=12,'core'=2,'bands'=4] {'yh','x','bands'}, dimensions={0} | all-to-all | bytes 393216 | tf_op jit(solution)/shard_map/all_to_all | solution.py:36
  127.9 0.0 copy-done.1
  127.9 10.3 %shard_map.37 = bf16[56,512]{1,0:T(8,128)(2,1)} custom-call(s32[1]{0:T(128)} %bitcast.band_ref, f32[32,3,4,128]{3,2,1,0:T(4,128)} %all_to_all.22.rows_ref, bf16[224,512]{1,0:T(8,128)(2,1)} %bitcast.27), custom_call_target="tpu_custom_call" | custom-call | tf_op jit(solution)/shard_map/pallas_call | solution.py:140
  (18 shorter events, 0.2 us)
Async XLA Ops:
  0.0 14.7 %copy-start = (bf16[1,729,729]{2,1,0:T(8,128)(2,1)S(1)}, bf16[1,729,729]{2,1,0:T(8,128)(2,1)}, u32[]{:S(2)}) copy-start(bf16[1,729,729]{2,1,0:T(8,128)(2,1)} %param.4) | copy-start | bytes 3188650
  0.9 17.4 %collective-permute-start = (bf16[56,64]{1,0:T(8,128)(2,1)S(1)}, bf16[56,64]{1,0:T(8,128)(2,1)S(1)}, u32[]{:S(2)}, u32[]{:S(2)}) collective-permute-start(bf16[56,64]{1,0:T(8,128)(2,1)S(1)} %get-tuple-element.23), channel_id=1, source_target_pairs={{4,8},{12,16},{20,24},{28,32},{36,40},{44,48},{52,56},{60,64},{68,... | collective-permute-start | bytes 21512 | tf_op jit(solution)/shard_map/ppermute | solution.py:29
  6.3 12.1 %collective-permute-start.1 = (bf16[56,64]{1,0:T(8,128)(2,1)S(1)}, bf16[56,64]{1,0:T(8,128)(2,1)S(1)}, u32[]{:S(2)}, u32[]{:S(2)}) collective-permute-start(bf16[56,64]{1,0:T(8,128)(2,1)S(1)} %get-tuple-element.24), channel_id=1, source_target_pairs={{0,4},{4,0},{1,5},{5,1},{2,6},{6,2},{3,7},{7,3},{8,12},{12,8},{9,1... | collective-permute-start | bytes 21512 | tf_op jit(solution)/shard_map/ppermute | solution.py:30
  17.1 1.2 copy-start.2
  19.0 5.2 %collective-permute-start.2 = (f32[56,128]{1,0:T(8,128)S(1)}, f32[56,128]{1,0:T(8,128)S(1)}, u32[]{:S(2)}, u32[]{:S(2)}) collective-permute-start(f32[56,128]{1,0:T(8,128)S(1)} %get-tuple-element.11), channel_id=1, source_target_pairs={{4,8},{12,16},{20,24},{28,32},{36,40},{44,48},{52,56},{60,64},{68,... | collective-permute-start | bytes 86024 | tf_op jit(solution)/shard_map/ppermute | solution.py:29
  21.0 3.3 %collective-permute-start.3 = (f32[56,128]{1,0:T(8,128)S(1)}, f32[56,128]{1,0:T(8,128)S(1)}, u32[]{:S(2)}, u32[]{:S(2)}) collective-permute-start(f32[56,128]{1,0:T(8,128)S(1)} %get-tuple-element.12), channel_id=1, source_target_pairs={{0,4},{4,0},{1,5},{5,1},{2,6},{6,2},{3,7},{7,3},{8,12},{12,8},{9,1... | collective-permute-start | bytes 86024 | tf_op jit(solution)/shard_map/ppermute | solution.py:30
  24.9 5.4 %collective-permute-start.4 = (f32[56,128]{1,0:T(8,128)S(1)}, f32[56,128]{1,0:T(8,128)S(1)}, u32[]{:S(2)}, u32[]{:S(2)}) collective-permute-start(f32[56,128]{1,0:T(8,128)S(1)} %get-tuple-element.9), channel_id=1, source_target_pairs={{4,8},{12,16},{20,24},{28,32},{36,40},{44,48},{52,56},{60,64},{68,... | collective-permute-start | bytes 86024 | tf_op jit(solution)/shard_map/ppermute | solution.py:29
  28.4 3.1 %collective-permute-start.5 = (f32[56,128]{1,0:T(8,128)S(1)}, f32[56,128]{1,0:T(8,128)S(1)}, u32[]{:S(2)}, u32[]{:S(2)}) collective-permute-start(f32[56,128]{1,0:T(8,128)S(1)} %get-tuple-element.10), channel_id=1, source_target_pairs={{0,4},{4,0},{1,5},{5,1},{2,6},{6,2},{3,7},{7,3},{8,12},{12,8},{9,1... | collective-permute-start | bytes 86024 | tf_op jit(solution)/shard_map/ppermute | solution.py:30
  32.2 5.2 %collective-permute-start.6 = (f32[56,128]{1,0:T(8,128)S(1)}, f32[56,128]{1,0:T(8,128)S(1)}, u32[]{:S(2)}, u32[]{:S(2)}) collective-permute-start(f32[56,128]{1,0:T(8,128)S(1)} %get-tuple-element.7), channel_id=1, source_target_pairs={{4,8},{12,16},{20,24},{28,32},{36,40},{44,48},{52,56},{60,64},{68,... | collective-permute-start | bytes 86024 | tf_op jit(solution)/shard_map/ppermute | solution.py:29
  34.6 3.1 %collective-permute-start.7 = (f32[56,128]{1,0:T(8,128)S(1)}, f32[56,128]{1,0:T(8,128)S(1)}, u32[]{:S(2)}, u32[]{:S(2)}) collective-permute-start(f32[56,128]{1,0:T(8,128)S(1)} %get-tuple-element.8), channel_id=1, source_target_pairs={{0,4},{4,0},{1,5},{5,1},{2,6},{6,2},{3,7},{7,3},{8,12},{12,8},{9,1... | collective-permute-start | bytes 86024 | tf_op jit(solution)/shard_map/ppermute | solution.py:30
  38.6 11.4 %all-to-all-start = ((bf16[4,56,512]{2,1,0:T(8,128)(2,1)}), bf16[4,56,512]{2,1,0:T(8,128)(2,1)S(1)}, u32[]{:S(2)}, u32[]{:S(2)}) async-start(bf16[4,56,512]{2,1,0:T(8,128)(2,1)} %broadcast_in_dim.36), calls=%async_computation | async-start | bytes 458752 | tf_op jit(solution)/shard_map/all_to_all | solution.py:36
  50.1 77.8 %copy-start.1 = (bf16[4,56,512]{2,1,0:T(8,128)(2,1)}, bf16[4,56,512]{2,1,0:T(8,128)(2,1)S(1)}, u32[]{:S(2)}) copy-start(bf16[4,56,512]{2,1,0:T(8,128)(2,1)S(1)} %all-to-all-done) | copy-start | bytes 688132
  104.4 8.5 %collective-permute-start.8 = (f32[3,4,128]{2,1,0:T(4,128)S(1)}, f32[3,4,128]{2,1,0:T(4,128)S(1)}, u32[]{:S(2)}, u32[]{:S(2)}) collective-permute-start(f32[3,4,128]{2,1,0:T(4,128)S(1)} %reduce_sum.19), channel_id=1, source_target_pairs={{0,4},{4,0},{1,5},{5,1},{2,6},{6,2},{3,7},{7,3},{8,12},{12,8},{9,1... | collective-permute-start | bytes 18440 | tf_op jit(solution)/shard_map/ppermute | solution.py:178

commit v5 on v4

--- a/solution.py
+++ b/solution.py
@@ -24,11 +24,12 @@
 filter_half = 2.25
 
 
-def exchange(to_right, to_left):
-    first_cell = lax.axis_index("core") == 0
-    outer = lax.ppermute(jnp.where(first_cell, to_left, to_right), CELLS, SWAPS)
-    inner = lax.ppermute(jnp.where(first_cell, to_right, to_left), "core", [(0, 1), (1, 0)])
-    return jnp.where(first_cell, outer, inner), jnp.where(first_cell, inner, outer)
+def swap_outer(value):
+    return lax.ppermute(value, CELLS, SWAPS)
+
+
+def swap_inner(value):
+    return lax.ppermute(value, "core", [(0, 1), (1, 0)])
 
 
 def from_everyone(shard, axis, size):
@@ -50,14 +51,18 @@
     pick = (local_index[:, None] == nodes).astype(jnp.bfloat16)
     high, low = split(dot(cell_ham, pick, ((1,), (0,))))
     total = dot(pick, high, ((0,), (0,))) + dot(pick, low, ((0,), (0,)))
-    return split(total)
-
-
-def next_term(applied, current, previous):
+    return total
+
+
+def raw_term(applied, current, previous):
     shifted = (applied - filter_center * current.astype(jnp.float32)) / filter_half
     if previous is None:
-        return shifted.astype(jnp.bfloat16)
-    return (2.0 * shifted - previous.astype(jnp.float32)).astype(jnp.bfloat16)
+        return shifted
+    return 2.0 * shifted - previous.astype(jnp.float32)
+
+
+def next_term(applied, current, previous):
+    return raw_term(applied, current, previous).astype(jnp.bfloat16)
 
 
 def packed_gram(band, gathered, third):
@@ -153,22 +158,58 @@
 def shards(start_bands, cell_ham, node_index):
     partition = lax.axis_index(CELLS)
     band = lax.axis_index("bands")
-    left, right = exchange(start_bands[:, NODE_DEV - SHARED :], start_bands[:, :SHARED])
+    first_cell = lax.axis_index("core") == 0
+
+    def outer(value, width=EDGE):
+        return jnp.where(first_cell, value[:, :width], value[:, value.shape[1] - width :])
+
+    def inner(value, width=EDGE):
+        return jnp.where(first_cell, value[:, value.shape[1] - width :], value[:, :width])
+
+    def sides(from_outer, from_inner):
+        return jnp.where(first_cell, from_outer, from_inner), jnp.where(first_cell, from_inner, from_outer)
+
+    def received(from_outer, from_inner):
+        left, right = sides(from_outer, from_inner)
+        middle = jnp.zeros((BLOCK, NODE_EXT - 2 * EDGE), jnp.float32)
+        return jnp.concatenate([left, middle, right], axis=1)
+
+    left, right = sides(swap_outer(outer(start_bands, SHARED)), swap_inner(inner(start_bands, SHARED)))
     local_index = node_index.reshape(-1) - partition * NODE_DEV
-    high, low = assembled(cell_ham[0], local_index)
+    total = assembled(cell_ham[0], local_index)
+    high, low = split(total)
+    outer_high, outer_low = outer(high), outer(low)
+    corner = jnp.where(first_cell, total[:EDGE, :EDGE], total[NODE_EXT - EDGE :, NODE_EXT - EDGE :])
     node = lax.broadcasted_iota(jnp.int32, (1, NODE_EXT), 1) + partition * NODE_DEV
     inside = (node >= SHARED) & (node < SHARED + N_CELLS * NODE_DEV)
 
-    def applied(bands_now):
-        partial = dot(bands_now, high, ((1,), (0,))) + dot(bands_now, low, ((1,), (0,)))
-        from_left, from_right = exchange(partial[:, NODE_EXT - EDGE :], partial[:, :EDGE])
-        zeros = jnp.zeros((BLOCK, NODE_EXT - 2 * EDGE), jnp.float32)
-        return jnp.where(inside, partial + jnp.concatenate([from_left, zeros, from_right], axis=1), 0.0)
+    def masked(value):
+        return jnp.where(inside, value, 0.0)
+
+    def times(value, upper, lower):
+        return dot(value, upper, ((1,), (0,))) + dot(value, lower, ((1,), (0,)))
 
     start = jnp.concatenate([left, start_bands, right], axis=1)
-    first = next_term(applied(start), start, None)
-    second = next_term(applied(first), first, start)
-    third = next_term(applied(second), second, first)[:, SHARED : SHARED + NODE_DEV]
+    part = times(start, high, low)
+    arrived = swap_outer(jnp.concatenate([outer(part), corner], axis=0))
+    edge, their_corner = arrived[:BLOCK], arrived[BLOCK:]
+    first = next_term(masked(part + received(edge, swap_inner(inner(part)))), start, None)
+
+    part = times(first, high, low)
+    within = swap_inner(inner(part))
+    mine = raw_term(masked(part + received(jnp.zeros_like(within), within)), first, start)
+    mine_high, mine_low = split(mine)
+    corner_high, corner_low = split(corner)
+    ahead = times(mine_high, outer_high, outer_low) + dot(outer(mine_low), corner_high, ((1,), (0,)))
+    arrived = swap_outer(jnp.concatenate([outer(part), ahead], axis=0))
+    edge, theirs = arrived[:BLOCK], arrived[BLOCK:]
+    second = next_term(masked(part + received(edge, within)), first, start)
+    their_high, their_low = split(their_corner)
+    sent_high, sent_low = split(outer(part) * (2.0 / filter_half))
+    theirs = theirs + times(sent_high, their_high, their_low) + dot(sent_low, their_high, ((1,), (0,)))
+    part = times(second, high, low)
+    third = next_term(masked(part + received(theirs, swap_inner(inner(part)))), second, first)
+    third = third[:, SHARED : SHARED + NODE_DEV]
 
     gathered = from_everyone(third, "bands", 4)
     place = jnp.full((1,), band, jnp.int32)

time: 139 us -> 136 us (0.978)
  starting transfers between devices: 38.8 us -> 34.6 us
  blocking collectives: 68.9 us -> 65.8 us
  waiting for transfers between devices: 11.2 us -> 14.3 us
    ppermute x8 -> x7, waiting for transfers between devices: 3.55 us -> 6.69 us  [the longest x3 3.44 us: swap_outer(): return lax.ppermute(value, CELLS, SWAPS)]
    ppermute x8 -> x7, starting transfers between devices: 26.6 us -> 23.5 us  [the longest x4 13.4 us: swap_inner(): return lax.ppermute(value, 'core', [(0, 1), (1, 0)])]
    all_to_all x2, blocking collectives: 29.6 us -> 27.2 us  [from_everyone(): return lax.all_to_all(copies, axis, split_axis=0, concat_axis=0, tiled=True)]
    dot_general x10 -> x16, matrix products: 5.57 us -> 6.34 us  [dot(): lax.dot_general(a, b, (dims, ((), ())), preferred_element_type=jnp.float32)]
  transfers between devices with their start and end apart: 10 -> 9, of which waited for: 6 -> 7; matrix products, arithmetic and copies ran while one was open for 3% -> 3% of each run, Pallas kernels for 0% -> 0%
where the time goes in v5:
time: 136 us; the launch traced here: 135 us
  blocking collectives  65.8 us (48%)
  starting transfers between devices  34.6 us (25%)
  waiting for transfers between devices  14.3 us (11%)
  Pallas kernels  10.3 us (8%)
  matrix products  6.34 us (5%)
  other arithmetic  2.34 us (2%)
    all_to_all x1, blocking collectives, shards(): lax.all_to_all(rows, SPREAD, split_axis=0, concat_axis=0, tiled=True)  38.5 us
    all_to_all x2, blocking collectives, from_everyone(): return lax.all_to_all(copies, axis, split_axis=0, concat_axis=0, tiled=True)  27.2 us
    ppermute x4, starting transfers between devices, swap_inner(): return lax.ppermute(value, 'core', [(0, 1), (1, 0)])  13.4 us
    pallas_call x1, Pallas kernels, finished(): pl.pallas_call(finish_kernel, out_shape=jax.ShapeDtypeStruct((BLOCK, NODE...  10.3 us
    ppermute x3, starting transfers between devices, swap_outer(): return lax.ppermute(value, CELLS, SWAPS)  10.1 us
    ppermute x1, starting transfers between devices, shards(): rows = rows + lax.ppermute(rows, 'core', [(0, 1), (1, 0)])  7.76 us
    all_to_all x1, waiting for transfers between devices, from_everyone(): return lax.all_to_all(copies, axis, split_axis=0, concat_axis=0, tiled=True)  6.83 us
    dot_general x16, matrix products, dot(): lax.dot_general(a, b, (dims, ((), ())), preferred_element_type=jnp.float32)  6.34 us
  transfers between devices with their start and end apart: 9, of which 7 were waited for; matrix products, arithmetic and copies ran while one was open for 3% of the time, Pallas kernels for 0%

profile of v5, /device:TPU:1, one launch (start us, length us, event | category | flops | bytes accessed | tf_op | source)
XLA Modules:
  0.0 135.0 jit_solution(18270078135741547349)
XLA Ops:
  0.0 0.9 broadcast_select_fusion.7
  0.9 5.4 %collective-permute-start = (bf16[56,64]{1,0:T(8,128)(2,1)S(1)}, bf16[56,64]{1,0:T(8,128)(2,1)S(1)}, u32[]{:S(2)}, u32[]{:S(2)}) collective-permute-start(bf16[56,64]{1,0:T(8,128)(2,1)S(1)} %get-tuple-element.25), channel_id=1, source_target_pairs={{4,8},{12,16},{20,24},{28,32},{36,40},{44,48},{52,56},{60,64},{68,... | collective-permute-start | bytes 21512 | tf_op jit(solution)/shard_map/ppermute | solution.py:28
  6.3 7.7 %collective-permute-start.1 = (bf16[56,64]{1,0:T(8,128)(2,1)S(1)}, bf16[56,64]{1,0:T(8,128)(2,1)S(1)}, u32[]{:S(2)}, u32[]{:S(2)}) collective-permute-start(bf16[56,64]{1,0:T(8,128)(2,1)S(1)} %get-tuple-element.26), channel_id=1, source_target_pairs={{0,4},{4,0},{1,5},{5,1},{2,6},{6,2},{3,7},{7,3},{8,12},{12,8},{9,1... | collective-permute-start | bytes 21512 | tf_op jit(solution)/shard_map/ppermute | solution.py:32
  14.0 0.7 subtract_reduce_fusion
  14.7 1.2 fusion.3
  15.9 1.2 fusion.1
  17.1 0.0 copy-start.2
  17.1 1.2 reduce-precision_convert_fusion.1
  18.3 0.0 collective-permute-done
  18.3 0.0 collective-permute-done.1
  18.4 0.3 fusion.53
  18.7 0.3 convolution_add_fusion.2
  19.0 1.9 %collective-permute-start.2 = (f32[184,128]{1,0:T(8,128)S(1)}, f32[184,128]{1,0:T(8,128)S(1)}, u32[]{:S(2)}, u32[]{:S(2)}) collective-permute-start(f32[184,128]{1,0:T(8,128)S(1)} %pad_maximum_fusion.1), channel_id=1, source_target_pairs={{4,8},{12,16},{20,24},{28,32},{36,40},{44,48},{52,56},{60,64},{68,... | collective-permute-start | bytes 282632 | tf_op jit(solution)/shard_map/ppermute | solution.py:28
  21.0 1.9 %collective-permute-start.3 = (f32[56,128]{1,0:T(8,128)S(1)}, f32[56,128]{1,0:T(8,128)S(1)}, u32[]{:S(2)}, u32[]{:S(2)}) collective-permute-start(f32[56,128]{1,0:T(8,128)S(1)} %get-tuple-element.14), channel_id=1, source_target_pairs={{0,4},{4,0},{1,5},{5,1},{2,6},{6,2},{3,7},{7,3},{8,12},{12,8},{9,1... | collective-permute-start | bytes 86024 | tf_op jit(solution)/shard_map/ppermute | solution.py:32
  22.9 1.1 collective-permute-done.3
  24.1 0.9 collective-permute-done.2
  24.9 0.1 fusion.54
  25.0 0.3 fusion.56
  25.3 0.3 convolution_add_fusion.1
  25.6 1.9 %collective-permute-start.4 = (f32[56,128]{1,0:T(8,128)S(1)}, f32[56,128]{1,0:T(8,128)S(1)}, u32[]{:S(2)}, u32[]{:S(2)}) collective-permute-start(f32[56,128]{1,0:T(8,128)S(1)} %get-tuple-element.12), channel_id=1, source_target_pairs={{0,4},{4,0},{1,5},{5,1},{2,6},{6,2},{3,7},{7,3},{8,12},{12,8},{9,1... | collective-permute-start | bytes 86024 | tf_op jit(solution)/shard_map/ppermute | solution.py:32
  27.5 0.1 slice.129
  27.6 1.1 collective-permute-done.4
  28.7 0.1 fusion.16
  28.8 0.2 fusion.12
  29.0 0.2 convolution_add_fusion.5
  29.2 0.1 convolution_add_fusion.4
  29.3 2.8 %collective-permute-start.5 = (f32[112,128]{1,0:T(8,128)S(1)}, f32[112,128]{1,0:T(8,128)S(1)}, u32[]{:S(2)}, u32[]{:S(2)}) collective-permute-start(f32[112,128]{1,0:T(8,128)S(1)} %pad_maximum_fusion.3), channel_id=1, source_target_pairs={{4,8},{12,16},{20,24},{28,32},{36,40},{44,48},{52,56},{60,64},{68,... | collective-permute-start | bytes 172040 | tf_op jit(solution)/shard_map/ppermute | solution.py:28
  32.1 0.1 fusion.36
  32.3 2.6 %collective-permute-done.5 = f32[112,128]{1,0:T(8,128)S(1)} collective-permute-done((f32[112,128]{1,0:T(8,128)S(1)}, f32[112,128]{1,0:T(8,128)S(1)}, u32[]{:S(2)}, u32[]{:S(2)}) %collective-permute-start.5) | collective-permute-done | bytes 57376 | tf_op jit(solution)/shard_map/ppermute | solution.py:28
  34.8 0.1 fusion.20
  34.9 0.3 fusion.57
  35.2 0.3 convolution_add_fusion
  35.5 1.9 %collective-permute-start.6 = (f32[56,128]{1,0:T(8,128)S(1)}, f32[56,128]{1,0:T(8,128)S(1)}, u32[]{:S(2)}, u32[]{:S(2)}) collective-permute-start(f32[56,128]{1,0:T(8,128)S(1)} %slice_select_fusion.5), channel_id=1, source_target_pairs={{0,4},{4,0},{1,5},{5,1},{2,6},{6,2},{3,7},{7,3},{8,12},{12,8},{9,1... | collective-permute-start | bytes 86024 | tf_op jit(solution)/shard_map/ppermute | solution.py:32
  37.4 0.1 convolution_add_fusion.3
  37.6 1.0 collective-permute-done.6
  38.6 0.1 broadcast_select_fusion.3
  38.8 0.2 fusion.28
  38.9 0.7 broadcast_in_dim.44
  39.6 3.4 %all-to-all-start = ((bf16[4,56,512]{2,1,0:T(8,128)(2,1)}), bf16[4,56,512]{2,1,0:T(8,128)(2,1)S(1)}, u32[]{:S(2)}, u32[]{:S(2)}) async-start(bf16[4,56,512]{2,1,0:T(8,128)(2,1)} %broadcast_in_dim.44), calls=%async_computation | async-start | bytes 458752 | tf_op jit(solution)/shard_map/all_to_all | solution.py:37
  43.1 6.8 %all-to-all-done = bf16[4,56,512]{2,1,0:T(8,128)(2,1)S(1)} async-done(((bf16[4,56,512]{2,1,0:T(8,128)(2,1)}), bf16[4,56,512]{2,1,0:T(8,128)(2,1)S(1)}, u32[]{:S(2)}, u32[]{:S(2)}) %all-to-all-start) | async-done | bytes 229408 | tf_op jit(solution)/shard_map/all_to_all | solution.py:37
  49.9 0.2 fusion.33
  50.1 0.1 fusion.35
  50.2 38.5 %all_to_all.20 = f32[8,3,4,128]{3,2,1,0:T(4,128)S(1)} all-to-all(f32[8,3,4,128]{3,2,1,0:T(4,128)S(1)} %bitcast.36), channel_id=1, replica_groups=mesh['yh'=2,'x'=4,'z'=12,'core'=2,'bands'=4] {'yh','x'}, dimensions={0} | all-to-all | bytes 98304 | tf_op jit(solution)/shard_map/all_to_all | solution.py:217
  88.8 12.4 %all_to_all.21 = f32[12,3,4,128]{3,2,1,0:T(4,128)S(1)} all-to-all(f32[12,3,4,128]{3,2,1,0:T(4,128)S(1)} %broadcast_in_dim.45), channel_id=1, replica_groups=mesh['yh'=2,'x'=4,'z'=12,'core'=2,'bands'=4] {'z'}, dimensions={0} | all-to-all | bytes 147456 | tf_op jit(solution)/shard_map/all_to_all | solution.py:37
  101.3 7.8 %collective-permute-start.7 = (f32[3,4,128]{2,1,0:T(4,128)S(1)}, f32[3,4,128]{2,1,0:T(4,128)S(1)}, u32[]{:S(2)}, u32[]{:S(2)}) collective-permute-start(f32[3,4,128]{2,1,0:T(4,128)S(1)} %reduce_sum.19), channel_id=1, source_target_pairs={{0,4},{4,0},{1,5},{5,1},{2,6},{6,2},{3,7},{7,3},{8,12},{12,8},{9,1... | collective-permute-start | bytes 18440 | tf_op jit(solution)/shard_map/ppermute | solution.py:219
  109.0 0.8 collective-permute-done.7
  109.9 14.8 %all_to_all.22.rows_ref = f32[32,3,4,128]{3,2,1,0:T(4,128)} all-to-all(f32[32,3,4,128]{3,2,1,0:T(4,128)S(1)} %broadcast_in_dim.46), channel_id=1, replica_groups=mesh['yh'=2,'x'=4,'z'=12,'core'=2,'bands'=4] {'yh','x','bands'}, dimensions={0} | all-to-all | bytes 393216 | tf_op jit(solution)/shard_map/all_to_all | solution.py:37
  124.7 10.3 %shard_map.37 = bf16[56,512]{1,0:T(8,128)(2,1)} custom-call(s32[1]{0:T(128)} %bitcast.band_ref, f32[32,3,4,128]{3,2,1,0:T(4,128)} %all_to_all.22.rows_ref, bf16[224,512]{1,0:T(8,128)(2,1)} %bitcast.35), custom_call_target="tpu_custom_call" | custom-call | tf_op jit(solution)/shard_map/pallas_call | solution.py:145
  (26 shorter events, 0.3 us)
Async XLA Ops:
  0.0 14.7 %copy-start = (bf16[1,729,729]{2,1,0:T(8,128)(2,1)S(1)}, bf16[1,729,729]{2,1,0:T(8,128)(2,1)}, u32[]{:S(2)}) copy-start(bf16[1,729,729]{2,1,0:T(8,128)(2,1)} %param.4) | copy-start | bytes 3188650
  0.9 17.4 %collective-permute-start = (bf16[56,64]{1,0:T(8,128)(2,1)S(1)}, bf16[56,64]{1,0:T(8,128)(2,1)S(1)}, u32[]{:S(2)}, u32[]{:S(2)}) collective-permute-start(bf16[56,64]{1,0:T(8,128)(2,1)S(1)} %get-tuple-element.25), channel_id=1, source_target_pairs={{4,8},{12,16},{20,24},{28,32},{36,40},{44,48},{52,56},{60,64},{68,... | collective-permute-start | bytes 21512 | tf_op jit(solution)/shard_map/ppermute | solution.py:28
  6.3 12.1 %collective-permute-start.1 = (bf16[56,64]{1,0:T(8,128)(2,1)S(1)}, bf16[56,64]{1,0:T(8,128)(2,1)S(1)}, u32[]{:S(2)}, u32[]{:S(2)}) collective-permute-start(bf16[56,64]{1,0:T(8,128)(2,1)S(1)} %get-tuple-element.26), channel_id=1, source_target_pairs={{0,4},{4,0},{1,5},{5,1},{2,6},{6,2},{3,7},{7,3},{8,12},{12,8},{9,1... | collective-permute-start | bytes 21512 | tf_op jit(solution)/shard_map/ppermute | solution.py:32
  17.1 1.3 copy-start.2
  19.0 5.9 %collective-permute-start.2 = (f32[184,128]{1,0:T(8,128)S(1)}, f32[184,128]{1,0:T(8,128)S(1)}, u32[]{:S(2)}, u32[]{:S(2)}) collective-permute-start(f32[184,128]{1,0:T(8,128)S(1)} %pad_maximum_fusion.1), channel_id=1, source_target_pairs={{4,8},{12,16},{20,24},{28,32},{36,40},{44,48},{52,56},{60,64},{68,... | collective-permute-start | bytes 282632 | tf_op jit(solution)/shard_map/ppermute | solution.py:28
  21.0 3.1 %collective-permute-start.3 = (f32[56,128]{1,0:T(8,128)S(1)}, f32[56,128]{1,0:T(8,128)S(1)}, u32[]{:S(2)}, u32[]{:S(2)}) collective-permute-start(f32[56,128]{1,0:T(8,128)S(1)} %get-tuple-element.14), channel_id=1, source_target_pairs={{0,4},{4,0},{1,5},{5,1},{2,6},{6,2},{3,7},{7,3},{8,12},{12,8},{9,1... | collective-permute-start | bytes 86024 | tf_op jit(solution)/shard_map/ppermute | solution.py:32
  25.6 3.1 %collective-permute-start.4 = (f32[56,128]{1,0:T(8,128)S(1)}, f32[56,128]{1,0:T(8,128)S(1)}, u32[]{:S(2)}, u32[]{:S(2)}) collective-permute-start(f32[56,128]{1,0:T(8,128)S(1)} %get-tuple-element.12), channel_id=1, source_target_pairs={{0,4},{4,0},{1,5},{5,1},{2,6},{6,2},{3,7},{7,3},{8,12},{12,8},{9,1... | collective-permute-start | bytes 86024 | tf_op jit(solution)/shard_map/ppermute | solution.py:32
  29.3 5.5 %collective-permute-start.5 = (f32[112,128]{1,0:T(8,128)S(1)}, f32[112,128]{1,0:T(8,128)S(1)}, u32[]{:S(2)}, u32[]{:S(2)}) collective-permute-start(f32[112,128]{1,0:T(8,128)S(1)} %pad_maximum_fusion.3), channel_id=1, source_target_pairs={{4,8},{12,16},{20,24},{28,32},{36,40},{44,48},{52,56},{60,64},{68,... | collective-permute-start | bytes 172040 | tf_op jit(solution)/shard_map/ppermute | solution.py:28
  35.5 3.1 %collective-permute-start.6 = (f32[56,128]{1,0:T(8,128)S(1)}, f32[56,128]{1,0:T(8,128)S(1)}, u32[]{:S(2)}, u32[]{:S(2)}) collective-permute-start(f32[56,128]{1,0:T(8,128)S(1)} %slice_select_fusion.5), channel_id=1, source_target_pairs={{0,4},{4,0},{1,5},{5,1},{2,6},{6,2},{3,7},{7,3},{8,12},{12,8},{9,1... | collective-permute-start | bytes 86024 | tf_op jit(solution)/shard_map/ppermute | solution.py:32
  39.6 10.3 %all-to-all-start = ((bf16[4,56,512]{2,1,0:T(8,128)(2,1)}), bf16[4,56,512]{2,1,0:T(8,128)(2,1)S(1)}, u32[]{:S(2)}, u32[]{:S(2)}) async-start(bf16[4,56,512]{2,1,0:T(8,128)(2,1)} %broadcast_in_dim.44), calls=%async_computation | async-start | bytes 458752 | tf_op jit(solution)/shard_map/all_to_all | solution.py:37
  49.9 74.8 %copy-start.1 = (bf16[4,56,512]{2,1,0:T(8,128)(2,1)}, bf16[4,56,512]{2,1,0:T(8,128)(2,1)S(1)}, u32[]{:S(2)}) copy-start(bf16[4,56,512]{2,1,0:T(8,128)(2,1)S(1)} %all-to-all-done) | copy-start | bytes 688132
  101.3 8.6 %collective-permute-start.7 = (f32[3,4,128]{2,1,0:T(4,128)S(1)}, f32[3,4,128]{2,1,0:T(4,128)S(1)}, u32[]{:S(2)}, u32[]{:S(2)}) collective-permute-start(f32[3,4,128]{2,1,0:T(4,128)S(1)} %reduce_sum.19), channel_id=1, source_target_pairs={{0,4},{4,0},{1,5},{5,1},{2,6},{6,2},{3,7},{7,3},{8,12},{12,8},{9,1... | collective-permute-start | bytes 18440 | tf_op jit(solution)/shard_map/ppermute | solution.py:219

commit v6 on v5

--- a/solution.py
+++ b/solution.py
@@ -118,8 +118,12 @@
         for j in range(0, BLOCK, GROUP):
             columns = [jnp.broadcast_to(both[:, j + k : j + k + 1], (BLOCK, 128)) for k in range(GROUP)]
             lines = [spread(both, j + k) for k in range(GROUP)]
+            pivot = spread(columns[0], j)
             for k in range(GROUP):
-                reciprocal = 1.0 / spread(columns[k], j + k)
+                reciprocal = 1.0 / pivot
+                if k + 1 < GROUP:
+                    beside = spread(columns[k], j + k + 1)
+                    pivot = spread(columns[k + 1], j + k + 1) - beside * beside * reciprocal
                 factor = jnp.where(row > j + k, columns[k], 0.0) * reciprocal
                 for m in range(k + 1, GROUP):
                     entry = spread(columns[k], j + m)
@@ -174,7 +178,9 @@
         middle = jnp.zeros((BLOCK, NODE_EXT - 2 * EDGE), jnp.float32)
         return jnp.concatenate([left, middle, right], axis=1)
 
-    left, right = sides(swap_outer(outer(start_bands, SHARED)), swap_inner(inner(start_bands, SHARED)))
+    none = jnp.zeros((BLOCK, SHARED), jnp.bfloat16)
+    left, right = sides(none, swap_inner(inner(start_bands, SHARED)))
+    base = jnp.concatenate([left, start_bands, right], axis=1)
     local_index = node_index.reshape(-1) - partition * NODE_DEV
     total = assembled(cell_ham[0], local_index)
     high, low = split(total)
@@ -189,10 +195,16 @@
     def times(value, upper, lower):
         return dot(value, upper, ((1,), (0,))) + dot(value, lower, ((1,), (0,)))
 
-    start = jnp.concatenate([left, start_bands, right], axis=1)
-    part = times(start, high, low)
-    arrived = swap_outer(jnp.concatenate([outer(part), corner], axis=0))
-    edge, their_corner = arrived[:BLOCK], arrived[BLOCK:]
+    part = times(base, high, low)
+    shared = outer(base)
+    arrived = swap_outer(jnp.concatenate([outer(part), shared.astype(jnp.float32), corner], axis=0))
+    edge, halo, their_corner = arrived[:BLOCK], arrived[BLOCK : 2 * BLOCK].astype(jnp.bfloat16), arrived[2 * BLOCK :]
+    their_high, their_low = split(their_corner)
+    edge = edge + times(shared, their_high, their_low)
+    part = part + dot(halo, outer_high, ((1,), (1,))) + dot(halo, outer_low, ((1,), (1,)))
+    left, right = sides(halo, jnp.zeros_like(halo))
+    middle = jnp.zeros((BLOCK, NODE_EXT - 2 * EDGE), jnp.bfloat16)
+    start = base + jnp.concatenate([left, middle, right], axis=1)
     first = next_term(masked(part + received(edge, swap_inner(inner(part)))), start, None)
 
     part = times(first, high, low)
@@ -204,7 +216,6 @@
     arrived = swap_outer(jnp.concatenate([outer(part), ahead], axis=0))
     edge, theirs = arrived[:BLOCK], arrived[BLOCK:]
     second = next_term(masked(part + received(edge, within)), first, start)
-    their_high, their_low = split(their_corner)
     sent_high, sent_low = split(outer(part) * (2.0 / filter_half))
     theirs = theirs + times(sent_high, their_high, their_low) + dot(sent_low, their_high, ((1,), (0,)))
     part = times(second, high, low)

time: 136 us -> 132 us (0.971)
  blocking collectives: 65.8 us -> 59.7 us
  waiting for transfers between devices: 14.3 us -> 18.1 us
  starting transfers between devices: 34.6 us -> 32.9 us
    all_to_all x1, blocking collectives: 38.5 us -> 28.1 us  [shards(): lax.all_to_all(rows, SPREAD, split_axis=0, concat_axis=0, tiled=True)]
    ppermute x3 -> x2, starting transfers between devices: 10.1 us -> 3.84 us  [swap_outer(): return lax.ppermute(value, CELLS, SWAPS)]
    ppermute x4, starting transfers between devices: 13.4 us -> 18.3 us  [swap_inner(): return lax.ppermute(value, 'core', [(0, 1), (1, 0)])]
    all_to_all x2, blocking collectives: 27.2 us -> 31.6 us  [from_everyone(): return lax.all_to_all(copies, axis, split_axis=0, concat_axis=0, tiled=True)]
    ppermute x3 -> x2, waiting for transfers between devices: 3.44 us -> 7.64 us  [swap_outer(): return lax.ppermute(value, CELLS, SWAPS)]
    dot_general x16 -> x20, matrix products: 6.34 us -> 7.02 us  [dot(): lax.dot_general(a, b, (dims, ((), ())), preferred_element_type=jnp.float32)]
  transfers between devices with their start and end apart: 9 -> 8, of which waited for: 7 -> 7; matrix products, arithmetic and copies ran while one was open for 3% -> 4% of each run, Pallas kernels for 0% -> 0%
where the time goes in v6:
time: 132 us; the launch traced here: 131 us
  blocking collectives  59.7 us (45%)
  starting transfers between devices  32.9 us (25%)
  waiting for transfers between devices  18.1 us (14%)
  Pallas kernels  9.82 us (7%)
  matrix products  7.02 us (5%)
  other arithmetic  2.46 us (2%)
    all_to_all x2, blocking collectives, from_everyone(): return lax.all_to_all(copies, axis, split_axis=0, concat_axis=0, tiled=True)  31.6 us
    all_to_all x1, blocking collectives, shards(): lax.all_to_all(rows, SPREAD, split_axis=0, concat_axis=0, tiled=True)  28.1 us
    ppermute x4, starting transfers between devices, swap_inner(): return lax.ppermute(value, 'core', [(0, 1), (1, 0)])  18.3 us
    pallas_call x1, Pallas kernels, finished(): pl.pallas_call(finish_kernel, out_shape=jax.ShapeDtypeStruct((BLOCK, NODE...  9.82 us
    ppermute x2, waiting for transfers between devices, swap_outer(): return lax.ppermute(value, CELLS, SWAPS)  7.64 us
    ppermute x1, starting transfers between devices, shards(): rows = rows + lax.ppermute(rows, 'core', [(0, 1), (1, 0)])  7.39 us
    dot_general x20, matrix products, dot(): lax.dot_general(a, b, (dims, ((), ())), preferred_element_type=jnp.float32)  7.02 us
    all_to_all x1, waiting for transfers between devices, from_everyone(): return lax.all_to_all(copies, axis, split_axis=0, concat_axis=0, tiled=True)  6.83 us
  transfers between devices with their start and end apart: 8, of which 7 were waited for; matrix products, arithmetic and copies ran while one was open for 4% of the time, Pallas kernels for 0%

profile of v6, /device:TPU:1, one launch (start us, length us, event | category | flops | bytes accessed | tf_op | source)
XLA Modules:
  0.0 131.3 jit_solution(12108071314886383791)
XLA Ops:
  0.0 0.9 slice_select_fusion.16
  0.9 12.4 %collective-permute-start = (bf16[56,64]{1,0:T(8,128)(2,1)S(1)}, bf16[56,64]{1,0:T(8,128)(2,1)S(1)}, u32[]{:S(2)}, u32[]{:S(2)}) collective-permute-start(bf16[56,64]{1,0:T(8,128)(2,1)S(1)} %slice_select_fusion.16), channel_id=1, source_target_pairs={{0,4},{4,0},{1,5},{5,1},{2,6},{6,2},{3,7},{7,3},{8,12},{12,8},{9,1... | collective-permute-start | bytes 21512 | tf_op jit(solution)/shard_map/ppermute | solution.py:32
  13.3 0.7 subtract_reduce_fusion
  14.0 1.2 fusion.3
  15.2 1.2 fusion.1
  16.4 1.1 reduce-precision_convert_fusion.1
  17.6 0.1 fusion.57
  17.7 0.3 fusion.54
  18.0 0.3 convolution_add_fusion.3
  18.4 1.9 %collective-permute-start.1 = (f32[240,128]{1,0:T(8,128)S(1)}, f32[240,128]{1,0:T(8,128)S(1)}, u32[]{:S(2)}, u32[]{:S(2)}) collective-permute-start(f32[240,128]{1,0:T(8,128)S(1)} %pad_maximum_fusion.1), channel_id=1, source_target_pairs={{4,8},{12,16},{20,24},{28,32},{36,40},{44,48},{52,56},{60,64},{68,... | collective-permute-start | bytes 368648 | tf_op jit(solution)/shard_map/ppermute | solution.py:28
  20.4 4.2 %collective-permute-done.1 = f32[240,128]{1,0:T(8,128)S(1)} collective-permute-done((f32[240,128]{1,0:T(8,128)S(1)}, f32[240,128]{1,0:T(8,128)S(1)}, u32[]{:S(2)}, u32[]{:S(2)}) %collective-permute-start.1) | collective-permute-done | bytes 122912 | tf_op jit(solution)/shard_map/ppermute | solution.py:28
  24.6 0.2 fusion.35
  24.8 0.3 fusion.6
  25.1 1.9 %collective-permute-start.2 = (f32[56,128]{1,0:T(8,128)S(1)}, f32[56,128]{1,0:T(8,128)S(1)}, u32[]{:S(2)}, u32[]{:S(2)}) collective-permute-start(f32[56,128]{1,0:T(8,128)S(1)} %slice_select_fusion.4), channel_id=1, source_target_pairs={{0,4},{4,0},{1,5},{5,1},{2,6},{6,2},{3,7},{7,3},{8,12},{12,8},{9,1... | collective-permute-start | bytes 86024 | tf_op jit(solution)/shard_map/ppermute | solution.py:32
  27.0 0.1 fusion.46
  27.1 0.1 convolution_add_fusion.7
  27.3 0.9 collective-permute-done.2
  28.2 0.1 fusion.55
  28.3 0.3 fusion.59
  28.6 0.3 convolution_add_fusion.2
  28.9 2.1 %collective-permute-start.3 = (f32[56,128]{1,0:T(8,128)S(1)}, f32[56,128]{1,0:T(8,128)S(1)}, u32[]{:S(2)}, u32[]{:S(2)}) collective-permute-start(f32[56,128]{1,0:T(8,128)S(1)} %get-tuple-element.18), channel_id=1, source_target_pairs={{0,4},{4,0},{1,5},{5,1},{2,6},{6,2},{3,7},{7,3},{8,12},{12,8},{9,1... | collective-permute-start | bytes 86024 | tf_op jit(solution)/shard_map/ppermute | solution.py:32
  31.0 0.9 collective-permute-done.3
  32.0 0.1 fusion.12
  32.1 0.2 fusion.34
  32.2 0.2 convolution_add_fusion.6
  32.4 0.1 convolution_add_fusion.5
  32.6 1.9 %collective-permute-start.4 = (f32[112,128]{1,0:T(8,128)S(1)}, f32[112,128]{1,0:T(8,128)S(1)}, u32[]{:S(2)}, u32[]{:S(2)}) collective-permute-start(f32[112,128]{1,0:T(8,128)S(1)} %pad_maximum_fusion.3), channel_id=1, source_target_pairs={{4,8},{12,16},{20,24},{28,32},{36,40},{44,48},{52,56},{60,64},{68,... | collective-permute-start | bytes 172040 | tf_op jit(solution)/shard_map/ppermute | solution.py:28
  34.5 0.1 fusion.44
  34.6 3.4 %collective-permute-done.4 = f32[112,128]{1,0:T(8,128)S(1)} collective-permute-done((f32[112,128]{1,0:T(8,128)S(1)}, f32[112,128]{1,0:T(8,128)S(1)}, u32[]{:S(2)}, u32[]{:S(2)}) %collective-permute-start.4) | collective-permute-done | bytes 57376 | tf_op jit(solution)/shard_map/ppermute | solution.py:28
  38.1 0.1 fusion.16
  38.2 0.3 fusion.60
  38.5 0.3 convolution_add_fusion.1
  38.7 1.9 %collective-permute-start.5 = (f32[56,128]{1,0:T(8,128)S(1)}, f32[56,128]{1,0:T(8,128)S(1)}, u32[]{:S(2)}, u32[]{:S(2)}) collective-permute-start(f32[56,128]{1,0:T(8,128)S(1)} %slice_select_fusion.3), channel_id=1, source_target_pairs={{0,4},{4,0},{1,5},{5,1},{2,6},{6,2},{3,7},{7,3},{8,12},{12,8},{9,1... | collective-permute-start | bytes 86024 | tf_op jit(solution)/shard_map/ppermute | solution.py:32
  40.7 0.1 convolution_add_fusion.4
  40.8 1.0 collective-permute-done.5
  41.8 0.1 broadcast_select_fusion.3
  42.0 0.2 fusion.24
  42.2 0.7 broadcast_in_dim.56
  42.9 3.4 %all-to-all-start = ((bf16[4,56,512]{2,1,0:T(8,128)(2,1)}), bf16[4,56,512]{2,1,0:T(8,128)(2,1)S(1)}, u32[]{:S(2)}, u32[]{:S(2)}) async-start(bf16[4,56,512]{2,1,0:T(8,128)(2,1)} %broadcast_in_dim.56), calls=%async_computation | async-start | bytes 458752 | tf_op jit(solution)/shard_map/all_to_all | solution.py:37
  46.3 6.8 %all-to-all-done = bf16[4,56,512]{2,1,0:T(8,128)(2,1)S(1)} async-done(((bf16[4,56,512]{2,1,0:T(8,128)(2,1)}), bf16[4,56,512]{2,1,0:T(8,128)(2,1)S(1)}, u32[]{:S(2)}, u32[]{:S(2)}) %all-to-all-start) | async-done | bytes 229408 | tf_op jit(solution)/shard_map/all_to_all | solution.py:37
  53.2 0.2 fusion.29
  53.4 0.1 fusion.31
  53.5 28.1 %all_to_all.20 = f32[8,3,4,128]{3,2,1,0:T(4,128)S(1)} all-to-all(f32[8,3,4,128]{3,2,1,0:T(4,128)S(1)} %bitcast.40), channel_id=1, replica_groups=mesh['yh'=2,'x'=4,'z'=12,'core'=2,'bands'=4] {'yh','x'}, dimensions={0} | all-to-all | bytes 98304 | tf_op jit(solution)/shard_map/all_to_all | solution.py:228
  81.7 16.8 %all_to_all.21 = f32[12,3,4,128]{3,2,1,0:T(4,128)S(1)} all-to-all(f32[12,3,4,128]{3,2,1,0:T(4,128)S(1)} %broadcast_in_dim.57), channel_id=1, replica_groups=mesh['yh'=2,'x'=4,'z'=12,'core'=2,'bands'=4] {'z'}, dimensions={0} | all-to-all | bytes 147456 | tf_op jit(solution)/shard_map/all_to_all | solution.py:37
  98.5 7.4 %collective-permute-start.6 = (f32[3,4,128]{2,1,0:T(4,128)S(1)}, f32[3,4,128]{2,1,0:T(4,128)S(1)}, u32[]{:S(2)}, u32[]{:S(2)}) collective-permute-start(f32[3,4,128]{2,1,0:T(4,128)S(1)} %reduce_sum.19), channel_id=1, source_target_pairs={{0,4},{4,0},{1,5},{5,1},{2,6},{6,2},{3,7},{7,3},{8,12},{12,8},{9,1... | collective-permute-start | bytes 18440 | tf_op jit(solution)/shard_map/ppermute | solution.py:230
  105.9 0.8 collective-permute-done.6
  106.7 14.8 %all_to_all.22.rows_ref = f32[32,3,4,128]{3,2,1,0:T(4,128)} all-to-all(f32[32,3,4,128]{3,2,1,0:T(4,128)S(1)} %broadcast_in_dim.58), channel_id=1, replica_groups=mesh['yh'=2,'x'=4,'z'=12,'core'=2,'bands'=4] {'yh','x','bands'}, dimensions={0} | all-to-all | bytes 393216 | tf_op jit(solution)/shard_map/all_to_all | solution.py:37
  121.5 9.8 %shard_map.37 = bf16[56,512]{1,0:T(8,128)(2,1)} custom-call(s32[1]{0:T(128)} %bitcast.band_ref, f32[32,3,4,128]{3,2,1,0:T(4,128)} %all_to_all.22.rows_ref, bf16[224,512]{1,0:T(8,128)(2,1)} %bitcast.39), custom_call_target="tpu_custom_call" | custom-call | tf_op jit(solution)/shard_map/pallas_call | solution.py:149
  (34 shorter events, 0.4 us)
Async XLA Ops:
  0.0 14.0 %copy-start = (bf16[1,729,729]{2,1,0:T(8,128)(2,1)S(1)}, bf16[1,729,729]{2,1,0:T(8,128)(2,1)}, u32[]{:S(2)}) copy-start(bf16[1,729,729]{2,1,0:T(8,128)(2,1)} %param.4) | copy-start | bytes 3188650
  0.9 16.7 %collective-permute-start = (bf16[56,64]{1,0:T(8,128)(2,1)S(1)}, bf16[56,64]{1,0:T(8,128)(2,1)S(1)}, u32[]{:S(2)}, u32[]{:S(2)}) collective-permute-start(bf16[56,64]{1,0:T(8,128)(2,1)S(1)} %slice_select_fusion.16), channel_id=1, source_target_pairs={{0,4},{4,0},{1,5},{5,1},{2,6},{6,2},{3,7},{7,3},{8,12},{12,8},{9,1... | collective-permute-start | bytes 21512 | tf_op jit(solution)/shard_map/ppermute | solution.py:32
  16.4 1.2 copy-start.1
  18.4 6.2 %collective-permute-start.1 = (f32[240,128]{1,0:T(8,128)S(1)}, f32[240,128]{1,0:T(8,128)S(1)}, u32[]{:S(2)}, u32[]{:S(2)}) collective-permute-start(f32[240,128]{1,0:T(8,128)S(1)} %pad_maximum_fusion.1), channel_id=1, source_target_pairs={{4,8},{12,16},{20,24},{28,32},{36,40},{44,48},{52,56},{60,64},{68,... | collective-permute-start | bytes 368648 | tf_op jit(solution)/shard_map/ppermute | solution.py:28
  25.1 3.1 %collective-permute-start.2 = (f32[56,128]{1,0:T(8,128)S(1)}, f32[56,128]{1,0:T(8,128)S(1)}, u32[]{:S(2)}, u32[]{:S(2)}) collective-permute-start(f32[56,128]{1,0:T(8,128)S(1)} %slice_select_fusion.4), channel_id=1, source_target_pairs={{0,4},{4,0},{1,5},{5,1},{2,6},{6,2},{3,7},{7,3},{8,12},{12,8},{9,1... | collective-permute-start | bytes 86024 | tf_op jit(solution)/shard_map/ppermute | solution.py:32
  28.9 3.1 %collective-permute-start.3 = (f32[56,128]{1,0:T(8,128)S(1)}, f32[56,128]{1,0:T(8,128)S(1)}, u32[]{:S(2)}, u32[]{:S(2)}) collective-permute-start(f32[56,128]{1,0:T(8,128)S(1)} %get-tuple-element.18), channel_id=1, source_target_pairs={{0,4},{4,0},{1,5},{5,1},{2,6},{6,2},{3,7},{7,3},{8,12},{12,8},{9,1... | collective-permute-start | bytes 86024 | tf_op jit(solution)/shard_map/ppermute | solution.py:32
  32.6 5.5 %collective-permute-start.4 = (f32[112,128]{1,0:T(8,128)S(1)}, f32[112,128]{1,0:T(8,128)S(1)}, u32[]{:S(2)}, u32[]{:S(2)}) collective-permute-start(f32[112,128]{1,0:T(8,128)S(1)} %pad_maximum_fusion.3), channel_id=1, source_target_pairs={{4,8},{12,16},{20,24},{28,32},{36,40},{44,48},{52,56},{60,64},{68,... | collective-permute-start | bytes 172040 | tf_op jit(solution)/shard_map/ppermute | solution.py:28
  38.7 3.1 %collective-permute-start.5 = (f32[56,128]{1,0:T(8,128)S(1)}, f32[56,128]{1,0:T(8,128)S(1)}, u32[]{:S(2)}, u32[]{:S(2)}) collective-permute-start(f32[56,128]{1,0:T(8,128)S(1)} %slice_select_fusion.3), channel_id=1, source_target_pairs={{0,4},{4,0},{1,5},{5,1},{2,6},{6,2},{3,7},{7,3},{8,12},{12,8},{9,1... | collective-permute-start | bytes 86024 | tf_op jit(solution)/shard_map/ppermute | solution.py:32
  42.9 10.3 %all-to-all-start = ((bf16[4,56,512]{2,1,0:T(8,128)(2,1)}), bf16[4,56,512]{2,1,0:T(8,128)(2,1)S(1)}, u32[]{:S(2)}, u32[]{:S(2)}) async-start(bf16[4,56,512]{2,1,0:T(8,128)(2,1)} %broadcast_in_dim.56), calls=%async_computation | async-start | bytes 458752 | tf_op jit(solution)/shard_map/all_to_all | solution.py:37
  53.2 68.4 %copy-start.2 = (bf16[4,56,512]{2,1,0:T(8,128)(2,1)}, bf16[4,56,512]{2,1,0:T(8,128)(2,1)S(1)}, u32[]{:S(2)}) copy-start(bf16[4,56,512]{2,1,0:T(8,128)(2,1)S(1)} %all-to-all-done) | copy-start | bytes 688132
  98.5 8.2 %collective-permute-start.6 = (f32[3,4,128]{2,1,0:T(4,128)S(1)}, f32[3,4,128]{2,1,0:T(4,128)S(1)}, u32[]{:S(2)}, u32[]{:S(2)}) collective-permute-start(f32[3,4,128]{2,1,0:T(4,128)S(1)} %reduce_sum.19), channel_id=1, source_target_pairs={{0,4},{4,0},{1,5},{5,1},{2,6},{6,2},{3,7},{7,3},{8,12},{12,8},{9,1... | collective-permute-start | bytes 18440 | tf_op jit(solution)/shard_map/ppermute | solution.py:230

commit v7 on v6

--- a/solution.py
+++ b/solution.py
@@ -46,12 +46,9 @@
     return lax.dot_general(a, b, (dims, ((), ())), preferred_element_type=jnp.float32)
 
 
-def assembled(cell_ham, local_index):
+def one_hot(local_index):
     nodes = lax.broadcasted_iota(jnp.int32, (CELL_NODES, NODE_EXT), 1)
-    pick = (local_index[:, None] == nodes).astype(jnp.bfloat16)
-    high, low = split(dot(cell_ham, pick, ((1,), (0,))))
-    total = dot(pick, high, ((0,), (0,))) + dot(pick, low, ((0,), (0,)))
-    return total
+    return (local_index[:, None] == nodes).astype(jnp.bfloat16)
 
 
 def raw_term(applied, current, previous):
@@ -182,10 +179,10 @@
     left, right = sides(none, swap_inner(inner(start_bands, SHARED)))
     base = jnp.concatenate([left, start_bands, right], axis=1)
     local_index = node_index.reshape(-1) - partition * NODE_DEV
-    total = assembled(cell_ham[0], local_index)
-    high, low = split(total)
-    outer_high, outer_low = outer(high), outer(low)
-    corner = jnp.where(first_cell, total[:EDGE, :EDGE], total[NODE_EXT - EDGE :, NODE_EXT - EDGE :])
+    pick = one_hot(local_index)
+    half_high, half_low = split(dot(cell_ham[0], pick, ((1,), (0,))))
+    picked = outer(pick)
+    corner = dot(picked, outer(half_high), ((0,), (0,))) + dot(picked, outer(half_low), ((0,), (0,)))
     node = lax.broadcasted_iota(jnp.int32, (1, NODE_EXT), 1) + partition * NODE_DEV
     inside = (node >= SHARED) & (node < SHARED + N_CELLS * NODE_DEV)
 
@@ -195,9 +192,13 @@
     def times(value, upper, lower):
         return dot(value, upper, ((1,), (0,))) + dot(value, lower, ((1,), (0,)))
 
-    part = times(base, high, low)
+    part = times(dot(base, pick, ((1,), (1,))).astype(jnp.bfloat16), half_high, half_low)
     shared = outer(base)
-    arrived = swap_outer(jnp.concatenate([outer(part), shared.astype(jnp.float32), corner], axis=0))
+    sent = jnp.concatenate([outer(part), shared.astype(jnp.float32), corner], axis=0)
+    sent, pick, half_high, half_low = lax.optimization_barrier((sent, pick, half_high, half_low))
+    arrived = swap_outer(sent)
+    high, low = split(dot(pick, half_high, ((0,), (0,))) + dot(pick, half_low, ((0,), (0,))))
+    outer_high, outer_low = outer(high), outer(low)
     edge, halo, their_corner = arrived[:BLOCK], arrived[BLOCK : 2 * BLOCK].astype(jnp.bfloat16), arrived[2 * BLOCK :]
     their_high, their_low = split(their_corner)
     edge = edge + times(shared, their_high, their_low)

time: 132 us -> 131 us (level)
  waiting for transfers between devices: 18.1 us -> 16.2 us
    ppermute x2, waiting for transfers between devices: 7.64 us -> 5.71 us  [swap_outer(): return lax.ppermute(value, CELLS, SWAPS)]
    dot_general x20 -> x23, matrix products: 7.02 us -> 7.74 us  [dot(): lax.dot_general(a, b, (dims, ((), ())), preferred_element_type=jnp.float32)]
where the time goes in v7:
time: 131 us
  blocking collectives  59.7 us (46%)
  starting transfers between devices  32.9 us (25%)
  waiting for transfers between devices  16.2 us (12%)
  Pallas kernels  9.81 us (7%)
  matrix products  7.74 us (6%)
  other arithmetic  2.68 us (2%)
    all_to_all x2, blocking collectives, from_everyone(): return lax.all_to_all(copies, axis, split_axis=0, concat_axis=0, tiled=True)  31.6 us
    all_to_all x1, blocking collectives, shards(): lax.all_to_all(rows, SPREAD, split_axis=0, concat_axis=0, tiled=True)  28.2 us
    ppermute x4, starting transfers between devices, swap_inner(): return lax.ppermute(value, 'core', [(0, 1), (1, 0)])  18.3 us
    pallas_call x1, Pallas kernels, finished(): pl.pallas_call(finish_kernel, out_shape=jax.ShapeDtypeStruct((BLOCK, NODE...  9.81 us
    dot_general x23, matrix products, dot(): lax.dot_general(a, b, (dims, ((), ())), preferred_element_type=jnp.float32)  7.74 us
    ppermute x1, starting transfers between devices, shards(): rows = rows + lax.ppermute(rows, 'core', [(0, 1), (1, 0)])  7.39 us
    all_to_all x1, waiting for transfers between devices, from_everyone(): return lax.all_to_all(copies, axis, split_axis=0, concat_axis=0, tiled=True)  6.83 us
    ppermute x2, waiting for transfers between devices, swap_outer(): return lax.ppermute(value, CELLS, SWAPS)  5.71 us
  transfers between devices with their start and end apart: 8, of which 7 were waited for; matrix products, arithmetic and copies ran while one was open for 4% of the time, Pallas kernels for 0%

profile of v7, /device:TPU:1, one launch (start us, length us, event | category | flops | bytes accessed | tf_op | source)
XLA Modules:
  0.0 130.6 jit_solution(10294483256652681192)
XLA Ops:
  0.0 0.9 slice_select_fusion.22
  0.9 12.4 %collective-permute-start = (bf16[56,64]{1,0:T(8,128)(2,1)S(1)}, bf16[56,64]{1,0:T(8,128)(2,1)S(1)}, u32[]{:S(2)}, u32[]{:S(2)}) collective-permute-start(bf16[56,64]{1,0:T(8,128)(2,1)S(1)} %slice_select_fusion.22), channel_id=1, source_target_pairs={{0,4},{4,0},{1,5},{5,1},{2,6},{6,2},{3,7},{7,3},{8,12},{12,8},{9,1... | collective-permute-start | bytes 21512 | tf_op jit(solution)/shard_map/ppermute | solution.py:32
  13.3 0.7 subtract_reduce_fusion
  14.0 0.2 fusion.1
  14.2 1.2 fusion
  15.4 0.3 fusion.11
  15.7 0.3 convolution_add_fusion.5
  16.1 0.2 copy-done.2
  16.3 0.6 fusion.6
  17.0 0.3 fusion.62
  17.2 0.3 convolution_add_fusion.1
  17.6 1.9 %collective-permute-start.1 = (f32[240,128]{1,0:T(8,128)S(1)}, f32[240,128]{1,0:T(8,128)S(1)}, u32[]{:S(2)}, u32[]{:S(2)}) collective-permute-start(f32[240,128]{1,0:T(8,128)S(1)} %pad_maximum_fusion.1), channel_id=1, source_target_pairs={{4,8},{12,16},{20,24},{28,32},{36,40},{44,48},{52,56},{60,64},{68,... | collective-permute-start | bytes 368648 | tf_op jit(solution)/shard_map/ppermute | solution.py:28
  19.5 1.0 fusion.63
  20.5 1.0 reduce-precision_convert_fusion.1
  21.5 2.3 %collective-permute-done.1 = f32[240,128]{1,0:T(8,128)S(1)} collective-permute-done((f32[240,128]{1,0:T(8,128)S(1)}, f32[240,128]{1,0:T(8,128)S(1)}, u32[]{:S(2)}, u32[]{:S(2)}) %collective-permute-start.1) | collective-permute-done | bytes 122912 | tf_op jit(solution)/shard_map/ppermute | solution.py:28
  23.8 0.2 fusion.38
  24.0 0.3 fusion.5
  24.3 1.9 %collective-permute-start.2 = (f32[56,128]{1,0:T(8,128)S(1)}, f32[56,128]{1,0:T(8,128)S(1)}, u32[]{:S(2)}, u32[]{:S(2)}) collective-permute-start(f32[56,128]{1,0:T(8,128)S(1)} %slice_select_fusion.8), channel_id=1, source_target_pairs={{0,4},{4,0},{1,5},{5,1},{2,6},{6,2},{3,7},{7,3},{8,12},{12,8},{9,1... | collective-permute-start | bytes 86024 | tf_op jit(solution)/shard_map/ppermute | solution.py:32
  26.2 0.1 fusion.49
  26.3 0.1 convolution_add_fusion.9
  26.5 0.9 collective-permute-done.2
  27.5 0.3 fusion.64
  27.8 0.3 convolution_add_fusion.4
  28.1 2.1 %collective-permute-start.3 = (f32[56,128]{1,0:T(8,128)S(1)}, f32[56,128]{1,0:T(8,128)S(1)}, u32[]{:S(2)}, u32[]{:S(2)}) collective-permute-start(f32[56,128]{1,0:T(8,128)S(1)} %get-tuple-element.28), channel_id=1, source_target_pairs={{0,4},{4,0},{1,5},{5,1},{2,6},{6,2},{3,7},{7,3},{8,12},{12,8},{9,1... | collective-permute-start | bytes 86024 | tf_op jit(solution)/shard_map/ppermute | solution.py:32
  30.2 0.9 collective-permute-done.3
  31.3 0.2 fusion.37
  31.5 0.2 convolution_add_fusion.8
  31.6 0.1 convolution_add_fusion.7
  31.8 1.9 %collective-permute-start.4 = (f32[112,128]{1,0:T(8,128)S(1)}, f32[112,128]{1,0:T(8,128)S(1)}, u32[]{:S(2)}, u32[]{:S(2)}) collective-permute-start(f32[112,128]{1,0:T(8,128)S(1)} %pad_maximum_fusion.3), channel_id=1, source_target_pairs={{4,8},{12,16},{20,24},{28,32},{36,40},{44,48},{52,56},{60,64},{68,... | collective-permute-start | bytes 172040 | tf_op jit(solution)/shard_map/ppermute | solution.py:28
  33.7 0.1 fusion.47
  33.9 3.4 %collective-permute-done.4 = f32[112,128]{1,0:T(8,128)S(1)} collective-permute-done((f32[112,128]{1,0:T(8,128)S(1)}, f32[112,128]{1,0:T(8,128)S(1)}, u32[]{:S(2)}, u32[]{:S(2)}) %collective-permute-start.4) | collective-permute-done | bytes 57376 | tf_op jit(solution)/shard_map/ppermute | solution.py:28
  37.4 0.3 fusion.65
  37.7 0.3 convolution_add_fusion.3
  38.0 1.9 %collective-permute-start.5 = (f32[56,128]{1,0:T(8,128)S(1)}, f32[56,128]{1,0:T(8,128)S(1)}, u32[]{:S(2)}, u32[]{:S(2)}) collective-permute-start(f32[56,128]{1,0:T(8,128)S(1)} %slice_select_fusion.7), channel_id=1, source_target_pairs={{0,4},{4,0},{1,5},{5,1},{2,6},{6,2},{3,7},{7,3},{8,12},{12,8},{9,1... | collective-permute-start | bytes 86024 | tf_op jit(solution)/shard_map/ppermute | solution.py:32
  39.9 0.1 convolution_add_fusion.6
  40.0 1.0 collective-permute-done.5
  41.1 0.1 broadcast_select_fusion.3
  41.2 0.2 fusion.27
  41.4 0.7 broadcast_in_dim.56
  42.1 3.4 %all-to-all-start = ((bf16[4,56,512]{2,1,0:T(8,128)(2,1)}), bf16[4,56,512]{2,1,0:T(8,128)(2,1)S(1)}, u32[]{:S(2)}, u32[]{:S(2)}) async-start(bf16[4,56,512]{2,1,0:T(8,128)(2,1)} %broadcast_in_dim.56), calls=%async_computation | async-start | bytes 458752 | tf_op jit(solution)/shard_map/all_to_all | solution.py:37
  45.5 6.8 %all-to-all-done = bf16[4,56,512]{2,1,0:T(8,128)(2,1)S(1)} async-done(((bf16[4,56,512]{2,1,0:T(8,128)(2,1)}), bf16[4,56,512]{2,1,0:T(8,128)(2,1)S(1)}, u32[]{:S(2)}, u32[]{:S(2)}) %all-to-all-start) | async-done | bytes 229408 | tf_op jit(solution)/shard_map/all_to_all | solution.py:37
  52.4 0.2 fusion.32
  52.7 28.2 %all_to_all.20 = f32[8,3,4,128]{3,2,1,0:T(4,128)S(1)} all-to-all(f32[8,3,4,128]{3,2,1,0:T(4,128)S(1)} %bitcast.44), channel_id=1, replica_groups=mesh['yh'=2,'x'=4,'z'=12,'core'=2,'bands'=4] {'yh','x'}, dimensions={0} | all-to-all | bytes 98304 | tf_op jit(solution)/shard_map/all_to_all | solution.py:229
  80.9 16.8 %all_to_all.21 = f32[12,3,4,128]{3,2,1,0:T(4,128)S(1)} all-to-all(f32[12,3,4,128]{3,2,1,0:T(4,128)S(1)} %broadcast_in_dim.57), channel_id=1, replica_groups=mesh['yh'=2,'x'=4,'z'=12,'core'=2,'bands'=4] {'z'}, dimensions={0} | all-to-all | bytes 147456 | tf_op jit(solution)/shard_map/all_to_all | solution.py:37
  97.7 7.4 %collective-permute-start.6 = (f32[3,4,128]{2,1,0:T(4,128)S(1)}, f32[3,4,128]{2,1,0:T(4,128)S(1)}, u32[]{:S(2)}, u32[]{:S(2)}) collective-permute-start(f32[3,4,128]{2,1,0:T(4,128)S(1)} %reduce_sum.19), channel_id=1, source_target_pairs={{0,4},{4,0},{1,5},{5,1},{2,6},{6,2},{3,7},{7,3},{8,12},{12,8},{9,1... | collective-permute-start | bytes 18440 | tf_op jit(solution)/shard_map/ppermute | solution.py:231
  105.1 0.8 collective-permute-done.6
  105.9 14.8 %all_to_all.22.rows_ref = f32[32,3,4,128]{3,2,1,0:T(4,128)} all-to-all(f32[32,3,4,128]{3,2,1,0:T(4,128)S(1)} %broadcast_in_dim.58), channel_id=1, replica_groups=mesh['yh'=2,'x'=4,'z'=12,'core'=2,'bands'=4] {'yh','x','bands'}, dimensions={0} | all-to-all | bytes 393216 | tf_op jit(solution)/shard_map/all_to_all | solution.py:37
  120.8 9.8 %shard_map.37 = bf16[56,512]{1,0:T(8,128)(2,1)} custom-call(s32[1]{0:T(128)} %bitcast.band_ref, f32[32,3,4,128]{3,2,1,0:T(4,128)} %all_to_all.22.rows_ref, bf16[224,512]{1,0:T(8,128)(2,1)} %bitcast.43), custom_call_target="tpu_custom_call" | custom-call | tf_op jit(solution)/shard_map/pallas_call | solution.py:146
  (37 shorter events, 0.9 us)
Async XLA Ops:
  0.0 14.2 %copy-start = (bf16[1,729,729]{2,1,0:T(8,128)(2,1)S(1)}, bf16[1,729,729]{2,1,0:T(8,128)(2,1)}, u32[]{:S(2)}) copy-start(bf16[1,729,729]{2,1,0:T(8,128)(2,1)} %param.4) | copy-start | bytes 3188650
  0.9 15.1 %collective-permute-start = (bf16[56,64]{1,0:T(8,128)(2,1)S(1)}, bf16[56,64]{1,0:T(8,128)(2,1)S(1)}, u32[]{:S(2)}, u32[]{:S(2)}) collective-permute-start(bf16[56,64]{1,0:T(8,128)(2,1)S(1)} %slice_select_fusion.22), channel_id=1, source_target_pairs={{0,4},{4,0},{1,5},{5,1},{2,6},{6,2},{3,7},{7,3},{8,12},{12,8},{9,1... | collective-permute-start | bytes 21512 | tf_op jit(solution)/shard_map/ppermute | solution.py:32
  15.4 0.8 copy-start.2
  17.6 6.2 %collective-permute-start.1 = (f32[240,128]{1,0:T(8,128)S(1)}, f32[240,128]{1,0:T(8,128)S(1)}, u32[]{:S(2)}, u32[]{:S(2)}) collective-permute-start(f32[240,128]{1,0:T(8,128)S(1)} %pad_maximum_fusion.1), channel_id=1, source_target_pairs={{4,8},{12,16},{20,24},{28,32},{36,40},{44,48},{52,56},{60,64},{68,... | collective-permute-start | bytes 368648 | tf_op jit(solution)/shard_map/ppermute | solution.py:28
  24.3 3.1 %collective-permute-start.2 = (f32[56,128]{1,0:T(8,128)S(1)}, f32[56,128]{1,0:T(8,128)S(1)}, u32[]{:S(2)}, u32[]{:S(2)}) collective-permute-start(f32[56,128]{1,0:T(8,128)S(1)} %slice_select_fusion.8), channel_id=1, source_target_pairs={{0,4},{4,0},{1,5},{5,1},{2,6},{6,2},{3,7},{7,3},{8,12},{12,8},{9,1... | collective-permute-start | bytes 86024 | tf_op jit(solution)/shard_map/ppermute | solution.py:32
  28.1 3.1 %collective-permute-start.3 = (f32[56,128]{1,0:T(8,128)S(1)}, f32[56,128]{1,0:T(8,128)S(1)}, u32[]{:S(2)}, u32[]{:S(2)}) collective-permute-start(f32[56,128]{1,0:T(8,128)S(1)} %get-tuple-element.28), channel_id=1, source_target_pairs={{0,4},{4,0},{1,5},{5,1},{2,6},{6,2},{3,7},{7,3},{8,12},{12,8},{9,1... | collective-permute-start | bytes 86024 | tf_op jit(solution)/shard_map/ppermute | solution.py:32
  31.8 5.5 %collective-permute-start.4 = (f32[112,128]{1,0:T(8,128)S(1)}, f32[112,128]{1,0:T(8,128)S(1)}, u32[]{:S(2)}, u32[]{:S(2)}) collective-permute-start(f32[112,128]{1,0:T(8,128)S(1)} %pad_maximum_fusion.3), channel_id=1, source_target_pairs={{4,8},{12,16},{20,24},{28,32},{36,40},{44,48},{52,56},{60,64},{68,... | collective-permute-start | bytes 172040 | tf_op jit(solution)/shard_map/ppermute | solution.py:28
  38.0 3.1 %collective-permute-start.5 = (f32[56,128]{1,0:T(8,128)S(1)}, f32[56,128]{1,0:T(8,128)S(1)}, u32[]{:S(2)}, u32[]{:S(2)}) collective-permute-start(f32[56,128]{1,0:T(8,128)S(1)} %slice_select_fusion.7), channel_id=1, source_target_pairs={{0,4},{4,0},{1,5},{5,1},{2,6},{6,2},{3,7},{7,3},{8,12},{12,8},{9,1... | collective-permute-start | bytes 86024 | tf_op jit(solution)/shard_map/ppermute | solution.py:32
  42.1 10.3 %all-to-all-start = ((bf16[4,56,512]{2,1,0:T(8,128)(2,1)}), bf16[4,56,512]{2,1,0:T(8,128)(2,1)S(1)}, u32[]{:S(2)}, u32[]{:S(2)}) async-start(bf16[4,56,512]{2,1,0:T(8,128)(2,1)} %broadcast_in_dim.56), calls=%async_computation | async-start | bytes 458752 | tf_op jit(solution)/shard_map/all_to_all | solution.py:37
  52.4 68.4 %copy-start.1 = (bf16[4,56,512]{2,1,0:T(8,128)(2,1)}, bf16[4,56,512]{2,1,0:T(8,128)(2,1)S(1)}, u32[]{:S(2)}) copy-start(bf16[4,56,512]{2,1,0:T(8,128)(2,1)S(1)} %all-to-all-done) | copy-start | bytes 688132
  97.7 8.2 %collective-permute-start.6 = (f32[3,4,128]{2,1,0:T(4,128)S(1)}, f32[3,4,128]{2,1,0:T(4,128)S(1)}, u32[]{:S(2)}, u32[]{:S(2)}) collective-permute-start(f32[3,4,128]{2,1,0:T(4,128)S(1)} %reduce_sum.19), channel_id=1, source_target_pairs={{0,4},{4,0},{1,5},{5,1},{2,6},{6,2},{3,7},{7,3},{8,12},{12,8},{9,1... | collective-permute-start | bytes 18440 | tf_op jit(solution)/shard_map/ppermute | solution.py:231

commit v8 on v7

--- a/solution.py
+++ b/solution.py
@@ -79,7 +79,7 @@
     return lax.dot_general(a, b, (dims, ((), ())), precision=lax.Precision.HIGHEST, preferred_element_type=jnp.float32)
 
 
-def finish_kernel(band_ref, rows_ref, gathered_ref, out_ref, packed_ref, left_ref, inverse_ref):
+def finish_kernel(band_ref, rows_ref, gathered_ref, out_ref, packed_ref, left_ref):
     for i in range(8):
         for b in range(4):
             for j in range(3):
@@ -98,9 +98,6 @@
             left_ref[r : r + half, s : s + BLOCK] = packed_ref[b, BLOCK : BLOCK + half, :BLOCK] * scale
             left_ref[r + half : r + BLOCK, s : s + BLOCK] = packed_ref[b, BLOCK : BLOCK + half, BLOCK : 2 * BLOCK] * scale
 
-    at_row = lax.broadcasted_iota(jnp.int32, (BANDS, BANDS), 0)
-    at_column = lax.broadcasted_iota(jnp.int32, (BANDS, BANDS), 1)
-    inverse_ref[...] = (at_row == at_column).astype(jnp.float32)
     row = lax.broadcasted_iota(jnp.int32, (BLOCK, 128), 0)
     column = lax.broadcasted_iota(jnp.int32, (BLOCK, 128), 1)
     unit = (row + BLOCK == column).astype(jnp.float32)
@@ -129,15 +126,17 @@
                 both = both - factor * lines[k]
         pivots = jnp.sum(jnp.where(row == column, both, 0.0), axis=1, keepdims=True)
         scaled = both[:, BLOCK : 2 * BLOCK] * lax.rsqrt(pivots)
-        lines = exact_dot(scaled, inverse_ref[start:stop, :], ((1,), (0,)))
-        inverse_ref[start:stop, :] = lines
+        left_ref[start:stop, start:stop] = unit[:, BLOCK : 2 * BLOCK]
+        lines = exact_dot(scaled, left_ref[start:stop, :], ((1,), (0,)))
+        left_ref[start:stop, :] = lines
         if stop < BANDS:
-            upper = exact_dot(scaled, left_ref[start:stop, :], ((1,), (0,)))
-            right = upper[:, stop:]
-            left_ref[stop:, :] = left_ref[stop:, :] - exact_dot(right, upper, ((0,), (0,)))
-            inverse_ref[stop:, :] = inverse_ref[stop:, :] - exact_dot(right, lines, ((0,), (0,)))
-
-    band_rows = inverse_ref[pl.ds(pl.multiple_of(band_ref[0] * BLOCK, 8), BLOCK), :].astype(jnp.bfloat16)
+            left_ref[stop:, start:stop] = jnp.zeros((BANDS - stop, BLOCK), jnp.float32)
+            left_ref[stop:, :] = left_ref[stop:, :] - exact_dot(lines[:, stop:], lines, ((0,), (0,)))
+
+    first_row = band_ref[0] * BLOCK
+    band_rows = left_ref[pl.ds(pl.multiple_of(first_row, 8), BLOCK), :]
+    passed = lax.broadcasted_iota(jnp.int32, (BLOCK, BANDS), 1) < first_row + BLOCK
+    band_rows = jnp.where(passed, band_rows, 0.0).astype(jnp.bfloat16)
     out_ref[...] = dot(band_rows, gathered_ref[...], ((1,), (0,))).astype(jnp.bfloat16)
 
 
@@ -150,7 +149,6 @@
         out_specs=vmem,
         scratch_shapes=[
             pltpu.VMEM((4, 8 * ROWS, 128), jnp.float32),
-            pltpu.VMEM((BANDS, BANDS), jnp.float32),
             pltpu.VMEM((BANDS, BANDS), jnp.float32),
         ],
     )(band, rows, gathered)

time: 131 us -> 131 us (level)
  no operation moved by 1% of the time
where the time goes in v8:
time: 131 us; the launch traced here: 130 us
  blocking collectives  59.7 us (46%)
  starting transfers between devices  32.9 us (25%)
  waiting for transfers between devices  16.2 us (12%)
  Pallas kernels  9.6 us (7%)
  matrix products  7.74 us (6%)
  other arithmetic  2.68 us (2%)
    all_to_all x2, blocking collectives, from_everyone(): return lax.all_to_all(copies, axis, split_axis=0, concat_axis=0, tiled=True)  31.6 us
    all_to_all x1, blocking collectives, shards(): lax.all_to_all(rows, SPREAD, split_axis=0, concat_axis=0, tiled=True)  28.2 us
    ppermute x4, starting transfers between devices, swap_inner(): return lax.ppermute(value, 'core', [(0, 1), (1, 0)])  18.3 us
    pallas_call x1, Pallas kernels, finished(): pl.pallas_call(finish_kernel, out_shape=jax.ShapeDtypeStruct((BLOCK, NODE...  9.6 us
    dot_general x23, matrix products, dot(): lax.dot_general(a, b, (dims, ((), ())), preferred_element_type=jnp.float32)  7.74 us
    ppermute x1, starting transfers between devices, shards(): rows = rows + lax.ppermute(rows, 'core', [(0, 1), (1, 0)])  7.39 us
    all_to_all x1, waiting for transfers between devices, from_everyone(): return lax.all_to_all(copies, axis, split_axis=0, concat_axis=0, tiled=True)  6.83 us
    ppermute x2, waiting for transfers between devices, swap_outer(): return lax.ppermute(value, CELLS, SWAPS)  5.71 us
  transfers between devices with their start and end apart: 8, of which 7 were waited for; matrix products, arithmetic and copies ran while one was open for 4% of the time, Pallas kernels for 0%

profile of v8, /device:TPU:1, one launch (start us, length us, event | category | flops | bytes accessed | tf_op | source)
XLA Modules:
  0.0 130.4 jit_solution(7701263833354609255)
XLA Ops:
  0.0 0.9 slice_select_fusion.22
  0.9 12.4 %collective-permute-start = (bf16[56,64]{1,0:T(8,128)(2,1)S(1)}, bf16[56,64]{1,0:T(8,128)(2,1)S(1)}, u32[]{:S(2)}, u32[]{:S(2)}) collective-permute-start(bf16[56,64]{1,0:T(8,128)(2,1)S(1)} %slice_select_fusion.22), channel_id=1, source_target_pairs={{0,4},{4,0},{1,5},{5,1},{2,6},{6,2},{3,7},{7,3},{8,12},{12,8},{9,1... | collective-permute-start | bytes 21512 | tf_op jit(solution)/shard_map/ppermute | solution.py:32
  13.3 0.7 subtract_reduce_fusion
  14.0 0.2 fusion.1
  14.2 1.2 fusion
  15.4 0.3 fusion.11
  15.7 0.3 convolution_add_fusion.5
  16.1 0.2 copy-done.2
  16.3 0.6 fusion.6
  17.0 0.3 fusion.62
  17.2 0.3 convolution_add_fusion.1
  17.6 1.9 %collective-permute-start.1 = (f32[240,128]{1,0:T(8,128)S(1)}, f32[240,128]{1,0:T(8,128)S(1)}, u32[]{:S(2)}, u32[]{:S(2)}) collective-permute-start(f32[240,128]{1,0:T(8,128)S(1)} %pad_maximum_fusion.1), channel_id=1, source_target_pairs={{4,8},{12,16},{20,24},{28,32},{36,40},{44,48},{52,56},{60,64},{68,... | collective-permute-start | bytes 368648 | tf_op jit(solution)/shard_map/ppermute | solution.py:28
  19.5 1.0 fusion.63
  20.5 1.0 reduce-precision_convert_fusion.1
  21.5 2.3 %collective-permute-done.1 = f32[240,128]{1,0:T(8,128)S(1)} collective-permute-done((f32[240,128]{1,0:T(8,128)S(1)}, f32[240,128]{1,0:T(8,128)S(1)}, u32[]{:S(2)}, u32[]{:S(2)}) %collective-permute-start.1) | collective-permute-done | bytes 122912 | tf_op jit(solution)/shard_map/ppermute | solution.py:28
  23.8 0.2 fusion.38
  24.0 0.3 fusion.5
  24.3 1.9 %collective-permute-start.2 = (f32[56,128]{1,0:T(8,128)S(1)}, f32[56,128]{1,0:T(8,128)S(1)}, u32[]{:S(2)}, u32[]{:S(2)}) collective-permute-start(f32[56,128]{1,0:T(8,128)S(1)} %slice_select_fusion.8), channel_id=1, source_target_pairs={{0,4},{4,0},{1,5},{5,1},{2,6},{6,2},{3,7},{7,3},{8,12},{12,8},{9,1... | collective-permute-start | bytes 86024 | tf_op jit(solution)/shard_map/ppermute | solution.py:32
  26.2 0.1 fusion.49
  26.3 0.1 convolution_add_fusion.9
  26.5 0.9 collective-permute-done.2
  27.5 0.3 fusion.64
  27.8 0.3 convolution_add_fusion.4
  28.1 2.1 %collective-permute-start.3 = (f32[56,128]{1,0:T(8,128)S(1)}, f32[56,128]{1,0:T(8,128)S(1)}, u32[]{:S(2)}, u32[]{:S(2)}) collective-permute-start(f32[56,128]{1,0:T(8,128)S(1)} %get-tuple-element.28), channel_id=1, source_target_pairs={{0,4},{4,0},{1,5},{5,1},{2,6},{6,2},{3,7},{7,3},{8,12},{12,8},{9,1... | collective-permute-start | bytes 86024 | tf_op jit(solution)/shard_map/ppermute | solution.py:32
  30.2 0.9 collective-permute-done.3
  31.3 0.2 fusion.37
  31.5 0.2 convolution_add_fusion.8
  31.6 0.1 convolution_add_fusion.7
  31.8 1.9 %collective-permute-start.4 = (f32[112,128]{1,0:T(8,128)S(1)}, f32[112,128]{1,0:T(8,128)S(1)}, u32[]{:S(2)}, u32[]{:S(2)}) collective-permute-start(f32[112,128]{1,0:T(8,128)S(1)} %pad_maximum_fusion.3), channel_id=1, source_target_pairs={{4,8},{12,16},{20,24},{28,32},{36,40},{44,48},{52,56},{60,64},{68,... | collective-permute-start | bytes 172040 | tf_op jit(solution)/shard_map/ppermute | solution.py:28
  33.7 0.1 fusion.47
  33.9 3.4 %collective-permute-done.4 = f32[112,128]{1,0:T(8,128)S(1)} collective-permute-done((f32[112,128]{1,0:T(8,128)S(1)}, f32[112,128]{1,0:T(8,128)S(1)}, u32[]{:S(2)}, u32[]{:S(2)}) %collective-permute-start.4) | collective-permute-done | bytes 57376 | tf_op jit(solution)/shard_map/ppermute | solution.py:28
  37.4 0.3 fusion.65
  37.7 0.3 convolution_add_fusion.3
  38.0 1.9 %collective-permute-start.5 = (f32[56,128]{1,0:T(8,128)S(1)}, f32[56,128]{1,0:T(8,128)S(1)}, u32[]{:S(2)}, u32[]{:S(2)}) collective-permute-start(f32[56,128]{1,0:T(8,128)S(1)} %slice_select_fusion.7), channel_id=1, source_target_pairs={{0,4},{4,0},{1,5},{5,1},{2,6},{6,2},{3,7},{7,3},{8,12},{12,8},{9,1... | collective-permute-start | bytes 86024 | tf_op jit(solution)/shard_map/ppermute | solution.py:32
  39.9 0.1 convolution_add_fusion.6
  40.0 1.0 collective-permute-done.5
  41.1 0.1 broadcast_select_fusion.3
  41.2 0.2 fusion.27
  41.4 0.7 broadcast_in_dim.56
  42.1 3.4 %all-to-all-start = ((bf16[4,56,512]{2,1,0:T(8,128)(2,1)}), bf16[4,56,512]{2,1,0:T(8,128)(2,1)S(1)}, u32[]{:S(2)}, u32[]{:S(2)}) async-start(bf16[4,56,512]{2,1,0:T(8,128)(2,1)} %broadcast_in_dim.56), calls=%async_computation | async-start | bytes 458752 | tf_op jit(solution)/shard_map/all_to_all | solution.py:37
  45.5 6.8 %all-to-all-done = bf16[4,56,512]{2,1,0:T(8,128)(2,1)S(1)} async-done(((bf16[4,56,512]{2,1,0:T(8,128)(2,1)}), bf16[4,56,512]{2,1,0:T(8,128)(2,1)S(1)}, u32[]{:S(2)}, u32[]{:S(2)}) %all-to-all-start) | async-done | bytes 229408 | tf_op jit(solution)/shard_map/all_to_all | solution.py:37
  52.4 0.2 fusion.32
  52.7 28.2 %all_to_all.20 = f32[8,3,4,128]{3,2,1,0:T(4,128)S(1)} all-to-all(f32[8,3,4,128]{3,2,1,0:T(4,128)S(1)} %bitcast.44), channel_id=1, replica_groups=mesh['yh'=2,'x'=4,'z'=12,'core'=2,'bands'=4] {'yh','x'}, dimensions={0} | all-to-all | bytes 98304 | tf_op jit(solution)/shard_map/all_to_all | solution.py:227
  80.9 16.8 %all_to_all.21 = f32[12,3,4,128]{3,2,1,0:T(4,128)S(1)} all-to-all(f32[12,3,4,128]{3,2,1,0:T(4,128)S(1)} %broadcast_in_dim.57), channel_id=1, replica_groups=mesh['yh'=2,'x'=4,'z'=12,'core'=2,'bands'=4] {'z'}, dimensions={0} | all-to-all | bytes 147456 | tf_op jit(solution)/shard_map/all_to_all | solution.py:37
  97.7 7.4 %collective-permute-start.6 = (f32[3,4,128]{2,1,0:T(4,128)S(1)}, f32[3,4,128]{2,1,0:T(4,128)S(1)}, u32[]{:S(2)}, u32[]{:S(2)}) collective-permute-start(f32[3,4,128]{2,1,0:T(4,128)S(1)} %reduce_sum.19), channel_id=1, source_target_pairs={{0,4},{4,0},{1,5},{5,1},{2,6},{6,2},{3,7},{7,3},{8,12},{12,8},{9,1... | collective-permute-start | bytes 18440 | tf_op jit(solution)/shard_map/ppermute | solution.py:229
  105.1 0.8 collective-permute-done.6
  105.9 14.8 %all_to_all.22.rows_ref = f32[32,3,4,128]{3,2,1,0:T(4,128)} all-to-all(f32[32,3,4,128]{3,2,1,0:T(4,128)S(1)} %broadcast_in_dim.58), channel_id=1, replica_groups=mesh['yh'=2,'x'=4,'z'=12,'core'=2,'bands'=4] {'yh','x','bands'}, dimensions={0} | all-to-all | bytes 393216 | tf_op jit(solution)/shard_map/all_to_all | solution.py:37
  120.8 9.6 %shard_map.37 = bf16[56,512]{1,0:T(8,128)(2,1)} custom-call(s32[1]{0:T(128)} %bitcast.band_ref, f32[32,3,4,128]{3,2,1,0:T(4,128)} %all_to_all.22.rows_ref, bf16[224,512]{1,0:T(8,128)(2,1)} %bitcast.43), custom_call_target="tpu_custom_call" | custom-call | tf_op jit(solution)/shard_map/pallas_call | solution.py:145
  (37 shorter events, 0.9 us)
Async XLA Ops:
  0.0 14.2 %copy-start = (bf16[1,729,729]{2,1,0:T(8,128)(2,1)S(1)}, bf16[1,729,729]{2,1,0:T(8,128)(2,1)}, u32[]{:S(2)}) copy-start(bf16[1,729,729]{2,1,0:T(8,128)(2,1)} %param.4) | copy-start | bytes 3188650
  0.9 15.1 %collective-permute-start = (bf16[56,64]{1,0:T(8,128)(2,1)S(1)}, bf16[56,64]{1,0:T(8,128)(2,1)S(1)}, u32[]{:S(2)}, u32[]{:S(2)}) collective-permute-start(bf16[56,64]{1,0:T(8,128)(2,1)S(1)} %slice_select_fusion.22), channel_id=1, source_target_pairs={{0,4},{4,0},{1,5},{5,1},{2,6},{6,2},{3,7},{7,3},{8,12},{12,8},{9,1... | collective-permute-start | bytes 21512 | tf_op jit(solution)/shard_map/ppermute | solution.py:32
  15.4 0.8 copy-start.2
  17.6 6.2 %collective-permute-start.1 = (f32[240,128]{1,0:T(8,128)S(1)}, f32[240,128]{1,0:T(8,128)S(1)}, u32[]{:S(2)}, u32[]{:S(2)}) collective-permute-start(f32[240,128]{1,0:T(8,128)S(1)} %pad_maximum_fusion.1), channel_id=1, source_target_pairs={{4,8},{12,16},{20,24},{28,32},{36,40},{44,48},{52,56},{60,64},{68,... | collective-permute-start | bytes 368648 | tf_op jit(solution)/shard_map/ppermute | solution.py:28
  24.3 3.1 %collective-permute-start.2 = (f32[56,128]{1,0:T(8,128)S(1)}, f32[56,128]{1,0:T(8,128)S(1)}, u32[]{:S(2)}, u32[]{:S(2)}) collective-permute-start(f32[56,128]{1,0:T(8,128)S(1)} %slice_select_fusion.8), channel_id=1, source_target_pairs={{0,4},{4,0},{1,5},{5,1},{2,6},{6,2},{3,7},{7,3},{8,12},{12,8},{9,1... | collective-permute-start | bytes 86024 | tf_op jit(solution)/shard_map/ppermute | solution.py:32
  28.1 3.1 %collective-permute-start.3 = (f32[56,128]{1,0:T(8,128)S(1)}, f32[56,128]{1,0:T(8,128)S(1)}, u32[]{:S(2)}, u32[]{:S(2)}) collective-permute-start(f32[56,128]{1,0:T(8,128)S(1)} %get-tuple-element.28), channel_id=1, source_target_pairs={{0,4},{4,0},{1,5},{5,1},{2,6},{6,2},{3,7},{7,3},{8,12},{12,8},{9,1... | collective-permute-start | bytes 86024 | tf_op jit(solution)/shard_map/ppermute | solution.py:32
  31.8 5.5 %collective-permute-start.4 = (f32[112,128]{1,0:T(8,128)S(1)}, f32[112,128]{1,0:T(8,128)S(1)}, u32[]{:S(2)}, u32[]{:S(2)}) collective-permute-start(f32[112,128]{1,0:T(8,128)S(1)} %pad_maximum_fusion.3), channel_id=1, source_target_pairs={{4,8},{12,16},{20,24},{28,32},{36,40},{44,48},{52,56},{60,64},{68,... | collective-permute-start | bytes 172040 | tf_op jit(solution)/shard_map/ppermute | solution.py:28
  38.0 3.1 %collective-permute-start.5 = (f32[56,128]{1,0:T(8,128)S(1)}, f32[56,128]{1,0:T(8,128)S(1)}, u32[]{:S(2)}, u32[]{:S(2)}) collective-permute-start(f32[56,128]{1,0:T(8,128)S(1)} %slice_select_fusion.7), channel_id=1, source_target_pairs={{0,4},{4,0},{1,5},{5,1},{2,6},{6,2},{3,7},{7,3},{8,12},{12,8},{9,1... | collective-permute-start | bytes 86024 | tf_op jit(solution)/shard_map/ppermute | solution.py:32
  42.1 10.3 %all-to-all-start = ((bf16[4,56,512]{2,1,0:T(8,128)(2,1)}), bf16[4,56,512]{2,1,0:T(8,128)(2,1)S(1)}, u32[]{:S(2)}, u32[]{:S(2)}) async-start(bf16[4,56,512]{2,1,0:T(8,128)(2,1)} %broadcast_in_dim.56), calls=%async_computation | async-start | bytes 458752 | tf_op jit(solution)/shard_map/all_to_all | solution.py:37
  52.4 68.4 %copy-start.1 = (bf16[4,56,512]{2,1,0:T(8,128)(2,1)}, bf16[4,56,512]{2,1,0:T(8,128)(2,1)S(1)}, u32[]{:S(2)}) copy-start(bf16[4,56,512]{2,1,0:T(8,128)(2,1)S(1)} %all-to-all-done) | copy-start | bytes 688132
  97.7 8.2 %collective-permute-start.6 = (f32[3,4,128]{2,1,0:T(4,128)S(1)}, f32[3,4,128]{2,1,0:T(4,128)S(1)}, u32[]{:S(2)}, u32[]{:S(2)}) collective-permute-start(f32[3,4,128]{2,1,0:T(4,128)S(1)} %reduce_sum.19), channel_id=1, source_target_pairs={{0,4},{4,0},{1,5},{5,1},{2,6},{6,2},{3,7},{7,3},{8,12},{12,8},{9,1... | collective-permute-start | bytes 18440 | tf_op jit(solution)/shard_map/ppermute | solution.py:229
